TPU v7x, 128 devices: a whole 4x4x4 slice. The times are simulated.
128 devices in a mesh: grp: 4 (over x), seq: 2 (over core), shard: 16 (over z, y).
Axes of the slice: x: 4, y: 4, z: 4, core: 2. Of those that a mesh axis runs over, the one named last changes fastest.
Arguments:
- states: bfloat16 [4, 4096, 1280], P('grp', ('seq', 'shard')), may hold values from -6 to 6
- w_query: bfloat16 [1280, 1280], P('shard'), may hold values from -0.15625 to 0.15625
- w_key: bfloat16 [1280, 1280], P('shard'), may hold values from -0.15625 to 0.15625
- w_value: bfloat16 [1280, 1280], P('shard'), may hold values from -0.15625 to 0.15625
- w_out: bfloat16 [1280, 1280], P('shard'), may hold values from -0.15625 to 0.15625
- w_up: bfloat16 [1280, 5120], P('shard'), may hold values from -0.15625 to 0.15625
- w_gate: bfloat16 [1280, 5120], P('shard'), may hold values from -0.15625 to 0.15625
- w_down: bfloat16 [5120, 1280], P('shard'), may hold values from -0.078125 to 0.078125
- scale_qk: bfloat16 [1280], P('shard'), may hold values from 0.796875 to 1.59375
- alpha_attn: bfloat16 [1280], P('shard'), may hold values from 0.14941406 to 0.59765625
- alpha_mlp: bfloat16 [1280], P('shard'), may hold values from 0.14941406 to 0.59765625
- scale_up: bfloat16 [5120], P('shard'), may hold values from 0.5 to 2
- scale_gate: bfloat16 [5120], P('shard'), may hold values from 0.5 to 2
- lengths: int32 [4], P('grp'), may hold values from 1024 to 4096, as said below
- cotangent: bfloat16 [4, 4096, 1280], P('grp', ('seq', 'shard')), may hold values from -6 to 6
Outputs:
- result: bfloat16 [4, 4096, 1280], P('grp', ('seq', 'shard'))
- grad_input: float32 [4, 4096, 1280], P('grp', ('seq', 'shard'))
- grad_query: float32 [1280, 1280], P('shard')
- grad_key: float32 [1280, 1280], P('shard')
- grad_value: float32 [1280, 1280], P('shard')
- grad_outproj: float32 [1280, 1280], P('shard')
- grad_up: float32 [1280, 5120], P('shard')
- grad_gate: float32 [1280, 5120], P('shard')
- grad_down: float32 [5120, 1280], P('shard')
- grad_scale_qk: float32 [1280], P('shard')
- grad_alpha_attn: float32 [1280], P('shard')
- grad_alpha_mlp: float32 [1280], P('shard')
- grad_scale_up: float32 [5120], P('shard')
- grad_scale_gate: float32 [5120], P('shard')
Inputs may be any that keep to these rules, and one draw needn't show every extreme that they name: `lengths`: each slot holds one sequence from its first position on; positions from its length on are padding. Some slot is full in every draw.
All inputs are finite; a program needn't handle non-finite values.
Results may differ from a plain program's by a relative error of at most 0.028.
Values may be sent and summed in bfloat16 or wider, within the bound.
A program may use at most 320 MiB of HBM per device.

v0:
```python
import math

import jax
import jax.numpy as jnp
from jax import lax
from jax.sharding import PartitionSpec as P

HEADS = 20
HDIM = 64


def in_one_piece(arrays, axis, dim, along):
    columns = [a.reshape(*a.shape[:along], -1) for a in arrays]
    both = jnp.concatenate(columns, axis=along)
    out, at, outs = (lax.all_gather(both, axis, axis=dim, tiled=True), 0, [])
    for a, column in zip(arrays, columns):
        slab = out[..., at : at + column.shape[along]]
        outs.append(slab.reshape(*slab.shape[:along], *a.shape[along:]))
        at += column.shape[along]
    return tuple(outs)


def in_one_piece_2(arrays, axis, dim, along):
    ends, at = ([], 0)
    for a in arrays[:-1]:
        at += a.shape[along]
        ends.append(at)
    both = jnp.concatenate(arrays, axis=along)
    return tuple(jnp.split(lax.all_gather(both, axis, axis=dim, tiled=True), ends, axis=along))


def packed_total(arrays, axis):
    ends = [0]
    for a in arrays:
        ends.append(ends[-1] + a.size)
    so_far = lax.psum(jnp.concatenate([a.ravel() for a in arrays]), axis)
    return tuple((so_far[b:e].reshape(a.shape) for a, b, e in zip(arrays, ends, ends[1:])))


def unit_rms(values):
    return values * lax.rsqrt(jnp.mean(values * values, axis=-1, keepdims=True) + 1e-06)


def rotate(values, positions):
    rows = values.shape[0]
    width = values.shape[1] // HEADS
    half = width // 2
    freqs = jnp.exp(jnp.arange(half, dtype=jnp.float32) * (-2.0 * math.log(10000.0) / width))
    angles = positions.astype(jnp.float32)[:, None] * freqs[None, :]
    cosine = jnp.cos(angles)[:, None, :]
    sine = jnp.sin(angles)[:, None, :]
    shaped = values.reshape(rows, HEADS, width)
    former = shaped[..., :half]
    latter = shaped[..., half:]
    turned = jnp.concatenate(
        [former * cosine - latter * sine, latter * cosine + former * sine], axis=-1
    )
    return turned.reshape(rows, HEADS * width)


def head_norm(values, positions, scale):
    rows = values.shape[0]
    turned = rotate(values, positions)
    return unit_rms(turned.reshape(rows, HEADS, -1)).reshape(values.shape) * scale


def attn_mix(states, mixed, rate):
    return unit_rms(states + rate * (unit_rms(mixed) - states))


def mlp_input(up_part, gate_part, scale_up, scale_gate):
    return up_part * scale_up * jax.nn.silu(gate_part * scale_gate)


def mlp_mix(first, down_part, rate, valid_rows):
    return unit_rms(first + rate * (unit_rms(down_part) - first)) * valid_rows


def times_transposed(left, right):
    return lax.dot_general(
        left, right, (((1,), (1,)), ((), ())), preferred_element_type=jnp.float32
    )


def outer_sum(left, right):
    return lax.dot_general(
        left, right, (((0,), (0,)), ((), ())), preferred_element_type=jnp.float32
    )


def key_positions(first_row, count, group_rows, tokens_here, shard_count):
    index = first_row + jnp.arange(count, dtype=jnp.int32)
    owner = index // group_rows
    within = index % group_rows
    return (within // tokens_here * shard_count + owner) * tokens_here + within % tokens_here


def shards(
    states,
    w_query,
    w_key,
    w_value,
    w_out,
    w_up,
    w_gate,
    w_down,
    scale_qk,
    alpha_attn,
    alpha_mlp,
    scale_up,
    scale_gate,
    lengths,
    cotangent,
):
    tokens_here = states.shape[1]
    seq_count = lax.axis_size("seq")
    shard_count = lax.axis_size("shard")
    shard_index = lax.axis_index("shard")
    block_index = lax.axis_index("seq") * shard_count + shard_index
    positions = block_index * tokens_here + jnp.arange(tokens_here, dtype=jnp.int32)
    length = lengths[0]
    valid_rows = (positions < length).astype(jnp.float32)[:, None]
    inputs = states[0]
    residual = inputs.astype(jnp.float32)
    local_heads = HEADS // seq_count
    group_rows = seq_count * tokens_here
    score_scale = HDIM ** (-0.5)
    attn_full = in_one_piece((w_query, w_key, w_value, w_out, scale_qk, alpha_attn), "shard", 0, 1)
    full_query, full_key, full_value, full_out, full_scale_qk, full_alpha_attn = attn_full
    scale_qk_f = full_scale_qk.astype(jnp.float32)
    alpha_attn_f = full_alpha_attn.astype(jnp.float32)
    q_raw = jnp.dot(inputs, full_query, preferred_element_type=jnp.float32)
    k_raw = jnp.dot(inputs, full_key, preferred_element_type=jnp.float32)
    v_low = jnp.dot(inputs, full_value, preferred_element_type=jnp.float32).astype(jnp.bfloat16)
    q_low = head_norm(q_raw, positions, scale_qk_f).astype(jnp.bfloat16)
    k_low = head_norm(k_raw, positions, scale_qk_f).astype(jnp.bfloat16)
    heads_q, heads_k, heads_v = (
        lax.all_to_all(q_low, "seq", split_axis=1, concat_axis=0, tiled=True),
        lax.all_to_all(k_low, "seq", split_axis=1, concat_axis=0, tiled=True),
        lax.all_to_all(v_low, "seq", split_axis=1, concat_axis=0, tiled=True),
    )
    query_count = heads_q.shape[0]
    query_heads = heads_q.reshape(query_count, local_heads, HDIM)
    query_pos = key_positions(
        shard_index * group_rows, query_count, group_rows, tokens_here, shard_count
    )

    def split_blocks(piece, first_row):
        key_piece, value_piece = piece
        count = key_piece.shape[0]
        size = 512
        blocks = count // size
        key_pos = key_positions(first_row, count, group_rows, tokens_here, shard_count).reshape(
            blocks, size
        )
        key_blocks = key_piece.reshape(blocks, size, local_heads, HDIM)
        value_blocks = value_piece.reshape(blocks, size, local_heads, HDIM)
        return (key_blocks, value_blocks, key_pos)

    def allowed_of(positions_block):
        return (
            (positions_block[None, :] <= query_pos[:, None]) & (positions_block[None, :] < length)
        )[:, None, :]

    start_state = (
        jnp.full((query_count, local_heads), -1e30, jnp.float32),
        jnp.zeros((query_count, local_heads), jnp.float32),
        jnp.zeros((query_count, local_heads, HDIM), jnp.float32),
    )
    whole_keys = in_one_piece_2((heads_k, heads_v), "shard", 0, 1)
    carry = start_state

    def attend_inner(state, block_in):
        key_block, value_block, positions_block = block_in
        allowed = allowed_of(positions_block)
        scores = (
            jnp.einsum("qhd,khd->qhk", query_heads, key_block, preferred_element_type=jnp.float32)
            * score_scale
        )
        scores = jnp.where(allowed, scores, -1e30)
        run_max, run_total, run_acc = state
        new_max = jnp.maximum(run_max, jnp.max(scores, axis=-1))
        factor = jnp.exp(run_max - new_max)
        weights = jnp.where(allowed, jnp.exp(scores - new_max[..., None]), 0.0)
        run_total = run_total * factor + jnp.sum(weights, axis=-1)
        run_acc = run_acc * factor[..., None] + jnp.einsum(
            "qhk,khd->qhd",
            weights.astype(jnp.bfloat16),
            value_block,
            preferred_element_type=jnp.float32,
        )
        return ((new_max, run_total, run_acc), None)

    carry, unused = lax.scan(attend_inner, carry, split_blocks(whole_keys, 0))
    run_max, run_total, run_acc = carry
    attended_heads = run_acc / run_total[..., None]
    log_total = run_max + jnp.log(run_total)
    attended_low = attended_heads.reshape(query_count, -1).astype(jnp.bfloat16)
    tokens_att = lax.all_to_all(attended_low, "seq", split_axis=0, concat_axis=1, tiled=True)
    mixed = jnp.dot(tokens_att, full_out, preferred_element_type=jnp.float32)
    first = attn_mix(residual, mixed, alpha_attn_f)
    first_low = first.astype(jnp.bfloat16)
    mlp_full = (
        *in_one_piece_2((w_up, w_gate), "shard", 0, 1),
        *in_one_piece((w_down, scale_up, scale_gate), "shard", 0, 1),
        lax.all_gather(alpha_mlp, "shard", axis=0, tiled=True),
    )
    full_up, full_gate, full_down, full_scale_up, full_scale_gate, full_alpha_mlp = mlp_full
    scale_up_f = full_scale_up.astype(jnp.float32)
    scale_gate_f = full_scale_gate.astype(jnp.float32)
    alpha_mlp_f = full_alpha_mlp.astype(jnp.float32)
    up_part = jnp.dot(first_low, full_up, preferred_element_type=jnp.float32)
    gate_part = jnp.dot(first_low, full_gate, preferred_element_type=jnp.float32)
    hidden_low = mlp_input(up_part, gate_part, scale_up_f, scale_gate_f).astype(jnp.bfloat16)
    down_part = jnp.dot(hidden_low, full_down, preferred_element_type=jnp.float32)
    output = mlp_mix(first, down_part, alpha_mlp_f, valid_rows)
    cot = cotangent[0].astype(jnp.float32)
    unused_out, back_mix = jax.vjp(
        lambda left, right, rate: mlp_mix(left, right, rate, valid_rows),
        first,
        down_part,
        alpha_mlp_f,
    )
    d_first, d_down, grad_alpha_m = back_mix(cot)
    d_down_low = d_down.astype(jnp.bfloat16)
    back_up, back_gate, back_down = (full_up, full_gate, full_down)
    d_hidden = times_transposed(d_down_low, back_down)
    grad_down = outer_sum(hidden_low, d_down_low)
    unused_in, back_in = jax.vjp(mlp_input, up_part, gate_part, scale_up_f, scale_gate_f)
    d_up, d_gate, grad_scale_u, grad_scale_g = back_in(d_hidden)
    d_up_low = d_up.astype(jnp.bfloat16)
    d_gate_low = d_gate.astype(jnp.bfloat16)
    d_first = (
        d_first + times_transposed(d_up_low, back_up) + times_transposed(d_gate_low, back_gate)
    )
    grad_up = outer_sum(first_low, d_up_low)
    grad_gate = outer_sum(first_low, d_gate_low)
    unused_attn, back_attn = jax.vjp(attn_mix, residual, mixed, alpha_attn_f)
    d_states, d_mixed, grad_alpha_a = back_attn(d_first)
    d_mixed_low = d_mixed.astype(jnp.bfloat16)
    back_query, back_key, back_value, back_out = (full_query, full_key, full_value, full_out)
    d_att_low = times_transposed(d_mixed_low, back_out).astype(jnp.bfloat16)
    grad_outproj = outer_sum(tokens_att, d_mixed_low)
    heads_grad = lax.all_to_all(d_att_low, "seq", split_axis=1, concat_axis=0, tiled=True)
    grad_heads = heads_grad.reshape(query_count, local_heads, HDIM)
    delta = jnp.sum(grad_heads.astype(jnp.float32) * attended_heads, axis=-1)
    key_rows_kept = 1
    grad_query_acc = jnp.zeros((query_count, local_heads, HDIM), jnp.float32)
    grad_keys = jnp.zeros((key_rows_kept, local_heads * HDIM), jnp.float32)
    grad_values = jnp.zeros((key_rows_kept, local_heads * HDIM), jnp.float32)

    def return_inner(acc, block_in):
        key_block, value_block, positions_block = block_in
        allowed = allowed_of(positions_block)
        scores = (
            jnp.einsum("qhd,khd->qhk", query_heads, key_block, preferred_element_type=jnp.float32)
            * score_scale
        )
        weights = jnp.where(allowed, jnp.exp(scores - log_total[..., None]), 0.0)
        weight_grad = jnp.einsum(
            "qhd,khd->qhk", grad_heads, value_block, preferred_element_type=jnp.float32
        )
        score_grad = (weights * (weight_grad - delta[..., None])).astype(jnp.bfloat16)
        acc = acc + score_scale * jnp.einsum(
            "qhk,khd->qhd", score_grad, key_block, preferred_element_type=jnp.float32
        )
        return (acc, None)

    key_blocks, value_blocks, key_pos = split_blocks(whole_keys, 0)
    count = whole_keys[0].shape[0]
    grad_query_acc, stacked = lax.scan(
        return_inner, grad_query_acc, (key_blocks, value_blocks, key_pos)
    )
    grad_q_heads, grad_keys, grad_values = (grad_query_acc, grad_keys, grad_values)
    own_key_heads = heads_k.reshape(query_count, local_heads, HDIM)
    own_value_heads = heads_v.reshape(query_count, local_heads, HDIM)
    all_lse, all_delta = in_one_piece_2((log_total, delta), "shard", 0, 1)
    owner_start = (
        jnp.zeros((query_count, local_heads, HDIM), jnp.float32),
        jnp.zeros((query_count, local_heads, HDIM), jnp.float32),
    )
    carry = owner_start
    query_piece, grad_piece = in_one_piece_2((heads_q, heads_grad), "shard", 0, 1)
    count = query_piece.shape[0]
    size = 512
    blocks = count // size
    pos_blocks = key_positions(jnp.int32(0), count, group_rows, tokens_here, shard_count).reshape(
        blocks, size
    )
    lse_piece = all_lse.reshape(blocks, size, local_heads)
    delta_piece = all_delta.reshape(blocks, size, local_heads)
    query_blocks = query_piece.reshape(blocks, size, local_heads, HDIM)
    grad_blocks = grad_piece.reshape(blocks, size, local_heads, HDIM)

    def owner_inner(acc, block_in):
        key_acc, value_acc = acc
        q_block, g_block, p_block, lse_block, delta_block = block_in
        allowed = ((query_pos[None, :] <= p_block[:, None]) & (query_pos[None, :] < length))[
            :, None, :
        ]
        scores = (
            jnp.einsum("qhd,khd->qhk", q_block, own_key_heads, preferred_element_type=jnp.float32)
            * score_scale
        )
        weights = jnp.where(allowed, jnp.exp(scores - lse_block[..., None]), 0.0)
        value_acc = value_acc + jnp.einsum(
            "qhk,qhd->khd",
            weights.astype(jnp.bfloat16),
            g_block,
            preferred_element_type=jnp.float32,
        )
        weight_grad = jnp.einsum(
            "qhd,khd->qhk", g_block, own_value_heads, preferred_element_type=jnp.float32
        )
        score_grad = (weights * (weight_grad - delta_block[..., None])).astype(jnp.bfloat16)
        key_acc = key_acc + score_scale * jnp.einsum(
            "qhk,qhd->khd", score_grad, q_block, preferred_element_type=jnp.float32
        )
        return ((key_acc, value_acc), None)

    carry, unused = lax.scan(
        owner_inner, carry, (query_blocks, grad_blocks, pos_blocks, lse_piece, delta_piece)
    )
    own_keys, own_values = carry
    dk_low = own_keys.reshape(query_count, -1).astype(jnp.bfloat16)
    dv_low = own_values.reshape(query_count, -1).astype(jnp.bfloat16)
    dq_low = grad_q_heads.reshape(query_count, -1).astype(jnp.bfloat16)
    tok_dq, tok_dk, tok_dv = (
        lax.all_to_all(dq_low, "seq", split_axis=0, concat_axis=1, tiled=True),
        lax.all_to_all(dk_low, "seq", split_axis=0, concat_axis=1, tiled=True),
        lax.all_to_all(dv_low, "seq", split_axis=0, concat_axis=1, tiled=True),
    )
    unused_q, back_q = jax.vjp(
        lambda raw, scale: head_norm(raw, positions, scale), q_raw, scale_qk_f
    )
    d_q_raw, grad_sqk_q = back_q(tok_dq.astype(jnp.float32))
    unused_k, back_k = jax.vjp(
        lambda raw, scale: head_norm(raw, positions, scale), k_raw, scale_qk_f
    )
    d_k_raw, grad_sqk_k = back_k(tok_dk.astype(jnp.float32))
    d_q_low = d_q_raw.astype(jnp.bfloat16)
    d_k_low = d_k_raw.astype(jnp.bfloat16)
    grad_input = (
        d_states
        + times_transposed(d_q_low, back_query)
        + times_transposed(d_k_low, back_key)
        + times_transposed(tok_dv, back_value)
    )
    grad_query = outer_sum(inputs, d_q_low)
    grad_key = outer_sum(inputs, d_k_low)
    grad_value = outer_sum(inputs, tok_dv)
    grad_sqk = grad_sqk_q + grad_sqk_k
    shares = (
        lax.psum_scatter(
            grad_query.astype(jnp.bfloat16), "shard", scatter_dimension=0, tiled=True
        ).astype(jnp.float32),
        lax.psum_scatter(
            grad_key.astype(jnp.bfloat16), "shard", scatter_dimension=0, tiled=True
        ).astype(jnp.float32),
        lax.psum_scatter(
            grad_value.astype(jnp.bfloat16), "shard", scatter_dimension=0, tiled=True
        ).astype(jnp.float32),
        lax.psum_scatter(
            grad_outproj.astype(jnp.bfloat16), "shard", scatter_dimension=0, tiled=True
        ).astype(jnp.float32),
        lax.psum_scatter(
            grad_up.astype(jnp.bfloat16), "shard", scatter_dimension=0, tiled=True
        ).astype(jnp.float32),
        lax.psum_scatter(
            grad_gate.astype(jnp.bfloat16), "shard", scatter_dimension=0, tiled=True
        ).astype(jnp.float32),
        lax.psum_scatter(
            grad_down.astype(jnp.bfloat16), "shard", scatter_dimension=0, tiled=True
        ).astype(jnp.float32),
        lax.psum_scatter(
            grad_sqk.astype(jnp.bfloat16), "shard", scatter_dimension=0, tiled=True
        ).astype(jnp.float32),
        lax.psum_scatter(
            grad_alpha_a.astype(jnp.bfloat16), "shard", scatter_dimension=0, tiled=True
        ).astype(jnp.float32),
        lax.psum_scatter(
            grad_alpha_m.astype(jnp.bfloat16), "shard", scatter_dimension=0, tiled=True
        ).astype(jnp.float32),
        lax.psum_scatter(
            grad_scale_u.astype(jnp.bfloat16), "shard", scatter_dimension=0, tiled=True
        ).astype(jnp.float32),
        lax.psum_scatter(
            grad_scale_g.astype(jnp.bfloat16), "shard", scatter_dimension=0, tiled=True
        ).astype(jnp.float32),
    )
    totals = tuple(
        (
            part.astype(jnp.float32)
            for part in packed_total(
                (
                    shares[0].astype(jnp.bfloat16),
                    shares[1].astype(jnp.bfloat16),
                    shares[2].astype(jnp.bfloat16),
                    shares[3].astype(jnp.bfloat16),
                    shares[4].astype(jnp.bfloat16),
                    shares[5].astype(jnp.bfloat16),
                    shares[6].astype(jnp.bfloat16),
                    shares[7].astype(jnp.bfloat16),
                    shares[8].astype(jnp.bfloat16),
                    shares[9].astype(jnp.bfloat16),
                    shares[10].astype(jnp.bfloat16),
                    shares[11].astype(jnp.bfloat16),
                ),
                ("grp", "seq"),
            )
        )
    )
    return (
        output.astype(jnp.bfloat16)[None],
        grad_input[None],
        totals[0],
        totals[1],
        totals[2],
        totals[3],
        totals[4],
        totals[5],
        totals[6],
        totals[7],
        totals[8],
        totals[9],
        totals[10],
        totals[11],
    )


def solution(mesh):
    return jax.shard_map(
        shards,
        mesh=mesh,
        in_specs=(
            P("grp", ("seq", "shard"), None),
            P("shard", None),
            P("shard", None),
            P("shard", None),
            P("shard", None),
            P("shard", None),
            P("shard", None),
            P("shard", None),
            P("shard"),
            P("shard"),
            P("shard"),
            P("shard"),
            P("shard"),
            P("grp"),
            P("grp", ("seq", "shard"), None),
        ),
        out_specs=(
            P("grp", ("seq", "shard"), None),
            P("grp", ("seq", "shard"), None),
            P("shard", None),
            P("shard", None),
            P("shard", None),
            P("shard", None),
            P("shard", None),
            P("shard", None),
            P("shard", None),
            P("shard"),
            P("shard"),
            P("shard"),
            P("shard"),
            P("shard"),
        ),
        check_vma=False,
    )
```

profile of v0, /device:TPU:1, one launch (start us, length us, event | category | flops | bytes accessed | tf_op | source)
XLA Modules:
  0.0 1339.2 jit_solution(1696350505632412736)
XLA Ops:
  14.8 93.8 %all-gather.6.cloned.1.call-done = bf16[1280,5122]{1,0:T(8,128)(2,1)} async-done(((bf16[80,5122]{1,0:T(8,128)(2,1)}), bf16[1280,5122]{1,0:T(8,128)(2,1)}) %all-gather.6.cloned.1.call-update) | async-done | bytes 13112336 | tf_op jit(solution)/shard_map/all_gather | solution.py:15
  135.8 31.9 %all-reduce.4 = bf16[1280]{0:T(1024)(128)(2,1)S(1)} all-reduce(bf16[1280]{0:T(1024)(128)(2,1)S(1)} %dynamic-update-slice), channel_id=1, replica_groups=mesh['grp'=4,'seq'=2,'shard'=16] {'shard'}, use_global_device_ids=true, to_apply=%add.4 | all-reduce | flops 1280 | bytes 5120
  167.8 11.5 all_to_all.124
  180.1 30.9 %all-gather.12.cloned.1.call-done = bf16[5120,1282]{1,0:T(8,128)(2,1)} async-done(((bf16[320,1282]{1,0:T(8,128)(2,1)}), bf16[5120,1282]{1,0:T(8,128)(2,1)}) %all-gather.12.cloned.1.call-update) | async-done | bytes 13127696 | tf_op jit(solution)/shard_map/all_gather | solution.py:15
  214.1 79.4 %all-gather.8.cloned.1.call-done = bf16[4096,1280]{1,0:T(8,128)(2,1)} async-done(((bf16[256,1280]{1,0:T(8,128)(2,1)}), bf16[4096,1280]{1,0:T(8,128)(2,1)}) %all-gather.8.cloned.1.call-update) | async-done | bytes 10485776 | tf_op jit(solution)/shard_map/all_gather | solution.py:29
  293.5 8.8 fusion.209
  302.3 8.3 copy.145
  310.6 5.9 copy.183
  320.7 8.4 copy.147
  329.1 6.1 copy.184
  339.4 99.1 %while.39 = (s32[]{:T(128)}, f32[256,10]{0,1:T(8,128)S(1)}, f32[256,10]{0,1:T(8,128)S(1)}, f32[256,10,64]{0,2,1:T(8,128)S(1)}, s32[8,512]{1,0:T(8,128)S(1)}, /*i...) while((s32[]{:T(128)}, f32[256,10]{0,1:T(8,128)S(1)}, ...), condition=%wide.region_5.6_spmd.clone, body=%wide.region_2.5_spmd.clone.sunk | while | flops 353361664 | bytes 40347816 | solution.py:194
  446.6 8.8 all-gather.10.cloned.1.call-done
  455.4 5.8 fusion.120
  461.2 6.1 multiply_convert_fusion.2
  467.3 6.5 multiply_reduce_fusion.11
  476.3 8.9 multiply_reduce_fusion
  485.3 8.5 fusion.118
  493.8 7.6 multiply_reduce_fusion.8
  515.7 8.5 convolution_convert_fusion.1
  524.3 8.0 convolution_convert_fusion.2
  536.3 8.0 convolution_convert_fusion
  545.4 82.9 %while.40 = (s32[]{:T(128)}, f32[256,10,64]{0,2,1:T(8,128)S(1)}, bf16[8,512,10,64]{1,3,2,0:T(8,128)(2,1)}, s32[8,512]{1,0:T(8,128)S(1)}, s32[]{:T(128)}, /*index...) while((s32[]{:T(128)}, f32[256,10,64]{0,2,1:T(8,128)S(1)}, ...), condition=%wide.region_16.17_spmd.clone, body=%wide.region_15.16_spmd.clone.sunk | while | flops 511945984 | bytes 14711443 | solution.py:271
  602.2 5.2 fusion.282
  623.0 5.2 fusion.282
  632.8 19.5 %all_gather.27 = f32[4096,20]{0,1:T(8,128)S(1)} all-gather(f32[256,20]{0,1:T(8,128)S(1)} %pad_maximum_fusion.5), channel_id=1, replica_groups=mesh['grp'=4,'seq'=2,'shard'=16] {'shard'}, dimensions={0}, use_global_device_ids=true | all-gather | bytes 348160 | tf_op jit(solution)/shard_map/all_gather | solution.py:29
  653.5 8.9 fusion.208
  662.3 8.1 copy.159
  670.5 5.9 copy.185
  680.7 8.0 copy.161
  688.7 6.1 copy.187
  698.9 134.5 %while.41 = (s32[]{:T(128)}, f32[256,10,64]{0,2,1:T(8,128)S(1)}, f32[256,10,64]{0,2,1:T(8,128)}, bf16[8,512,10,64]{1,3,2,0:T(8,128)(2,1)}, s32[8,512]{1,0:T(8,12...) while((s32[]{:T(128)}, f32[256,10,64]{0,2,1:T(8,128)S(1)}, ...), condition=%wide.region_19.20_spmd.clone, body=%wide.region_18.19_spmd.clone.sunk | while | flops 685299456 | bytes 22256292 | solution.py:321
  705.5 5.5 fusion.293
  711.0 5.4 fusion.294
  722.6 5.9 fusion.293
  739.6 5.4 fusion.293
  756.1 5.5 fusion.293
  772.7 5.4 fusion.293
  789.1 5.5 fusion.293
  805.8 5.5 fusion.293
  822.7 5.7 fusion.293
  833.6 7.9 all_to_all.127
  873.9 60.1 %all-reduce.10 = (bf16[1280]{0:T(1024)(128)(2,1)S(1)}, bf16[1280]{0:T(1024)(128)(2,1)S(1)}, bf16[1280]{0:T(1024)(128)(2,1)S(1)}, bf16[5120]{0:T(1024)(128)(2,1)S(1)}, bf16[5120]{0:T(1024)(128)(2,1)S(1)}) all-reduce(bf16[1280]{0:T(1024)(128)(2,1)S(1)} %convert_element_type.389, ...), channel_id=9, replica_groups=mesh['grp'=4,'seq'=2,'shard'=16] {'shard'}, use_global_device_ids=true, to_apply=%region_30.31.clone | all-reduce | flops 14080 | bytes 56320
  937.0 30.3 %reduce-scatter.20.cloned.1.call-done = bf16[320,1280]{1,0:T(8,128)(2,1)} async-done(((bf16[5120,1280]{1,0:T(8,128)(2,1)}), bf16[320,1280]{1,0:T(8,128)(2,1)}) %reduce-scatter.20.cloned.1.call-update) | async-done | bytes 819216 | tf_op jit(solution)/shard_map/reduce_scatter | solution.py:372
  969.3 75.1 %reduce-scatter.24.cloned.1.call-done = bf16[80,1280]{1,0:T(8,128)(2,1)} async-done(((bf16[1280,1280]{1,0:T(8,128)(2,1)}), bf16[80,1280]{1,0:T(8,128)(2,1)}) %reduce-scatter.24.cloned.1.call-update) | async-done | bytes 204816 | tf_op jit(solution)/shard_map/reduce_scatter | solution.py:357
  1046.2 77.2 %reduce-scatter.22.cloned.1.call-done = bf16[80,1280]{1,0:T(8,128)(2,1)} async-done(((bf16[1280,1280]{1,0:T(8,128)(2,1)}), bf16[80,1280]{1,0:T(8,128)(2,1)}) %reduce-scatter.22.cloned.1.call-update) | async-done | bytes 204816 | tf_op jit(solution)/shard_map/reduce_scatter | solution.py:354
  1125.3 76.9 %reduce-scatter.26.cloned.1.call-done = bf16[80,1280]{1,0:T(8,128)(2,1)} async-done(((bf16[1280,1280]{1,0:T(8,128)(2,1)}), bf16[80,1280]{1,0:T(8,128)(2,1)}) %reduce-scatter.26.cloned.1.call-update) | async-done | bytes 204816 | tf_op jit(solution)/shard_map/reduce_scatter | solution.py:360
  1204.1 43.6 %concatenate.37 = bf16[1639280]{0:T(1024)(128)(2,1)} concatenate(bf16[102400]{0:T(1024)(128)(2,1)} %reshape.592, bf16[102400]{0:T(1024)(128)(2,1)} %reshape.593, bf16[102400]{0:T(1024)(128)(2,1)} %reshape.594, bf16[102400]{0:T(1024)(128)(2,1)} %reshape.595, bf16[409600]{0:T(1024)(128)(2,1)S(1)} %bitcast.385, bf16[409600]{0:T(1024)(128)(2,1)S(1)} %bitcast.384, ...), dimensions={0} | concatenate | bytes 6557120 | tf_op jit(solution)/shard_map/concatenate | solution.py:36
  1258.1 58.1 %all-reduce.13.cloned.1.call-done = bf16[1639280]{0:T(1024)(128)(2,1)} async-done(((bf16[1639280]{0:T(1024)(128)(2,1)}), bf16[1639280]{0:T(1024)(128)(2,1)}) %all-reduce.13.cloned.1.call-update) | async-done | bytes 3278576 | tf_op jit(solution)/shard_map/psum | solution.py:36
  (476 shorter events, 411.8 us)
Async XLA Ops:
  7.2 102.9 %copy-start.9 = (bf16[1,128,1280]{2,1,0:T(8,128)(2,1)S(1)}, bf16[1,128,1280]{2,1,0:T(8,128)(2,1)}, u32[]{:S(2)}) copy-start(bf16[1,128,1280]{2,1,0:T(8,128)(2,1)} %param.21) | copy-start | bytes 983044
  7.2 101.5 %all-gather.6.cloned.1.call-start = ((), (), s32[]{:S(2)}) async-start(), calls=%async_computation.15 | async-start | bytes 14274560 | tf_op jit(solution)/shard_map/all_gather | solution.py:15
  10.9 200.0 %all-gather.12.cloned.1.call-start = ((), (), s32[]{:S(2)}) async-start(), calls=%async_computation.18 | async-start | bytes 15319040 | tf_op jit(solution)/shard_map/all_gather | solution.py:15
  14.6 278.9 %all-gather.8.cloned.1.call-start = ((), (), s32[]{:S(2)}) async-start(), calls=%async_computation.16 | async-start | bytes 11141120 | tf_op jit(solution)/shard_map/all_gather | solution.py:29
  14.8 101.3 %copy-start.37 = (f32[128,32]{0,1:T(8,128)}, f32[128,32]{0,1:T(8,128)S(1)}, u32[]{:S(2)}) copy-start(f32[128,32]{0,1:T(8,128)S(1)} %get-tuple-element.590) | copy-start | bytes 49156
  14.8 101.3 %copy-start.39 = (f32[128,32]{0,1:T(8,128)}, f32[128,32]{0,1:T(8,128)S(1)}, u32[]{:S(2)}) copy-start(f32[128,32]{0,1:T(8,128)S(1)} %get-tuple-element.591) | copy-start | bytes 49156
  116.5 5.9 copy-start.45
  116.5 5.9 copy-start.47
  122.6 8.4 copy-start.34
  125.8 8.4 copy-start.52
  125.8 9.7 copy-start.53
  131.0 324.4 %all-gather.10.cloned.1.call-start = ((), (), s32[]{:S(2)}) async-start(), calls=%async_computation.17 | async-start | bytes 27852800 | tf_op jit(solution)/shard_map/all_gather | solution.py:29
  133.5 519.9 %all-gather.14.cloned.1.call-start = ((), (), s32[]{:S(2)}) async-start(), calls=%async_computation.19 | async-start | bytes 11141120 | tf_op jit(solution)/shard_map/all_gather | solution.py:29
  344.7 6.0 copy-start
  358.6 4.5 copy-start
  438.4 4.9 copy-start.23
  467.3 6.6 copy-start.25
  467.3 6.6 copy-start.19
  476.3 8.9 copy-start.32
  485.3 8.6 copy-start.20
  485.3 8.6 copy-start.26
  501.9 10.0 copy-start.28
  511.5 359.0 %reduce-scatter.14.cloned.1.call-start = ((), (), s32[]{:S(2)}) async-start(), calls=%async_computation.20 | async-start | bytes 3481600 | tf_op jit(solution)/shard_map/reduce_scatter | solution.py:363
  515.7 418.7 %reduce-scatter.18.cloned.1.call-start = ((), (), s32[]{:S(2)}) async-start(), calls=%async_computation.22 | async-start | bytes 13926400 | tf_op jit(solution)/shard_map/reduce_scatter | solution.py:369
  524.3 411.4 %reduce-scatter.16.cloned.1.call-start = ((), (), s32[]{:S(2)}) async-start(), calls=%async_computation.21 | async-start | bytes 13926400 | tf_op jit(solution)/shard_map/reduce_scatter | solution.py:366
  532.4 434.9 %reduce-scatter.20.cloned.1.call-start = ((), (), s32[]{:S(2)}) async-start(), calls=%async_computation.23 | async-start | bytes 13926400 | tf_op jit(solution)/shard_map/reduce_scatter | solution.py:372
  629.1 23.5 %all-to-all-start.5 = ((bf16[2,128,640]{1,2,0:T(8,128)(2,1)}), bf16[2,128,640]{1,2,0:T(8,128)(2,1)S(1)}, u32[]{:S(2)}, u32[]{:S(2)}) async-start(bf16[2,128,640]{1,2,0:T(8,128)(2,1)} %copy.157), calls=%async_computation.5 | async-start | bytes 655360 | tf_op jit(solution)/shard_map/all_to_all | solution.py:329
  632.8 411.5 %reduce-scatter.24.cloned.1.call-start = ((), (), s32[]{:S(2)}) async-start(), calls=%async_computation.26 | async-start | bytes 3481600 | tf_op jit(solution)/shard_map/reduce_scatter | solution.py:357
  652.7 9.7 copy-start.17
  698.9 142.7 %copy-start.2 = (f32[128,20,32]{0,2,1:T(8,128)S(1)}, f32[128,20,32]{0,2,1:T(8,128)}, u32[]{:S(2)}) copy-start(f32[128,20,32]{0,2,1:T(8,128)} %copy-done.1) | copy-start | bytes 983044
  698.9 142.7 %copy-start.4 = (f32[128,20,32]{0,2,1:T(8,128)S(1)}, f32[128,20,32]{0,2,1:T(8,128)}, u32[]{:S(2)}) copy-start(f32[128,20,32]{0,2,1:T(8,128)} %copy-done.3) | copy-start | bytes 983044
  698.9 142.7 %copy-start.6 = (f32[128,20,32]{0,2,1:T(8,128)S(1)}, f32[128,20,32]{0,2,1:T(8,128)}, u32[]{:S(2)}) copy-start(f32[128,20,32]{0,2,1:T(8,128)} %copy-done.5) | copy-start | bytes 983044
  698.9 142.7 %copy-start.8 = (f32[128,20,32]{0,2,1:T(8,128)S(1)}, f32[128,20,32]{0,2,1:T(8,128)}, u32[]{:S(2)}) copy-start(f32[128,20,32]{0,2,1:T(8,128)} %copy-done.7) | copy-start | bytes 983044
  833.4 8.6 copy-start.48
  833.4 8.6 copy-start.46
  833.4 8.6 copy-start.42
  833.4 8.7 copy-start.44
  833.4 9.1 copy-start.38
  833.4 9.1 copy-start.40
  848.8 274.7 %reduce-scatter.22.cloned.1.call-start = ((), (), s32[]{:S(2)}) async-start(), calls=%async_computation.25 | async-start | bytes 3481600 | tf_op jit(solution)/shard_map/reduce_scatter | solution.py:354
  856.2 346.1 %reduce-scatter.26.cloned.1.call-start = ((), (), s32[]{:S(2)}) async-start(), calls=%async_computation.27 | async-start | bytes 3481600 | tf_op jit(solution)/shard_map/reduce_scatter | solution.py:360
  864.2 9.7 copy-start.49
  864.2 9.7 copy-start.50
  864.2 9.7 copy-start.51
  867.7 448.5 %all-reduce.13.cloned.1.call-start = ((), (), s32[]{:S(2)}) async-start(), calls=%async_computation.24 | async-start | bytes 6557696 | tf_op jit(solution)/shard_map/psum | solution.py:36
  1046.2 201.5 %copy-start.22 = (f32[128,1280]{1,0:T(8,128)S(1)}, f32[128,1280]{1,0:T(8,128)}, u32[]{:S(2)}) copy-start(f32[128,1280]{1,0:T(8,128)} %copy-done.21) | copy-start | bytes 1966084
  1046.2 201.5 %copy-start.30 = (bf16[128,20,64]{0,2,1:T(8,128)(2,1)S(1)}, bf16[128,20,64]{0,2,1:T(8,128)(2,1)}, u32[]{:S(2)}) copy-start(bf16[128,20,64]{0,2,1:T(8,128)(2,1)} %copy-done.29) | copy-start | bytes 983044
  1247.8 6.3 copy-start.14
  (27 other events, 62.4 us)
Sparse Core Ops, SparseCore 0:
  11.0 97.5 all-gather.5
  111.4 99.5 all-gather.11
  213.6 79.8 all-gather.7
  296.1 159.2 all-gather.9
  511.6 79.8 all-gather.13
  594.7 74.3 reduce-scatter.13
  672.5 96.7 reduce-scatter.17
  773.2 95.0 reduce-scatter.15
  871.8 95.3 reduce-scatter.19
  970.8 73.5 reduce-scatter.23
  1048.1 75.3 reduce-scatter.21
  1127.0 75.1 reduce-scatter.25
  1247.9 68.2 all-reduce.12
where the time goes:
time: 1350 us; the launch traced here: 1340 us
  waiting for transfers between devices  531 us (39%)
  matrix products  353 us (26%)
  local copies, waits for them, and re-layouts  198 us (15%)
  blocking collectives  152 us (11%)
  other arithmetic  81.8 us (6%)
  between operations  18.2 us (1%)
    all_gather x2, waiting for transfers between devices, in_one_piece(): out, at, outs = (lax.all_gather(both, axis, axis=dim, tiled=True), 0, [])  125 us
    unnamed x2, blocking collectives  92 us
    all_gather x3, waiting for transfers between devices, in_one_piece_2(): lax.all_gather(both, axis, axis=dim, tiled=True)  88.2 us
    reduce_scatter x1, waiting for transfers between devices, shards(): lax.psum_scatter(grad_query.astype(jnp.bfloat16), 'shard', scatter_dimens...  77.2 us
    reduce_scatter x1, waiting for transfers between devices, shards(): lax.psum_scatter(grad_value.astype(jnp.bfloat16), 'shard', scatter_dimens...  76.9 us
    reduce_scatter x1, waiting for transfers between devices, shards(): lax.psum_scatter(grad_key.astype(jnp.bfloat16), 'shard', scatter_dimensio...  75.1 us
    unnamed x129, local copies, waits for them, and re-layouts  60.5 us
    psum x1, waiting for transfers between devices, packed_total(): so_far = lax.psum(jnp.concatenate([a.ravel() for a in arrays]), axis)  58.1 us
  transfers between devices with their start and end apart: 14, of which 9 were waited for; matrix products, arithmetic and copies ran while one was open for 38% of the time, Pallas kernels for 0%

commit v1 on v0

v1 whole, which is shorter than its diff:
```python
import functools
import math

import jax
import jax.numpy as jnp
import numpy as np
from jax import lax
from jax.experimental import pallas as pl
from jax.experimental.pallas import tpu as pltpu
from jax.sharding import PartitionSpec as P


D, HEADS, HDIM, FF = 1280, 20, 64, 5120
ROWS, BLOCKS, HG = 128, 4, 5
GROUP = HG * HDIM
EPS = 1e-6
BF, F32 = jnp.bfloat16, jnp.float32
MESH = pl.DeviceIdType.MESH
VMEM_LIMIT = 60 << 20


def here():
    s = lax.axis_index("shard")
    return lax.axis_index("grp"), lax.axis_index("seq"), s // 4, s % 4


def dev(x, c, z, y):
    return (x, c, z * 4 + y)


def worker(z):
    return ((z + 1) // 2) % 2


def owner_z(w, i):
    return i * (3 - 2 * w) + w


def step(v, d):
    return (v + d) % 4


def rcopy(src, dst, ss, rs, to):
    return pltpu.make_async_remote_copy(
        src_ref=src, dst_ref=dst, send_sem=ss, recv_sem=rs, device_id=to, device_id_type=MESH
    )


def lcopy(src, dst, sem):
    return pltpu.make_async_copy(src, dst, sem)


def landed(dst, sem):
    pltpu.make_async_copy(dst, dst, sem).wait()


def greet(peers):
    bar = pltpu.get_barrier_semaphore()
    for p in peers:
        pl.semaphore_signal(bar, inc=1, device_id=p, device_id_type=MESH)
    pl.semaphore_wait(bar, len(peers))


def z_peers(x, c, z, y):
    far = [dev(x, cc, step(z, d), y) for d in (1, 2, 3) for cc in (0, 1)]
    return [dev(x, 1 - c, z, y)] + far


def z_gather_start(src, dst, ss, rs, x, c, z, y):
    w = worker(z)
    slot = c * 2 + z // 2
    for d in (2, 1, 3):
        rcopy(src, dst.at[slot], ss.at[d], rs.at[slot], dev(x, w, step(z, d), y)).start()

    @pl.when(c == w)
    def _():
        lcopy(src, dst.at[slot], rs.at[slot]).start()

    @pl.when(c != w)
    def _():
        rcopy(src, dst.at[slot], ss.at[0], rs.at[slot], dev(x, w, z, y)).start()


def z_gather_wait(src, dst, ss, rs, c, z):
    for j in range(BLOCKS):
        landed(dst.at[j], rs.at[j])
    for d in (1, 2, 3):
        landed(src, ss.at[d])

    @pl.when(c != worker(z))
    def _():
        landed(src, ss.at[0])


def z_scatter_start(part, dst, ss, rs, x, c, z, y):
    for j in range(BLOCKS):
        oc, oz = j // 2, owner_z(c, j % 2)
        mine = jnp.logical_and(c == oc, z == oz)

        @pl.when(mine)
        def _(j=j):
            lcopy(part.at[j], dst.at[z], rs.at[z]).start()

        @pl.when(jnp.logical_not(mine))
        def _(j=j, oc=oc, oz=oz):
            rcopy(part.at[j], dst.at[z], ss.at[j], rs.at[z], dev(x, oc, oz, y)).start()


def z_scatter_wait(part, dst, ss, rs, c, z):
    for k in range(4):
        landed(dst.at[k], rs.at[k])
    for j in range(BLOCKS):
        mine = jnp.logical_and(c == j // 2, z == owner_z(c, j % 2))

        @pl.when(jnp.logical_not(mine))
        def _(j=j):
            landed(part.at[j], ss.at[j])


def remote_call(kernel, outs, ins_spaces, scratch, cid, name):
    any_spec = pl.BlockSpec(memory_space=pl.ANY)
    vmem = pl.BlockSpec(memory_space=pltpu.VMEM)
    return pl.pallas_call(
        kernel,
        out_shape=[jax.ShapeDtypeStruct(s, d) for s, d, _ in outs],
        in_specs=[any_spec if s == "a" else vmem for s in ins_spaces],
        out_specs=[any_spec if s == "a" else vmem for _, _, s in outs],
        scratch_shapes=scratch,
        compiler_params=pltpu.CompilerParams(
            collective_id=cid, has_side_effects=True, vmem_limit_bytes=VMEM_LIMIT
        ),
        name=name,
    )


def local_call(kernel, outs, n_in, scratch, name, smem=0):
    vmem = pl.BlockSpec(memory_space=pltpu.VMEM)
    sm = pl.BlockSpec(memory_space=pltpu.SMEM)
    return pl.pallas_call(
        kernel,
        out_shape=[jax.ShapeDtypeStruct(s, d) for s, d in outs],
        in_specs=[sm] * smem + [vmem] * n_in,
        out_specs=[vmem for _ in outs],
        scratch_shapes=scratch,
        compiler_params=pltpu.CompilerParams(vmem_limit_bytes=VMEM_LIMIT),
        name=name,
    )


def dma(*shape):
    return pltpu.SemaphoreType.DMA(shape)


def open_kernel(st, wq, vec, wo, xg, wqkv, vecs, wog, xs, xr, s1, r1, s2, r2, s3, r3, sv, rv, so, ro, lo):
    x, c, z, y = here()
    sib = dev(x, 1 - c, z, y)
    half = pl.ds(pl.multiple_of(c * 640, 128), 640)
    other = pl.ds(pl.multiple_of((1 - c) * 640, 128), 640)
    greet(z_peers(x, c, z, y) + [dev(x, c, z, step(y, d)) for d in (1, 2, 3)])
    for d in (2, 1, 3):
        z2 = step(z, d)
        rcopy(wq.at[c, z2], wqkv.at[c, z, y], s1.at[d], r1.at[z], dev(x, c, z2, y)).start()
        rcopy(vec, vecs.at[z, y], sv.at[0, d], rv.at[0, z], dev(x, c, z2, y)).start()
    own = lcopy(wq.at[c, z], wqkv.at[c, z, y], lo.at[0])
    own.start()
    own_v = lcopy(vec, vecs.at[z, y], lo.at[1])
    own_v.start()
    own_o = lcopy(wo.at[:, half], wog.at[y, :, half], lo.at[2])
    own_o.start()
    for d in (2, 1, 3):
        rcopy(wo.at[:, half], wog.at[y, :, half], so.at[0, d], ro.at[0, y], dev(x, c, z, step(y, d))).start()
    rcopy(wo.at[:, half], wog.at[y, :, half], so.at[0, 0], ro.at[1, y], sib).start()
    z_gather_start(st, xg, xs, xr, x, c, z, y)
    for d in (1, 2, 3):
        z2 = step(z, d)
        landed(wqkv.at[c, z2, y], r1.at[z2])
        landed(vecs.at[z2, y], rv.at[0, z2])
    own.wait()
    own_v.wait()
    for d in (2, 1, 3):
        to = dev(x, c, z, step(y, d))
        rcopy(wqkv.at[c, :, y], wqkv.at[c, :, y], s2.at[d], r2.at[y], to).start()
        rcopy(vecs.at[:, y], vecs.at[:, y], sv.at[1, d], rv.at[1, y], to).start()
    rcopy(wqkv.at[c, :, y], wqkv.at[c, :, y], s3.at[0], r3.at[y], sib).start()
    for d in (1, 3, 2):
        y2 = step(y, d)
        landed(wog.at[y2, :, half], ro.at[0, y2])
        rcopy(wog.at[y2, :, half], wog.at[y2, :, half], so.at[1, d], ro.at[1, y2], sib).start()
        landed(wqkv.at[c, :, y2], r2.at[y2])
        rcopy(wqkv.at[c, :, y2], wqkv.at[c, :, y2], s3.at[d], r3.at[y2], sib).start()
    z_gather_wait(st, xg, xs, xr, c, z)
    own_o.wait()
    for k in range(4):
        landed(wqkv.at[1 - c, :, k], r3.at[k])
        landed(wog.at[k, :, other], ro.at[1, k])
        landed(wqkv.at[c, :, k], s3.at[k])
    landed(wo.at[:, half], so.at[0, 0])
    for d in (1, 2, 3):
        landed(vecs.at[:, step(y, d)], rv.at[1, step(y, d)])
        landed(wq.at[c, z], s1.at[d])
        landed(vec, sv.at[0, d])
        landed(vecs.at[:, y], sv.at[1, d])
        landed(wqkv.at[c, :, y], s2.at[d])
        landed(wo.at[:, half], so.at[0, d])
        landed(wog.at[y, :, half], so.at[1, d])


def open_gather(st, wq, vec, wo):
    return remote_call(
        open_kernel,
        [
            ((BLOCKS, ROWS, D), BF, "a"),
            ((2, 4, 4, 80, 512), BF, "a"),
            ((4, 4, 8, 896), F32, "a"),
            ((4, 80, D), BF, "a"),
        ],
        "aaaa",
        [dma(4), dma(4), dma(4), dma(4), dma(4), dma(4), dma(4), dma(4), dma(2, 4), dma(2, 4), dma(2, 4), dma(2, 4), dma(3)],
        0,
        "open_gather",
    )(st, wq, vec, wo)


def ff_kernel(wu, wg, wd, wff, wdn, s1, r1, s2, r2, s3, r3, lo):
    x, c, z, y = here()
    sib = dev(x, 1 - c, z, y)
    half = pl.ds(pl.multiple_of(c * 640, 128), 640)
    other = pl.ds(pl.multiple_of((1 - c) * 640, 128), 640)
    greet(
        [sib]
        + [dev(x, c, step(z, d), y) for d in (1, 2, 3)]
        + [dev(x, c, z, step(y, d)) for d in (1, 2, 3)]
    )

    def columns(ref, k):
        return ref.at[:, pl.ds(pl.multiple_of(k * D, 128), D)]

    for which, ref in ((0, wu), (1, wg)):

        @pl.when(c == which)
        def _(ref=ref):
            for d in (2, 1, 3):
                z2 = step(z, d)
                rcopy(columns(ref, z2), wff.at[c, z, y], s1.at[d], r1.at[z], dev(x, c, z2, y)).start()
            lcopy(columns(ref, z), wff.at[c, z, y], lo.at[0]).start()

    lcopy(wd.at[:, half], wdn.at[y, :, half], lo.at[1]).start()
    for d in (2, 1, 3):
        rcopy(wd.at[:, half], wdn.at[y, :, half], s2.at[0, d], r2.at[0, y], dev(x, c, z, step(y, d))).start()
    rcopy(wd.at[:, half], wdn.at[y, :, half], s3.at[0, 0], r3.at[0, y], sib).start()
    for d in (1, 2, 3):
        landed(wff.at[c, step(z, d), y], r1.at[step(z, d)])
    landed(wff.at[c, z, y], lo.at[0])
    for d in (2, 1, 3):
        rcopy(wff.at[c, :, y], wff.at[c, :, y], s2.at[1, d], r2.at[1, y], dev(x, c, z, step(y, d))).start()
    rcopy(wff.at[c, :, y], wff.at[c, :, y], s3.at[1, 0], r3.at[1, y], sib).start()
    for d in (1, 3, 2):
        y2 = step(y, d)
        landed(wdn.at[y2, :, half], r2.at[0, y2])
        rcopy(wdn.at[y2, :, half], wdn.at[y2, :, half], s3.at[0, d], r3.at[0, y2], sib).start()
    for d in (1, 3, 2):
        y2 = step(y, d)
        landed(wff.at[c, :, y2], r2.at[1, y2])
        rcopy(wff.at[c, :, y2], wff.at[c, :, y2], s3.at[1, d], r3.at[1, y2], sib).start()
    landed(wdn.at[y, :, half], lo.at[1])
    for k in range(4):
        landed(wdn.at[k, :, other], r3.at[0, k])
        landed(wff.at[1 - c, :, k], r3.at[1, k])
        landed(wdn.at[k, :, half], s3.at[0, k])
        landed(wff.at[c, :, k], s3.at[1, k])
    for d in (1, 2, 3):
        landed(wff.at[c, z, y], s1.at[d])
        landed(wdn.at[y, :, half], s2.at[0, d])
        landed(wff.at[c, :, y], s2.at[1, d])


def ff_gather(wu, wg, wd):
    return remote_call(
        ff_kernel,
        [((2, 4, 4, 80, D), BF, "a"), ((4, 320, D), BF, "a")],
        "aaa",
        [dma(4), dma(4), dma(2, 4), dma(2, 4), dma(2, 4), dma(2, 4), dma(2)],
        1,
        "ff_gather",
    )(wu, wg, wd)


def rope_tables():
    freqs = np.exp(np.arange(32) * (-2.0 * math.log(10000.0) / 64))
    freqs = np.concatenate([freqs, freqs])
    sign = np.concatenate([-np.ones(32), np.ones(32)])
    inner = np.arange(ROWS)[:, None] * freqs
    outer = (np.arange(32) * ROWS)[:, None] * freqs
    return (
        np.stack([np.cos(inner), np.sin(inner) * sign]).astype(np.float32),
        np.stack([np.cos(outer), np.sin(outer) * sign]).astype(np.float32),
    )


def block_index(c, y, j):
    return (j // 2) * 16 + owner_z(c, j % 2) * 4 + y


def turn_of(inner, outer, b):
    oc = outer[0, pl.ds(b, 1), :]
    os = outer[1, pl.ds(b, 1), :]
    return oc * inner[0] - os * inner[1], os * inner[0] + oc * inner[1]


def swap(v):
    return jnp.concatenate([v[:, 32:], v[:, :32]], axis=1)


def qkv_kernel(xg, w, scale, inner, outer, q_out, kv_out, t_out, y0, y1):
    _, c, _, y = here()
    xs = xg[...]
    y0[...] = jnp.dot(xs, w[0], preferred_element_type=F32)
    y1[...] = jnp.dot(xs, w[1], preferred_element_type=F32)

    def per_block(j, carry):
        rows = pl.ds(pl.multiple_of(j * ROWS, ROWS), ROWS)
        cosine, sine = turn_of(inner, outer, block_index(c, y, j))
        a0, a1 = y0[rows, :], y1[rows, :]
        for h in range(HG):
            cols = slice(h * HDIM, (h + 1) * HDIM)
            sc = scale[0:1, cols]
            turned = []
            for raw in (a0[:, cols], a1[:, cols]):
                t = raw * cosine + swap(raw) * sine
                turned.append(t)
            qn, kn = [
                t * lax.rsqrt(jnp.mean(t * t, axis=-1, keepdims=True) + EPS) * sc for t in turned
            ]
            q = qn.astype(BF).astype(F32) * 0.125
            if h < 3:
                v = a0[:, GROUP + h * HDIM : GROUP + (h + 1) * HDIM]
            else:
                v = a1[:, GROUP + (h - 3) * HDIM : GROUP + (h - 2) * HDIM]
            t_out[h, rows, :] = jnp.concatenate(turned, axis=1)
            q_out[h, rows, :] = jnp.concatenate([q, jnp.zeros_like(q)], axis=1).astype(BF)
            kv_out[h, rows, :] = jnp.concatenate([kn, v], axis=1).astype(BF)
        return carry

    lax.fori_loop(0, BLOCKS, per_block, 0)


def make_qkv(xg, w, scale, inner, outer):
    n = BLOCKS * ROWS
    return local_call(
        qkv_kernel,
        [((HG, n, 128), BF), ((HG, n, 128), BF), ((HG, n, 128), F32)],
        5,
        [pltpu.VMEM((n, 512), F32), pltpu.VMEM((n, 512), F32)],
        "make_qkv",
    )(xg, w, scale, inner, outer)


def kv_kernel(kv, out, sy, ry, ss, rs, lo):
    x, c, z, y = here()
    sib = dev(x, 1 - c, z, y)
    greet([sib] + [dev(x, c, z, step(y, d)) for d in (1, 2, 3)])

    def place(w, j, yy):
        return out.at[:, j // 2, owner_z(w, j % 2), yy]

    for j in range(BLOCKS):
        for d in (2, 1, 3):
            rcopy(kv.at[:, j], place(c, j, y), sy.at[d, j], ry.at[y, j], dev(x, c, z, step(y, d))).start()
        rcopy(kv.at[:, j], place(c, j, y), ss.at[0, j], rs.at[y, j], sib).start()
        lcopy(kv.at[:, j], place(c, j, y), lo.at[j]).start()
    for j in range(BLOCKS):
        for d in (1, 3, 2):
            y2 = step(y, d)
            landed(place(c, j, y2), ry.at[y2, j])
            rcopy(place(c, j, y2), place(c, j, y2), ss.at[d, j], rs.at[y2, j], sib).start()
    for j in range(BLOCKS):
        landed(kv.at[:, j], lo.at[j])
        for k in range(4):
            landed(place(1 - c, j, k), rs.at[k, j])
            landed(kv.at[:, j], ss.at[k, j])
        for d in (1, 2, 3):
            landed(kv.at[:, j], sy.at[d, j])


def kv_gather(kv):
    return remote_call(
        kv_kernel,
        [((HG, 2, 4, 4, ROWS, 128), BF, "a")],
        "a",
        [dma(4, 4), dma(4, 4), dma(4, 4), dma(4, 4), dma(4)],
        2,
        "kv_gather",
    )(kv)[0]


TILE = 512


def tiles_of(c, j):
    return (j // 2) * 4 + owner_z(c, j % 2) + 1


def causal(y):
    key = lax.broadcasted_iota(jnp.int32, (TILE, ROWS), 0)
    query = lax.broadcasted_iota(jnp.int32, (TILE, ROWS), 1)
    return key <= query + y * ROWS


def nt(a, b):
    return lax.dot_general(a, b, (((1,), (1,)), ((), ())), preferred_element_type=F32)


def tn(a, b):
    return lax.dot_general(a, b, (((0,), (0,)), ((), ())), preferred_element_type=F32)


def key_valid(length, t):
    pos = t * TILE + lax.broadcasted_iota(jnp.int32, (1, TILE), 1)
    return (pos < length).astype(F32)


def attend_kernel(length, q, kv, wo, part, att, lse, kvt, low):
    _, c, _, y = here()
    tri = causal(y)

    def per_head(h, carry):
        def flip(t, carry):
            keys = pl.ds(pl.multiple_of(t * TILE, TILE), TILE)
            valid = key_valid(length[0], t)
            turned = kv[h, keys, :].astype(F32).T * valid
            row = lax.broadcasted_iota(jnp.int32, (128, TILE), 0)
            kvt[t] = jnp.where(row < HDIM, valid, turned).astype(BF)
            return carry

        lax.fori_loop(0, 8, flip, 0)

        def per_block(j, carry):
            rows = pl.ds(pl.multiple_of(j * ROWS, ROWS), ROWS)
            qj = q[h, rows, :]
            last = tiles_of(c, j) - 1

            def scores(t):
                keys = pl.ds(pl.multiple_of(t * TILE, TILE), TILE)
                return nt(kv[h, keys, :], qj)

            def full(t, acc):
                p = jnp.exp(scores(t)).astype(BF)
                return acc + jnp.dot(kvt[t], p, preferred_element_type=F32)

            acc = lax.fori_loop(0, last, full, jnp.zeros((128, ROWS), F32))
            p = jnp.where(tri, jnp.exp(scores(last)), 0.0).astype(BF)
            acc = acc + jnp.dot(kvt[last], p, preferred_element_type=F32)
            total = acc[0:1]
            lse[h, pl.ds(j, 1), :] = jnp.log(total)
            out = (acc[HDIM:] / total).T
            att[h, rows, :] = out
            return carry

        lax.fori_loop(0, BLOCKS, per_block, 0)
        return carry

    lax.fori_loop(0, HG, per_head, 0)
    for h in range(HG):
        low[:, h * HDIM : (h + 1) * HDIM] = att[h].astype(BF)
    part[...] = jnp.dot(low[...], wo[...], preferred_element_type=F32).astype(BF)


def attend(length, q, kv, wo):
    n = BLOCKS * ROWS
    return local_call(
        attend_kernel,
        [((n, D), BF), ((HG, n, HDIM), F32), ((HG, BLOCKS, 128), F32)],
        3,
        [pltpu.VMEM((8, 128, TILE), BF), pltpu.VMEM((n, GROUP), BF)],
        "attend",
        smem=1,
    )(length, q, kv, wo)


def attend_back_kernel(length, q, kv, wo, dmix, att, lse, dq, dkv, gout, qdo, delta, kt, acc, low):
    _, c, _, y = here()
    tri = causal(y)
    d_att = nt(dmix[...], wo[...]).astype(BF)
    for h in range(HG):
        low[:, h * HDIM : (h + 1) * HDIM] = att[h].astype(BF)
        dh = d_att[:, h * HDIM : (h + 1) * HDIM].astype(F32)
        wide = jnp.concatenate([jnp.zeros_like(dh), dh], axis=1).astype(BF)
        prod = dh * att[h]
        for j in range(BLOCKS):
            rows = slice(j * ROWS, (j + 1) * ROWS)
            qdo[h, j, :ROWS] = q[h, rows, :]
            qdo[h, j, ROWS:] = wide[rows]
            delta[h, j : j + 1, :] = jnp.sum(prod[rows].T, axis=0, keepdims=True)
    gout[...] = tn(low[...], dmix[...]).astype(BF)

    def per_head(h, carry):
        def flip(t, carry):
            keys = pl.ds(pl.multiple_of(t * TILE, TILE), TILE)
            kt[t] = (kv[h, keys, :].astype(F32).T * key_valid(length[0], t)).astype(BF)
            acc[t] = jnp.zeros((TILE, 128), F32)
            return carry

        lax.fori_loop(0, 8, flip, 0)

        def per_block(j, carry):
            rows = pl.ds(pl.multiple_of(j * ROWS, ROWS), ROWS)
            both = qdo[h, j]
            l_row = lse[h, pl.ds(j, 1), :]
            d_row = delta[h, pl.ds(j, 1), :]
            last = tiles_of(c, j) - 1

            def tile(t, dqt, mask):
                keys = pl.ds(pl.multiple_of(t * TILE, TILE), TILE)
                sd = nt(kv[h, keys, :], both)
                p = jnp.exp(sd[:, :ROWS] - l_row)
                if mask:
                    p = jnp.where(tri, p, 0.0)
                ds = (p * (sd[:, ROWS:] - d_row)).astype(BF)
                pair = jnp.concatenate([ds, p.astype(BF)], axis=1)
                acc[t] += jnp.dot(pair, both, preferred_element_type=F32)
                return dqt + jnp.dot(kt[t], ds, preferred_element_type=F32)

            dqt = lax.fori_loop(0, last, lambda t, s: tile(t, s, False), jnp.zeros((128, ROWS), F32))
            dqt = tile(last, dqt, True)
            dq[h, rows, :] = dqt[:HDIM].T * 0.125
            return carry

        lax.fori_loop(0, BLOCKS, per_block, 0)

        def store(t, carry):
            keys = pl.ds(pl.multiple_of(t * TILE, TILE), TILE)
            dkv[h, keys, :] = acc[t].astype(BF)
            return carry

        lax.fori_loop(0, 8, store, 0)
        return carry

    lax.fori_loop(0, HG, per_head, 0)


def attend_back(length, q, kv, wo, dmix, att, lse):
    n = BLOCKS * ROWS
    return local_call(
        attend_back_kernel,
        [((HG, n, HDIM), F32), ((HG, 4096, 128), BF), ((GROUP, D), BF)],
        6,
        [
            pltpu.VMEM((HG, BLOCKS, 2 * ROWS, 128), BF),
            pltpu.VMEM((HG, BLOCKS, 128), F32),
            pltpu.VMEM((8, 128, TILE), BF),
            pltpu.VMEM((8, TILE, 128), F32),
            pltpu.VMEM((n, GROUP), BF),
        ],
        "attend_back",
        smem=1,
    )(length, q, kv, wo, dmix, att, lse)


def inv_rms(v):
    return lax.rsqrt(jnp.mean(v * v, axis=-1, keepdims=True) + EPS)


def back_rms(dy, yy, inv):
    return (dy - yy * jnp.mean(dy * yy, axis=-1, keepdims=True)) * inv


def total_of(buf):
    return (buf[0].astype(F32) + buf[1].astype(F32)) + (buf[2].astype(F32) + buf[3].astype(F32))


def mix_of(res, part, rate):
    inv_p = inv_rms(part)
    unit = part * inv_p
    diff = unit - res
    u = res + rate * diff
    inv_u = inv_rms(u)
    return u * inv_u, unit, inv_p, inv_u, diff


def mix_back(dy, res, part, rate):
    yy, unit, inv_p, inv_u, diff = mix_of(res, part, rate)
    du = back_rms(dy, yy, inv_u)
    return du * (1.0 - rate), back_rms(du * rate, unit, inv_p), jnp.sum(du * diff, axis=0, keepdims=True)


def meet(kernel, outs, ins_spaces, extra, cid, name):
    scratch = [
        pltpu.VMEM((4, ROWS, D), BF),
        pltpu.VMEM((ROWS, D), BF),
        dma(4),
        dma(4),
        dma(4),
        dma(4),
    ]
    return remote_call(kernel, outs, ins_spaces, scratch + extra, cid, name)


def first_kernel(part, st, rate, gathered, mixed, first, buf, low, s1, r1, s2, r2):
    x, c, z, y = here()
    greet(z_peers(x, c, z, y))
    z_scatter_start(part, buf, s1, r1, x, c, z, y)
    z_scatter_wait(part, buf, s1, r1, c, z)
    total = total_of(buf)
    mixed[...] = total
    out = mix_of(st[...].astype(F32), total, rate[0:1])[0]
    first[...] = out
    low[...] = out.astype(BF)
    z_gather_start(low, gathered, s2, r2, x, c, z, y)
    z_gather_wait(low, gathered, s2, r2, c, z)


def meet_first(part, st, rate):
    return meet(
        first_kernel,
        [((BLOCKS, ROWS, D), BF, "a"), ((ROWS, D), F32, "v"), ((ROWS, D), F32, "v")],
        "avv",
        [],
        3,
        "meet_first",
    )(part, st, rate)


def result_kernel(part, first, cot, rate, valid, gathered, result, d_first, grad, buf, low, s1, r1, s2, r2):
    x, c, z, y = here()
    greet(z_peers(x, c, z, y))
    z_scatter_start(part, buf, s1, r1, x, c, z, y)
    z_scatter_wait(part, buf, s1, r1, c, z)
    total = total_of(buf)
    live = valid[:, 0:1]
    base = first[...]
    am = rate[0:1]
    dy = cot[...].astype(F32) * live
    d_base, d_part, g = mix_back(dy, base, total, am)
    low[...] = d_part.astype(BF)
    z_gather_start(low, gathered, s2, r2, x, c, z, y)
    result[...] = (mix_of(base, total, am)[0] * live).astype(BF)
    d_first[...] = d_base
    grad[...] = jnp.broadcast_to(g, (8, D))
    z_gather_wait(low, gathered, s2, r2, c, z)


def meet_result(part, first, cot, rate, valid):
    return meet(
        result_kernel,
        [
            ((BLOCKS, ROWS, D), BF, "a"),
            ((ROWS, D), BF, "v"),
            ((ROWS, D), F32, "v"),
            ((8, D), F32, "v"),
        ],
        "avvvv",
        [],
        4,
        "meet_result",
    )(part, first, cot, rate, valid)


def back_kernel(part, d_base, st, mixed, rate, gathered, d_st, grad, buf, low, s1, r1, s2, r2):
    x, c, z, y = here()
    greet(z_peers(x, c, z, y))
    z_scatter_start(part, buf, s1, r1, x, c, z, y)
    z_scatter_wait(part, buf, s1, r1, c, z)
    dy = d_base[...] + total_of(buf)
    d_res, d_part, g = mix_back(dy, st[...].astype(F32), mixed[...], rate[0:1])
    low[...] = d_part.astype(BF)
    z_gather_start(low, gathered, s2, r2, x, c, z, y)
    d_st[...] = d_res
    grad[...] = jnp.broadcast_to(g, (8, D))
    z_gather_wait(low, gathered, s2, r2, c, z)


def meet_back(part, d_base, st, mixed, rate):
    return meet(
        back_kernel,
        [((BLOCKS, ROWS, D), BF, "a"), ((ROWS, D), F32, "v"), ((8, D), F32, "v")],
        "avvvv",
        [],
        5,
        "meet_back",
    )(part, d_base, st, mixed, rate)


def dkv_kernel(dkv, out, other, mine, got, ss, rs, sy, ry, lo):
    x, c, z, y = here()
    sib = dev(x, 1 - c, z, y)
    greet([sib] + [dev(x, c, z, step(y, d)) for d in (1, 2, 3)])
    for j in range(BLOCKS):
        oz, oc = owner_z(c, j % 2), owner_z(1 - c, j % 2)
        rcopy(dkv.at[:, j // 2, oc], other.at[:, j], ss.at[j], rs.at[j], sib).start()
        lcopy(dkv.at[:, j // 2, oz], mine.at[:, j], lo.at[j]).start()
    for j in range(BLOCKS):
        landed(mine.at[:, j], lo.at[j])
        landed(other.at[:, j], rs.at[j])
        for h in range(HG):
            mine[h, j] = (mine[h, j].astype(F32) + other[h, j].astype(F32)).astype(BF)
        for d in (2, 1, 3):
            y2 = step(y, d)
            rcopy(mine.at[:, j, y2], got.at[y, :, j], sy.at[d, j], ry.at[y, j], dev(x, c, z, y2)).start()
    for j in range(BLOCKS):
        for d in (1, 2, 3):
            landed(got.at[step(y, d), :, j], ry.at[step(y, d), j])
        for h in range(HG):
            acc = mine[h, j, y].astype(F32)
            for d in (1, 2, 3):
                acc = acc + got[step(y, d), h, j].astype(F32)
            out[h, j] = acc.astype(BF)
    for j in range(BLOCKS):
        landed(mine.at[:, j], ss.at[j])
        for d in (1, 2, 3):
            landed(mine.at[:, j, y], sy.at[d, j])


def dkv_reduce(dkv):
    return remote_call(
        dkv_kernel,
        [((HG, BLOCKS, ROWS, 128), BF, "v")],
        "a",
        [
            pltpu.VMEM((HG, BLOCKS, 4, ROWS, 128), BF),
            pltpu.VMEM((HG, BLOCKS, 4, ROWS, 128), BF),
            pltpu.VMEM((4, HG, BLOCKS, ROWS, 128), BF),
            dma(4),
            dma(4),
            dma(4, 4),
            dma(4, 4),
            dma(4),
        ],
        6,
        "dkv_reduce",
    )(dkv)[0]


def qkv_back_kernel(length, dq, dkv, t, scale, inner, outer, xg, w, part, gw, gs, d0, d1):
    _, c, _, y = here()
    gs[...] = jnp.zeros_like(gs)
    d1[:, 448:] = jnp.zeros((BLOCKS * ROWS, 64), BF)

    def per_block(j, carry):
        rows = pl.ds(pl.multiple_of(j * ROWS, ROWS), ROWS)
        b = block_index(c, y, j)
        cosine, sine = turn_of(inner, outer, b)
        live = (b * ROWS + lax.broadcasted_iota(jnp.int32, (ROWS, 1), 0) < length[0]).astype(F32)
        for h in range(HG):
            cols = slice(h * HDIM, (h + 1) * HDIM)
            sc = scale[0:1, cols]
            both = t[h, rows, :]
            kv = dkv[h, rows, :].astype(F32) * live
            for k, dy in ((0, dq[h, rows, :]), (1, kv[:, :HDIM])):
                dy = dy.astype(BF).astype(F32)
                tt = both[:, k * HDIM : (k + 1) * HDIM]
                inv = inv_rms(tt)
                unit = tt * inv
                gs[0:1, cols] += jnp.sum(dy * unit, axis=0, keepdims=True)
                dt = back_rms(dy * sc, unit, inv)
                draw = (dt * cosine + swap(dt * sine)).astype(BF)
                if k == 0:
                    d0[rows, cols] = draw
                else:
                    d1[rows, cols] = draw
            dv = kv[:, HDIM:].astype(BF)
            if h < 3:
                d0[rows, GROUP + h * HDIM : GROUP + (h + 1) * HDIM] = dv
            else:
                d1[rows, GROUP + (h - 3) * HDIM : GROUP + (h - 2) * HDIM] = dv
        return carry

    lax.fori_loop(0, BLOCKS, per_block, 0)
    part[...] = (nt(d0[...], w[0]) + nt(d1[...], w[1])).astype(BF)
    gw[0] = tn(xg[...], d0[...]).astype(BF)
    gw[1] = tn(xg[...], d1[...]).astype(BF)


def qkv_back(length, dq, dkv, t, scale, inner, outer, xg, w):
    n = BLOCKS * ROWS
    return local_call(
        qkv_back_kernel,
        [((n, D), BF), ((2, D, 512), BF), ((8, GROUP), F32)],
        8,
        [pltpu.VMEM((n, 512), BF), pltpu.VMEM((n, 512), BF)],
        "qkv_back",
        smem=1,
    )(length, dq, dkv, t, scale, inner, outer, xg, w)


def close_kernel(
    part, d_st, ga, gq, gd, go, vec,
    g_in, o_up, o_gate, o_qkv, o_down, o_out, o_vec,
    pbuf, ps, pr,
    ha, hq, hd, ra, rq, rd, fa, fq, fd, za, zq, zd, ob, oy, ox, o2, vs, vb,
    sc, rc, lo, sy, ry, sx, rx, s2, r2, sg, rg, sz, rz, sf, rf, so, ro, sv, rv,
):
    x, c, z, y = here()
    sib = dev(x, 1 - c, z, y)
    to_y = [None] + [dev(x, c, z, step(y, d)) for d in (1, 2, 3)]
    to_x = [None] + [dev(step(x, d), c, z, y) for d in (1, 2, 3)]
    greet(z_peers(x, c, z, y) + to_y[1:] + to_x[1:])
    z_scatter_start(part, pbuf, ps, pr, x, c, z, y)
    items = ((ga, ha, ra), (gq, hq, rq), (gd, hd, rd))
    for i, (g, h, _) in enumerate(items):
        rcopy(g.at[1 - c], h.at[1], sc.at[i], rc.at[i], sib).start()
        lcopy(g.at[c], h.at[0], lo.at[i]).start()
    rcopy(vec, vb.at[0], sv.at[0, 0], rv.at[0, 0], sib).start()
    rcopy(go, ob, so.at[0, 0], ro.at[0, 0], sib).start()
    lcopy(go, oy, lo.at[3]).start()

    def add_into(dst, terms, n):
        def body(k, carry):
            acc = terms[0](k).astype(F32)
            for f in terms[1:]:
                acc = acc + f(k).astype(F32)
            dst(k, acc)
            return carry

        lax.fori_loop(0, n, body, 0)

    for i, (g, h, _) in enumerate(items):
        landed(h.at[0], lo.at[i])
        landed(h.at[1], rc.at[i])

        def put(k, v, h=h):
            h[0, k // 4, k % 4] = v.astype(BF)

        add_into(put, [lambda k, h=h: h[0, k // 4, k % 4], lambda k, h=h: h[1, k // 4, k % 4]], 16)
        if i == 0:
            for d in (2, 1, 3):
                y2 = step(y, d)
                rcopy(ha.at[0, :, y2], ra.at[y], sy.at[0, d], ry.at[0, y], to_y[d]).start()
        elif i == 1:
            for d in (2, 1, 3):
                x2 = step(x, d)
                rcopy(hq.at[0, x2], rq.at[x], sx.at[0, d], rx.at[0, x], to_x[d]).start()
        else:
            for d in (2, 1, 3):
                x2 = step(x, d)
                rcopy(hd.at[0, :, x2], rd.at[x], sx.at[1, d], rx.at[1, x], to_x[d]).start()
    landed(oy, lo.at[3])
    landed(ob, ro.at[0, 0])
    vs[...] = vec[...]
    landed(vb.at[0], rv.at[0, 0])
    landed(vec, sv.at[0, 0])
    vs[...] = vs[...] + vb[0]
    for k in range(4):
        oy[k] = (oy[k].astype(F32) + ob[k].astype(F32)).astype(BF)
    for d in (2, 1, 3):
        y2 = step(y, d)
        rcopy(oy.at[y2], ox.at[y], sy.at[1, d], ry.at[1, y], to_y[d]).start()
        rcopy(vs, vb.at[d], sv.at[1, d], rv.at[1, d], to_y[d]).start()
    for d in (1, 2, 3):
        landed(ra.at[step(y, d)], ry.at[0, step(y, d)])

    def put_a(k, v):
        fa[0, k] = v.astype(BF)

    add_into(put_a, [lambda k: ha[0, k, y]] + [lambda k, d=d: ra[step(y, d), k] for d in (1, 2, 3)], 4)
    for d in (2, 1, 3):
        x2 = step(x, d)
        rcopy(fa.at[0, x2], fa.at[1, x], s2.at[0, d], r2.at[0, x], to_x[d]).start()
    for d in (1, 2, 3):
        landed(rq.at[step(x, d)], rx.at[0, step(x, d)])
        landed(rd.at[step(x, d)], rx.at[1, step(x, d)])

    def put_q(k, v):
        fq[0, k] = v.astype(BF)

    def put_d(k, v):
        fd[0, k] = v.astype(BF)

    add_into(put_q, [lambda k: hq[0, x, k]] + [lambda k, d=d: rq[step(x, d), k] for d in (1, 2, 3)], 4)
    add_into(put_d, [lambda k: hd[0, k, x]] + [lambda k, d=d: rd[step(x, d), k] for d in (1, 2, 3)], 4)
    for d in (2, 1, 3):
        y2 = step(y, d)
        rcopy(fq.at[0, y2], fq.at[1, y], s2.at[1, d], r2.at[1, y], to_y[d]).start()
        rcopy(fd.at[0, y2], fd.at[1, y], s2.at[2, d], r2.at[2, y], to_y[d]).start()
    acc = oy[y].astype(F32)
    tot = vs[...]
    for d in (1, 2, 3):
        landed(ox.at[step(y, d)], ry.at[1, step(y, d)])
        landed(vb.at[d], rv.at[1, d])
        landed(vs, sv.at[1, d])
        acc = acc + ox[step(y, d)].astype(F32)
        tot = tot + vb[d]
    ox[y] = acc.astype(BF)
    vs[...] = tot
    for d in (2, 1, 3):
        rcopy(ox.at[y], o2.at[d], so.at[1, d], ro.at[1, d], to_x[d]).start()
        rcopy(vs, vb.at[3 + d], sv.at[2, d], rv.at[2, d], to_x[d]).start()
    for d in (1, 2, 3):
        landed(fa.at[1, step(x, d)], r2.at[0, step(x, d)])
    sum_a = fa[0, x].astype(F32)
    for d in (1, 2, 3):
        sum_a = sum_a + fa[1, step(x, d)].astype(F32)
    za[0, x] = sum_a.astype(BF)
    for d in (2, 1, 3):
        rcopy(za.at[0, x], za.at[0, x], sg.at[0, d], rg.at[0, x], to_x[d]).start()
    for d in (1, 2, 3):
        landed(fq.at[1, step(y, d)], r2.at[1, step(y, d)])
        landed(fd.at[1, step(y, d)], r2.at[2, step(y, d)])
    sum_q = fq[0, y].astype(F32)
    sum_d = fd[0, y].astype(F32)
    for d in (1, 2, 3):
        sum_q = sum_q + fq[1, step(y, d)].astype(F32)
        sum_d = sum_d + fd[1, step(y, d)].astype(F32)
    zq[0, x] = sum_q.astype(BF)
    zd[c, x] = sum_d.astype(BF)
    for d in (2, 1, 3):
        rcopy(zq.at[0, x], zq.at[0, x], sg.at[1, d], rg.at[1, x], to_x[d]).start()
        rcopy(zd.at[c, x], zd.at[c, x], sg.at[2, d], rg.at[2, x], to_x[d]).start()
    acc = ox[y].astype(F32)
    tot = vs[...]
    for d in (1, 2, 3):
        landed(o2.at[d], ro.at[1, d])
        landed(vb.at[3 + d], rv.at[2, d])
        landed(vs, sv.at[2, d])
        acc = acc + o2[d].astype(F32)
        tot = tot + vb[3 + d]
    o_out[...] = acc
    vs[...] = tot
    for d in (2, 1, 3):
        rcopy(vs, vb.at[6 + d], sv.at[3, d], rv.at[3, d], dev(x, c, step(z, d), y)).start()
    for d in (1, 2, 3):
        landed(za.at[0, step(x, d)], rg.at[0, step(x, d)])
        landed(zq.at[0, step(x, d)], rg.at[1, step(x, d)])
    for d in (2, 1, 3):
        z2 = step(z, d)
        to = dev(x, c, z2, y)
        rcopy(za.at[0, z2], za.at[1 + c, z], sz.at[0, d], rz.at[0, z], to).start()
        rcopy(zq.at[0, z2], zq.at[1 + c, z], sz.at[1, d], rz.at[1, z], to).start()
    za[1 + c, z] = za[0, z]
    zq[1 + c, z] = zq[0, z]
    z_scatter_wait(part, pbuf, ps, pr, c, z)
    g_in[...] = d_st[...] + total_of(pbuf)
    for d in (1, 2, 3):
        landed(zd.at[c, step(x, d)], rg.at[2, step(x, d)])
    rcopy(zd.at[c], zd.at[c], sf.at[2], rf.at[2], sib).start()
    for d in (1, 2, 3):
        landed(za.at[1 + c, step(z, d)], rz.at[0, step(z, d)])
        landed(zq.at[1 + c, step(z, d)], rz.at[1, step(z, d)])
    rcopy(za.at[1 + c], za.at[1 + c], sf.at[0], rf.at[0], sib).start()
    rcopy(zq.at[1 + c], zq.at[1 + c], sf.at[1], rf.at[1], sib).start()
    tot = vs[...]
    for d in (1, 2, 3):
        landed(vb.at[6 + d], rv.at[3, d])
        landed(vs, sv.at[3, d])
        tot = tot + vb[6 + d]
    o_vec[0:2] = tot[0:2]
    o_vec[2:] = vs[2:]
    landed(za.at[2 - c], rf.at[0])
    landed(zq.at[2 - c], rf.at[1])
    landed(zd.at[1 - c], rf.at[2])
    for k in range(4):
        cols = slice(k * D, (k + 1) * D)
        o_up[:, cols] = za[1, k].astype(F32)
        o_gate[:, cols] = za[2, k].astype(F32)
        o_qkv[0, k] = zq[1, k].astype(F32)
        o_qkv[1, k] = zq[2, k].astype(F32)
        for half in range(2):
            o_down[k * 80 : (k + 1) * 80, half * 640 : (half + 1) * 640] = zd[half, k].astype(F32)
    for i, (g, h, r) in enumerate(items):
        landed(h.at[0], sc.at[i])
    landed(go, so.at[0, 0])
    landed(za.at[1], sf.at[0])
    landed(zq.at[1], sf.at[1])
    landed(zd.at[0], sf.at[2])
    for d in (1, 2, 3):
        landed(ra.at[0], sy.at[0, d])
        landed(ox.at[0], sy.at[1, d])
        landed(rq.at[0], sx.at[0, d])
        landed(rd.at[0], sx.at[1, d])
        landed(fa.at[0, 0], s2.at[0, d])
        landed(fq.at[0, 0], s2.at[1, d])
        landed(fd.at[0, 0], s2.at[2, d])
        landed(za.at[0, 0], sg.at[0, d])
        landed(zq.at[0, 0], sg.at[1, d])
        landed(zd.at[0, 0], sg.at[2, d])
        landed(za.at[0, 0], sz.at[0, d])
        landed(zq.at[0, 0], sz.at[1, d])
        landed(ox.at[0], so.at[1, d])


def close(part, d_st, ga, gq, gd, go, vec):
    V = pltpu.VMEM
    return remote_call(
        close_kernel,
        [
            ((ROWS, D), F32, "v"),
            ((80, FF), F32, "v"),
            ((80, FF), F32, "v"),
            ((2, 4, 80, 512), F32, "v"),
            ((320, D), F32, "v"),
            ((80, D), F32, "v"),
            ((8, D), F32, "v"),
        ],
        "avaaaav",
        [
            V((4, ROWS, D), BF), dma(4), dma(4),
            V((2, 4, 4, 80, D), BF), V((2, 4, 4, 80, 512), BF), V((2, 4, 4, 80, 640), BF),
            V((4, 4, 80, D), BF), V((4, 4, 80, 512), BF), V((4, 4, 80, 640), BF),
            V((2, 4, 80, D), BF), V((2, 4, 80, 512), BF), V((2, 4, 80, 640), BF),
            V((3, 4, 80, D), BF), V((3, 4, 80, 512), BF), V((2, 4, 80, 640), BF),
            V((4, 80, D), BF), V((4, 80, D), BF), V((4, 80, D), BF), V((4, 80, D), BF), V((8, D), F32), V((10, 8, D), F32),
            dma(3), dma(3), dma(4),
            dma(2, 4), dma(2, 4), dma(2, 4), dma(2, 4), dma(3, 4), dma(3, 4), dma(3, 4), dma(3, 4),
            dma(2, 4), dma(2, 4), dma(3), dma(3), dma(2, 4), dma(2, 4), dma(4, 4), dma(4, 4),
        ],
        7,
        "close",
    )(part, d_st, ga, gq, gd, go, vec)


def shards(
    states, w_query, w_key, w_value, w_out, w_up, w_gate, w_down,
    scale_qk, alpha_attn, alpha_mlp, scale_up, scale_gate, lengths, cotangent,
):
    x, c, z, y = here()
    st = states[0]
    position = (c * 16 + z * 4 + y) * ROWS + jnp.arange(ROWS, dtype=jnp.int32)
    valid = jnp.broadcast_to((position < lengths[0]).astype(F32)[:, None], (ROWS, 128))

    def heads(w):
        return w.reshape(80, 4, HG, HDIM)

    q4, k4, v4 = heads(w_query), heads(w_key), heads(w_value)
    half0 = jnp.concatenate([q4, v4[:, :, :3]], axis=2)
    half1 = jnp.concatenate([k4, v4[:, :, 3:], jnp.zeros_like(v4[:, :, :1])], axis=2)
    wq = jnp.stack([half0, half1]).reshape(2, 80, 4, 512).transpose(0, 2, 1, 3)
    vec = jnp.concatenate([scale_qk, alpha_attn, alpha_mlp, scale_up, scale_gate, jnp.zeros((16,), BF)])
    vec = jnp.broadcast_to(vec.astype(F32)[None], (8, 896))
    xg, wqkv, vecs, wo = open_gather(st, wq, vec, w_out)
    rows = vecs[:, :, 0].reshape(16, 896)
    mine = lax.dynamic_slice_in_dim(rows, z * 4, 4, 0)

    def wide(v):
        return jnp.broadcast_to(v.reshape(1, -1), (8, v.size))

    scale_g = wide(mine[:, :80])
    rate_a = wide(rows[:, 80:160])
    rate_m = wide(rows[:, 160:240])
    su = mine[:, 240:560].reshape(1, D)
    sg = mine[:, 560:880].reshape(1, D)

    wff, wdn = ff_gather(w_up, w_gate, w_down)
    wff = wff.reshape(2, D, D)
    wdn = wdn.reshape(D, D)
    inner, outer = (jnp.asarray(t) for t in rope_tables())
    n = BLOCKS * ROWS
    xg2 = xg.reshape(n, D)
    wqkv2 = wqkv.reshape(2, D, 512)
    q, kv, turned = make_qkv(xg2, wqkv2, scale_g, inner, outer)
    kv_all = kv_gather(kv.reshape(HG, BLOCKS, ROWS, 128)).reshape(HG, 4096, 128)
    wo2 = wo.reshape(GROUP, D)
    part, att, lse = attend(lengths, q, kv_all, wo2)
    first_g, mixed, first = meet_first(part.reshape(BLOCKS, ROWS, D), st, rate_a)

    first_g = first_g.reshape(n, D)
    up = jnp.dot(first_g, wff[0], preferred_element_type=F32)
    gate = jnp.dot(first_g, wff[1], preferred_element_type=F32)
    t = gate * sg
    sig = jax.nn.sigmoid(t)
    silu = t * sig
    hidden = (up * su * silu).astype(BF)
    part = jnp.dot(hidden, wdn, preferred_element_type=F32).astype(BF)
    dd, result, d_first, g_am = meet_result(part.reshape(BLOCKS, ROWS, D), first, cotangent[0], rate_m, valid)

    dd = dd.reshape(n, D)
    dh = lax.dot_general(dd, wdn, (((1,), (1,)), ((), ())), preferred_element_type=F32)
    dsilu = sig * (1.0 + t * (1.0 - sig))
    d_up = (dh * su * silu).astype(BF)
    d_gate = (dh * up * su * sg * dsilu).astype(BF)
    g_su = jnp.sum(dh * up * silu, axis=0)
    g_sg = jnp.sum(dh * up * su * gate * dsilu, axis=0)
    part = (
        lax.dot_general(d_up, wff[0], (((1,), (1,)), ((), ())), preferred_element_type=F32)
        + lax.dot_general(d_gate, wff[1], (((1,), (1,)), ((), ())), preferred_element_type=F32)
    ).astype(BF)
    dm, d_st, g_aa = meet_back(part.reshape(BLOCKS, ROWS, D), d_first, st, mixed, rate_a)

    def outer_sum(a, b):
        return lax.dot_general(a, b, (((0,), (0,)), ((), ())), preferred_element_type=F32).astype(BF)

    ga = jnp.stack([outer_sum(first_g, d_up), outer_sum(first_g, d_gate)]).reshape(2, 4, 4, 80, D)
    gd = jnp.stack([outer_sum(hidden, dd[:, :640]), outer_sum(hidden, dd[:, 640:])]).reshape(2, 4, 4, 80, 640)

    dq, dkv, go = attend_back(lengths, q, kv_all, wo2, dm.reshape(n, D), att, lse)
    dkv = dkv_reduce(dkv.reshape(HG, 2, 4, 4, ROWS, 128)).reshape(HG, n, 128)
    part, gq, g_sq = qkv_back(lengths, dq, dkv, turned, scale_g, inner, outer, xg2, wqkv2)
    vec = jnp.concatenate(
        [
            g_aa[0:1],
            g_am[0:1],
            g_su[None],
            g_sg[None],
            jnp.pad(g_sq[0:1], ((0, 0), (0, D - GROUP))),
            jnp.zeros((3, D), F32),
        ]
    )
    g_in, o_up, o_gate, o_qkv, o_down, o_out, o_vec = close(
        part.reshape(BLOCKS, ROWS, D),
        d_st,
        ga,
        gq.reshape(2, 4, 4, 80, 512),
        gd,
        go.reshape(4, 80, D),
        vec,
    )
    half0, half1 = (o_qkv[i].reshape(4, 80, 8, HDIM).transpose(1, 0, 2, 3) for i in (0, 1))
    gr_q = half0[:, :, :5].reshape(80, D)
    gr_k = half1[:, :, :5].reshape(80, D)
    gr_v = jnp.concatenate([half0[:, :, 5:], half1[:, :, 5:7]], axis=2).reshape(80, D)
    shard = z * 4 + y
    cut = lax.dynamic_slice_in_dim
    return (
        result[None],
        g_in[None],
        gr_q,
        gr_k,
        gr_v,
        o_out,
        o_up,
        o_gate,
        o_down,
        cut(o_vec[4], y * 80, 80, 0),
        cut(o_vec[0], shard * 80, 80, 0),
        cut(o_vec[1], shard * 80, 80, 0),
        cut(o_vec[2], y * 320, 320, 0),
        cut(o_vec[3], y * 320, 320, 0),
    )


def solution(mesh):
    row = P("grp", ("seq", "shard"), None)
    mat = P("shard", None)
    one = P("shard")
    return jax.shard_map(
        shards,
        mesh=mesh,
        in_specs=(row,) + (mat,) * 7 + (one,) * 5 + (P("grp"), row),
        out_specs=(row, row) + (mat,) * 7 + (one,) * 5,
        check_vma=False,
    )
```

time: 1350 us -> 606 us (0.45)
  waiting for transfers between devices: 531 us -> 0 us
  Pallas kernels: 0 us -> 523 us
  matrix products: 353 us -> 31.6 us
  local copies, waits for them, and re-layouts: 198 us -> 35.9 us
  blocking collectives: 152 us -> 0 us
  other arithmetic: 81.8 us -> 8.97 us
  between operations: 18.2 us -> 2.04 us
    pallas_call x0 -> x12, Pallas kernels: none -> 523 us  [the longest x1 109 us: close(): remote_call(close_kernel, [((ROWS, D), F32, 'v'), ((80, FF), F32, 'v'), (...]
    dot_general x77 -> x10, matrix products: 353 us -> 31.6 us  [the longest x1 7.22 us: shards(): lax.dot_general(dd, wdn, (((1,), (1,)), ((), ())), preferred_element_type...]
    reduce_scatter x7 -> x0, waiting for transfers between devices: 260 us -> none  [the longest x1 77.2 us: shards(): lax.psum_scatter(grad_query.astype(jnp.bfloat16), 'shard', scatter_dimens...]
    all_gather x5 -> x0, waiting for transfers between devices: 213 us -> none  [the longest x2 125 us: in_one_piece(): out, at, outs = (lax.all_gather(both, axis, axis=dim, tiled=True), 0, [])]
    unnamed x2 -> x0, blocking collectives: 92 us -> none
    psum x1 -> x0, waiting for transfers between devices: 58.1 us -> none  [packed_total(): so_far = lax.psum(jnp.concatenate([a.ravel() for a in arrays]), axis)]
    split x7 -> x0, local copies, waits for them, and re-layouts: 50.6 us -> none  [in_one_piece_2(): jnp.split(lax.all_gather(both, axis, axis=dim, tiled=True), ends, axis=al...]
    unnamed x129 -> x54, local copies, waits for them, and re-layouts: 60.5 us -> 14 us
  transfers between devices with their start and end apart: 14 -> 0, of which waited for: 9 -> 0; matrix products, arithmetic and copies ran while one was open for 38% -> 0% of each run, Pallas kernels for 0% -> 0%
where the time goes in v1:
time: 606 us; the launch traced here: 602 us
  Pallas kernels  523 us (86%)
  local copies, waits for them, and re-layouts  35.9 us (6%)
  matrix products  31.6 us (5%)
  other arithmetic  8.97 us (1%)
    pallas_call x1, Pallas kernels, close(): remote_call(close_kernel, [((ROWS, D), F32, 'v'), ((80, FF), F32, 'v'), (...  109 us
    pallas_call x1, Pallas kernels, ff_gather(): remote_call(ff_kernel, [((2, 4, 4, 80, D), BF, 'a'), ((4, 320, D), BF, 'a...  62.4 us
    pallas_call x1, Pallas kernels, attend_back(): local_call(attend_back_kernel, [((HG, n, HDIM), F32), ((HG, 4096, 128), B...  55 us
    pallas_call x1, Pallas kernels, attend(): local_call(attend_kernel, [((n, D), BF), ((HG, n, HDIM), F32), ((HG, BLOC...  45.7 us
    pallas_call x1, Pallas kernels, open_gather(): remote_call(open_kernel, [((BLOCKS, ROWS, D), BF, 'a'), ((2, 4, 4, 80, 51...  38.1 us
    pallas_call x1, Pallas kernels, meet_back(): meet(back_kernel, [((BLOCKS, ROWS, D), BF, 'a'), ((ROWS, D), F32, 'v'), (...  37.5 us
    pallas_call x1, Pallas kernels, dkv_reduce(): remote_call(dkv_kernel, [((HG, BLOCKS, ROWS, 128), BF, 'v')], 'a', [pltpu...  36.8 us
    pallas_call x1, Pallas kernels, meet_result(): meet(result_kernel, [((BLOCKS, ROWS, D), BF, 'a'), ((ROWS, D), BF, 'v'),...  36.5 us

profile of v1, /device:TPU:1, one launch (start us, length us, event | category | flops | bytes accessed | tf_op | source)
XLA Modules:
  0.0 601.5 jit_solution(16609147240429323023)
XLA Ops:
  0.7 1.2 copy.39
  1.9 1.1 copy.38
  4.1 0.9 maximum_bitcast_fusion.wq
  5.8 38.1 %open_gather.1 = (bf16[4,128,1280]{2,1,0:T(8,128)(2,1)}, bf16[2,4,4,80,512]{4,3,2,1,0:T(8,128)(2,1)}, f32[4,4,8,896]{3,2,1,0:T(8,128)}, bf16[4,80,1280]{2,1,0:T(8,128)(2,1)}) custom-call(bf16[128,1280]{1,0:T(8,128)(2,1)} %bitcast.91, bf16[2,4,80,512]{3,2,1,0:T(8,128)(2,1)} %maximum_bitcast_fusion.wq, f32[8,896]{1,0:T(8,128)} %broadcast_in_dim.52.vec, ...), custom_call_target="tpu_custom_call" | custom-call | tf_op jit(solution)/shard_map/open_gather/pallas_call | solution.py:209
  43.8 1.2 slice_reduce_fusion
  45.7 10.2 %make_qkv.1 = (bf16[5,512,128]{2,1,0:T(8,128)(2,1)}, bf16[5,512,128]{2,1,0:T(8,128)(2,1)}, f32[5,512,128]{2,1,0:T(8,128)}) custom-call(bf16[512,1280]{1,0:T(8,128)(2,1)} %bitcast.81, bf16[2,1280,512]{2,1,0:T(8,128)(2,1)} %bitcast.74, f32[8,320]{1,0:T(8,128)} %broadcast_in_dim.54.scale, f32[2,128,64]{2,1,0:T(8,128)} %constant.64.clone.inner, ...), custom_call_target="tpu_custom_call" | custom-call | tf_op jit(solution)/shard_map/make_qkv/pallas_call | solution.py:349
  55.9 35.2 %kv_gather.1 = bf16[5,2,4,4,128,128]{5,4,3,2,1,0:T(8,128)(2,1)} custom-call(bf16[5,4,128,128]{3,2,1,0:T(8,128)(2,1)} %bitcast.114), custom_call_target="tpu_custom_call" | custom-call | tf_op jit(solution)/shard_map/kv_gather/pallas_call | solution.py:386
  91.7 45.7 %attend.1 = (bf16[512,1280]{1,0:T(8,128)(2,1)}, f32[5,512,64]{2,1,0:T(8,128)}, f32[5,4,128]{2,1,0:T(4,128)}) custom-call(s32[1]{0:T(128)} %copy.58.length, bf16[5,512,128]{2,1,0:T(8,128)(2,1)} %get-tuple-element.52.q, bf16[5,4096,128]{2,1,0:T(8,128)(2,1)} %bitcast.72, bf16[320,1280]{1,0:T(8,128)(2,1)} %bitcast.89), custom_call_target="tpu_custom_call" | custom-call | tf_op jit(solution)/shard_map/attend/pallas_call | solution.py:470
  138.2 35.7 %meet_first.1 = (bf16[4,128,1280]{2,1,0:T(8,128)(2,1)}, f32[128,1280]{1,0:T(8,128)}, f32[128,1280]{1,0:T(8,128)}) custom-call(bf16[4,128,1280]{2,1,0:T(8,128)(2,1)} %bitcast.106, bf16[128,1280]{1,0:T(8,128)(2,1)} %bitcast.92, f32[8,1280]{1,0:T(8,128)} %broadcast_in_dim.56.rate), custom_call_target="tpu_custom_call" | custom-call | tf_op jit(solution)/shard_map/meet_first/pallas_call | solution.py:613
  173.9 62.4 %ff_gather.1 = (bf16[2,4,4,80,1280]{4,3,2,1,0:T(8,128)(2,1)}, bf16[4,320,1280]{2,1,0:T(8,128)(2,1)}) custom-call(bf16[80,5120]{1,0:T(8,128)(2,1)} %wu.1, bf16[80,5120]{1,0:T(8,128)(2,1)} %wg.1, bf16[320,1280]{1,0:T(8,128)(2,1)} %wd.1), custom_call_target="tpu_custom_call" | custom-call | tf_op jit(solution)/shard_map/ff_gather/pallas_call | solution.py:278
  236.3 5.3 fusion.7
  241.5 3.4 fusion.12
  245.2 6.8 %multiply_convert_fusion.2 = (bf16[512,1280]{1,0:T(8,128)(2,1)S(1)}, f32[512,1280]{1,0:T(8,128)}) fusion(f32[1280]{0:T(1024)S(1)} %mul.97, f32[512,1280]{1,0:T(8,128)} %fusion.12, f32[1280]{0:T(1024)S(1)} %mul.100, bf16[512,1280]{1,0:T(8,128)(2,1)} %bitcast.119, bf16[1280,1280]{1,0:T(8,128)(2,1)} %bitcast.85), kind=kOutput, calls=%fused_computation.14 | convolution fusion | flops 1682964480 | bytes 11151360 | tf_op jit(solution)/shard_map/dot_general | solution.py:1055
  252.0 2.9 convolution_convert_fusion.4
  254.9 0.7 broadcast_in_dim.59.valid
  256.3 36.5 %meet_result.1 = (bf16[4,128,1280]{2,1,0:T(8,128)(2,1)}, bf16[128,1280]{1,0:T(8,128)(2,1)}, f32[128,1280]{1,0:T(8,128)}, f32[8,1280]{1,0:T(8,128)}) custom-call(bf16[4,128,1280]{2,1,0:T(8,128)(2,1)} %bitcast.105, f32[128,1280]{1,0:T(8,128)} %get-tuple-element.59.first, bf16[128,1280]{1,0:T(8,128)(2,1)} %bitcast.115, f32[8,1280]{1,0:T(8,128)} %broadcast_in_dim.58.rate, ...), custom_call_target="tpu_custom_call" | custom-call | tf_op jit(solution)/shard_map/meet_result/pallas_call | solution.py:643
  292.8 7.2 %multiply_reduce_fusion = (f32[1280]{0:T(1024)S(1)}, f32[1280]{0:T(1024)S(1)}, bf16[512,1280]{1,0:T(8,128)(2,1)S(1)}, bf16[512,1280]{1,0:T(8,128)(2,1)S(1)}) fusion(f32[512,1280]{1,0:T(8,128)} %fusion.12, f32[1280]{0:T(1024)S(1)} %mul.97, f32[1280]{0:T(1024)S(1)} %mul.100, f32[512,1280]{1,0:T(8,128)} %get-tuple-element.116, bf16[512,1280]{1,0:T(8,128)(2,1)} %bitcast.123, ...), kind=kOutput, calls=%fused_computation.9 | convolution fusion | flops 1692136960 | bytes 12472320 | tf_op jit(solution)/shard_map/dot_general | solution.py:1065
  300.1 1.9 fusion.13
  302.0 3.1 fusion
  305.1 37.5 %meet_back.1 = (bf16[4,128,1280]{2,1,0:T(8,128)(2,1)}, f32[128,1280]{1,0:T(8,128)}, f32[8,1280]{1,0:T(8,128)}) custom-call(bf16[4,128,1280]{2,1,0:T(8,128)(2,1)} %bitcast.107, f32[128,1280]{1,0:T(8,128)} %get-tuple-element.62.d_base, bf16[128,1280]{1,0:T(8,128)(2,1)} %bitcast.93, f32[128,1280]{1,0:T(8,128)} %get-tuple-element.63.mixed, ...), custom_call_target="tpu_custom_call" | custom-call | tf_op jit(solution)/shard_map/meet_back/pallas_call | solution.py:673
  342.7 55.0 %attend_back.1 = (f32[5,512,64]{2,1,0:T(8,128)}, bf16[5,4096,128]{2,1,0:T(8,128)(2,1)}, bf16[320,1280]{1,0:T(8,128)(2,1)}) custom-call(s32[1]{0:T(128)} %copy.58.length, bf16[5,512,128]{2,1,0:T(8,128)(2,1)} %get-tuple-element.52.q, bf16[5,4096,128]{2,1,0:T(8,128)(2,1)} %bitcast.73, bf16[320,1280]{1,0:T(8,128)(2,1)} %bitcast.90, bf16[512,1280]{1,0:T(8,128)(2,1)} %bitcast.104, ...), custom_call_target="tpu_custom_call" | custom-call | tf_op jit(solution)/shard_map/attend_back/pallas_call | solution.py:543
  397.7 36.8 %dkv_reduce.1 = bf16[5,4,128,128]{3,2,1,0:T(8,128)(2,1)} custom-call(bf16[5,2,4,4,128,128]{5,4,3,2,1,0:T(8,128)(2,1)} %bitcast.80), custom_call_target="tpu_custom_call" | custom-call | tf_op jit(solution)/shard_map/dkv_reduce/pallas_call | solution.py:714
  434.5 20.6 %qkv_back.1 = (bf16[512,1280]{1,0:T(8,128)(2,1)}, bf16[2,1280,512]{2,1,0:T(8,128)(2,1)}, f32[8,320]{1,0:T(8,128)}) custom-call(s32[1]{0:T(128)} %copy.58.length, f32[5,512,64]{2,1,0:T(8,128)} %get-tuple-element.67.dq, bf16[5,512,128]{2,1,0:T(8,128)(2,1)} %bitcast.98, f32[5,512,128]{2,1,0:T(8,128)} %get-tuple-element.69.t, f32[8,320]{1,0:T(8,128)} %broadcast_in_dim.54.scale, ...), custom_call_target="tpu_custom_call" | custom-call | tf_op jit(solution)/shard_map/qkv_back/pallas_call | solution.py:775
  455.2 0.7 slice.96
  455.9 0.8 slice.94
  456.7 0.8 slice.95
  458.2 1.2 convolution_convert_fusion.3
  459.4 1.2 convolution_convert_fusion.2
  460.6 2.1 pad_maximum_fusion.1.gd
  463.3 1.9 convolution_convert_fusion.1
  465.3 1.9 convolution_convert_fusion
  467.2 3.3 pad_maximum_fusion.ga
  470.5 109.3 %close.1 = (f32[128,1280]{1,0:T(8,128)}, f32[80,5120]{1,0:T(8,128)}, f32[80,5120]{1,0:T(8,128)}, f32[2,4,80,512]{3,2,1,0:T(8,128)}, f32[320,1280]{1,0:T(8,128)}, /*index=5*/f32[80,1280]{1,0:T(8,128)}, f32[8,1280]{1,0:T(8,128)}) custom-call(bf16[4,128,1280]{2,1,0:T(8,128)(2,1)} %bitcast.103, f32[128,1280]{1,0:T(8,128)} %get-tuple-element.71.d_st, ...), custom_call_target="tpu_custom_call" | custom-call | tf_op jit(solution)/shard_map/close/pallas_call | solution.py:982
  579.8 1.0 fusion.11
  580.9 0.7 dynamic-slice_reduce_fusion
  582.1 1.4 fusion.8
  583.8 1.0 slice.116
  585.2 2.5 pad_maximum_fusion.2
  587.7 1.6 copy.45
  589.3 1.0 copy.48
  590.6 1.0 copy.46
  591.9 1.0 copy.47
  593.4 1.7 copy.59
  595.1 0.8 copy.60
  596.0 1.8 copy.61
  597.8 1.2 copy.62
  598.9 1.2 copy.63
  600.1 1.2 copy.64
  (78 shorter events, 7.9 us)
Async XLA Ops:
  0.6 2.8 copy-start.5
  3.2 1.8 copy-start.6
  3.2 1.8 copy-start.7
  3.2 1.8 copy-start.8
  3.2 1.8 copy-start.9
  3.2 1.8 copy-start.10
  236.3 5.3 copy-start.12
  245.2 6.8 %copy-start.11 = (bf16[4,320,1280]{2,1,0:T(8,128)(2,1)S(1)}, bf16[4,320,1280]{2,1,0:T(8,128)(2,1)}, u32[]{:S(2)}) copy-start(bf16[4,320,1280]{2,1,0:T(8,128)(2,1)} %get-tuple-element.58) | copy-start | bytes 9830404
  252.0 2.9 copy-start.15
  292.8 7.3 %copy-start = (bf16[1,4,4,80,1280]{4,3,2,1,0:T(8,128)(2,1)S(1)}, bf16[1,4,4,80,1280]{4,3,2,1,0:T(8,128)(2,1)}, u32[]{:S(2)}) copy-start(bf16[1,4,4,80,1280]{4,3,2,1,0:T(8,128)(2,1)} %get-tuple-element.102) | copy-start | bytes 9830404
  300.0 1.9 copy-start.17
  300.1 1.9 copy-start.19
  434.5 23.6 %copy-start.14 = (bf16[4,128,1280]{2,1,0:T(8,128)(2,1)S(1)}, bf16[4,128,1280]{2,1,0:T(8,128)(2,1)}, u32[]{:S(2)}) copy-start(bf16[4,128,1280]{2,1,0:T(8,128)(2,1)} %get-tuple-element.61) | copy-start | bytes 3932164
  434.5 23.6 %copy-start.16 = (bf16[512,1280]{1,0:T(8,128)(2,1)S(1)}, bf16[512,1280]{1,0:T(8,128)(2,1)}, u32[]{:S(2)}) copy-start(bf16[512,1280]{1,0:T(8,128)(2,1)} %copy-done.15) | copy-start | bytes 3932164
  460.6 2.1 copy-start.13
  460.6 2.7 copy-start.18
  463.3 1.9 copy-start.20
  591.5 3.6 copy-start.4
  591.8 5.9 copy-start.3
  595.1 3.8 copy-start.2
  597.8 2.3 copy-start.1

commit v2 on v1

v2 whole, which is shorter than its diff:
```python
import functools
import math

import jax
import jax.numpy as jnp
import numpy as np
from jax import lax
from jax.experimental import pallas as pl
from jax.experimental.pallas import tpu as pltpu
from jax.sharding import PartitionSpec as P


D, HEADS, HDIM, FF = 1280, 20, 64, 5120
ROWS, BLOCKS, HG = 128, 4, 5
GROUP = HG * HDIM
EPS = 1e-6
BF, F32 = jnp.bfloat16, jnp.float32
MESH = pl.DeviceIdType.MESH
VMEM_LIMIT = 60 << 20


def here():
    s = lax.axis_index("shard")
    return lax.axis_index("grp"), lax.axis_index("seq"), s // 4, s % 4


def dev(x, c, z, y):
    return (x, c, z * 4 + y)


def worker(z):
    return ((z + 1) // 2) % 2


def owner_z(w, i):
    return i * (3 - 2 * w) + w


def step(v, d):
    return (v + d) % 4


def rcopy(src, dst, ss, rs, to):
    return pltpu.make_async_remote_copy(
        src_ref=src, dst_ref=dst, send_sem=ss, recv_sem=rs, device_id=to, device_id_type=MESH
    )


def lcopy(src, dst, sem):
    return pltpu.make_async_copy(src, dst, sem)


def landed(dst, sem):
    pltpu.make_async_copy(dst, dst, sem).wait()


def greet(peers):
    bar = pltpu.get_barrier_semaphore()
    for p in peers:
        pl.semaphore_signal(bar, inc=1, device_id=p, device_id_type=MESH)
    pl.semaphore_wait(bar, len(peers))


def z_peers(x, c, z, y):
    far = [dev(x, cc, step(z, d), y) for d in (1, 2, 3) for cc in (0, 1)]
    return [dev(x, 1 - c, z, y)] + far


def z_gather_start(src, dst, ss, rs, x, c, z, y):
    w = worker(z)
    slot = (z // 2, c)
    for d in (1, 3, 2):
        rcopy(src, dst.at[slot], ss.at[d], rs.at[slot], dev(x, w, step(z, d), y)).start()

    @pl.when(c == w)
    def _():
        lcopy(src, dst.at[slot], rs.at[slot]).start()

    @pl.when(c != w)
    def _():
        rcopy(src, dst.at[slot], ss.at[0], rs.at[slot], dev(x, w, z, y)).start()


def z_gather_take(dst, rs, p):
    for k in range(2):
        landed(dst.at[p, k], rs.at[p, k])


def z_gather_sent(src, ss, c, z):
    for d in (1, 2, 3):
        landed(src, ss.at[d])

    @pl.when(c != worker(z))
    def _():
        landed(src, ss.at[0])


def z_gather_wait(src, dst, ss, rs, c, z):
    for p in range(2):
        z_gather_take(dst, rs, p)
    z_gather_sent(src, ss, c, z)


def z_scatter_pair(part, dst, ss, rs, p, x, c, z, y):
    oz = owner_z(c, p)
    for oc in range(2):
        mine = jnp.logical_and(c == oc, z == oz)

        @pl.when(mine)
        def _(oc=oc):
            lcopy(part.at[p, oc], dst.at[z], rs.at[z]).start()

        @pl.when(jnp.logical_not(mine))
        def _(oc=oc):
            rcopy(part.at[p, oc], dst.at[z], ss.at[p, oc], rs.at[z], dev(x, oc, oz, y)).start()


def z_scatter_start(part, dst, ss, rs, x, c, z, y):
    for p in range(2):
        z_scatter_pair(part, dst, ss, rs, p, x, c, z, y)


def z_scatter_take(dst, rs):
    for k in range(4):
        landed(dst.at[k], rs.at[k])


def z_scatter_sent(part, ss, c, z):
    for p in range(2):
        for oc in range(2):
            mine = jnp.logical_and(c == oc, z == owner_z(c, p))

            @pl.when(jnp.logical_not(mine))
            def _(p=p, oc=oc):
                landed(part.at[p, oc], ss.at[p, oc])


def remote_call(kernel, outs, ins_spaces, scratch, cid, name):
    spec = {
        "a": pl.BlockSpec(memory_space=pl.ANY),
        "v": pl.BlockSpec(memory_space=pltpu.VMEM),
        "s": pl.BlockSpec(memory_space=pltpu.SMEM),
    }
    return pl.pallas_call(
        kernel,
        out_shape=[jax.ShapeDtypeStruct(s, d) for s, d, _ in outs],
        in_specs=[spec[s] for s in ins_spaces],
        out_specs=[spec[s] for _, _, s in outs],
        scratch_shapes=scratch,
        compiler_params=pltpu.CompilerParams(
            collective_id=cid, has_side_effects=True, vmem_limit_bytes=VMEM_LIMIT
        ),
        name=name,
    )


def local_call(kernel, outs, n_in, scratch, name, smem=0):
    vmem = pl.BlockSpec(memory_space=pltpu.VMEM)
    sm = pl.BlockSpec(memory_space=pltpu.SMEM)
    return pl.pallas_call(
        kernel,
        out_shape=[jax.ShapeDtypeStruct(s, d) for s, d in outs],
        in_specs=[sm] * smem + [vmem] * n_in,
        out_specs=[vmem for _ in outs],
        scratch_shapes=scratch,
        compiler_params=pltpu.CompilerParams(vmem_limit_bytes=VMEM_LIMIT),
        name=name,
    )


def dma(*shape):
    return pltpu.SemaphoreType.DMA(shape)


def open_kernel(st, wq, vec, wo, xg, wqkv, vecs, wog, xs, xr, s1, r1, s2, r2, s3, r3, sv, rv, so, ro, lo):
    x, c, z, y = here()
    sib = dev(x, 1 - c, z, y)
    half = pl.ds(pl.multiple_of(c * 640, 128), 640)
    other = pl.ds(pl.multiple_of((1 - c) * 640, 128), 640)
    greet(z_peers(x, c, z, y) + [dev(x, c, z, step(y, d)) for d in (1, 2, 3)])
    for d in (2, 1, 3):
        z2 = step(z, d)
        rcopy(wq.at[c, z2], wqkv.at[c, z, y], s1.at[d], r1.at[z], dev(x, c, z2, y)).start()
        rcopy(vec, vecs.at[z, y], sv.at[0, d], rv.at[0, z], dev(x, c, z2, y)).start()
    own = lcopy(wq.at[c, z], wqkv.at[c, z, y], lo.at[0])
    own.start()
    own_v = lcopy(vec, vecs.at[z, y], lo.at[1])
    own_v.start()
    own_o = lcopy(wo.at[:, half], wog.at[y, :, half], lo.at[2])
    own_o.start()
    for d in (2, 1, 3):
        rcopy(wo.at[:, half], wog.at[y, :, half], so.at[0, d], ro.at[0, y], dev(x, c, z, step(y, d))).start()
    rcopy(wo.at[:, half], wog.at[y, :, half], so.at[0, 0], ro.at[1, y], sib).start()
    z_gather_start(st, xg, xs, xr, x, c, z, y)
    for d in (1, 2, 3):
        z2 = step(z, d)
        landed(wqkv.at[c, z2, y], r1.at[z2])
        landed(vecs.at[z2, y], rv.at[0, z2])
    own.wait()
    own_v.wait()
    for d in (2, 1, 3):
        to = dev(x, c, z, step(y, d))
        rcopy(wqkv.at[c, :, y], wqkv.at[c, :, y], s2.at[d], r2.at[y], to).start()
        rcopy(vecs.at[:, y], vecs.at[:, y], sv.at[1, d], rv.at[1, y], to).start()
    rcopy(wqkv.at[c, :, y], wqkv.at[c, :, y], s3.at[0], r3.at[y], sib).start()
    for d in (1, 3, 2):
        y2 = step(y, d)
        landed(wog.at[y2, :, half], ro.at[0, y2])
        rcopy(wog.at[y2, :, half], wog.at[y2, :, half], so.at[1, d], ro.at[1, y2], sib).start()
        landed(wqkv.at[c, :, y2], r2.at[y2])
        rcopy(wqkv.at[c, :, y2], wqkv.at[c, :, y2], s3.at[d], r3.at[y2], sib).start()
    z_gather_wait(st, xg, xs, xr, c, z)
    own_o.wait()
    for k in range(4):
        landed(wqkv.at[1 - c, :, k], r3.at[k])
        landed(wog.at[k, :, other], ro.at[1, k])
        landed(wqkv.at[c, :, k], s3.at[k])
    landed(wo.at[:, half], so.at[0, 0])
    for d in (1, 2, 3):
        landed(vecs.at[:, step(y, d)], rv.at[1, step(y, d)])
        landed(wq.at[c, z], s1.at[d])
        landed(vec, sv.at[0, d])
        landed(vecs.at[:, y], sv.at[1, d])
        landed(wqkv.at[c, :, y], s2.at[d])
        landed(wo.at[:, half], so.at[0, d])
        landed(wog.at[y, :, half], so.at[1, d])


def open_gather(st, wq, vec, wo):
    return remote_call(
        open_kernel,
        [
            ((2, 2, ROWS, D), BF, "a"),
            ((2, 4, 4, 80, 512), BF, "a"),
            ((4, 4, 8, 896), F32, "a"),
            ((4, 80, D), BF, "a"),
        ],
        "aaaa",
        [dma(4), dma(2, 2), dma(4), dma(4), dma(4), dma(4), dma(4), dma(4), dma(2, 4), dma(2, 4), dma(2, 4), dma(2, 4), dma(3)],
        0,
        "open_gather",
    )(st, wq, vec, wo)


def rope_tables():
    freqs = np.exp(np.arange(32) * (-2.0 * math.log(10000.0) / 64))
    freqs = np.concatenate([freqs, freqs])
    sign = np.concatenate([-np.ones(32), np.ones(32)])
    inner = np.arange(ROWS)[:, None] * freqs
    outer = (np.arange(32) * ROWS)[:, None] * freqs
    return (
        np.stack([np.cos(inner), np.sin(inner) * sign]).astype(np.float32),
        np.stack([np.cos(outer), np.sin(outer) * sign]).astype(np.float32),
    )


def block_index(c, y, j):
    return (j % 2) * 16 + owner_z(c, j // 2) * 4 + y


def turn_of(inner, outer, b):
    oc = outer[0, pl.ds(b, 1), :]
    os = outer[1, pl.ds(b, 1), :]
    return oc * inner[0] - os * inner[1], os * inner[0] + oc * inner[1]


def swap(v):
    return jnp.concatenate([v[:, 32:], v[:, :32]], axis=1)


def qkv_kernel(xg, w, scale, inner, outer, q_out, kv_out, t_out, y0, y1):
    _, c, _, y = here()
    xs = xg[...]
    y0[...] = jnp.dot(xs, w[0], preferred_element_type=F32)
    y1[...] = jnp.dot(xs, w[1], preferred_element_type=F32)

    def per_block(j, carry):
        rows = pl.ds(pl.multiple_of(j * ROWS, ROWS), ROWS)
        cosine, sine = turn_of(inner, outer, block_index(c, y, j))
        a0, a1 = y0[rows, :], y1[rows, :]
        for h in range(HG):
            cols = slice(h * HDIM, (h + 1) * HDIM)
            sc = scale[0:1, cols]
            turned = []
            for raw in (a0[:, cols], a1[:, cols]):
                t = raw * cosine + swap(raw) * sine
                turned.append(t)
            qn, kn = [
                t * lax.rsqrt(jnp.mean(t * t, axis=-1, keepdims=True) + EPS) * sc for t in turned
            ]
            q = qn.astype(BF).astype(F32) * 0.125
            if h < 3:
                v = a0[:, GROUP + h * HDIM : GROUP + (h + 1) * HDIM]
            else:
                v = a1[:, GROUP + (h - 3) * HDIM : GROUP + (h - 2) * HDIM]
            t_out[h, rows, :] = jnp.concatenate(turned, axis=1)
            q_out[h, rows, :] = jnp.concatenate([q, jnp.zeros_like(q)], axis=1).astype(BF)
            kv_out[h, rows, :] = jnp.concatenate([kn, v], axis=1).astype(BF)
        return carry

    lax.fori_loop(0, BLOCKS, per_block, 0)


def make_qkv(xg, w, scale, inner, outer):
    n = BLOCKS * ROWS
    return local_call(
        qkv_kernel,
        [((HG, n, 128), BF), ((HG, n, 128), BF), ((HG, n, 128), F32)],
        5,
        [pltpu.VMEM((n, 512), F32), pltpu.VMEM((n, 512), F32)],
        "make_qkv",
    )(xg, w, scale, inner, outer)


TILE = 512


def tiles_of(c, j):
    return (j % 2) * 4 + owner_z(c, j // 2) + 1


def causal(y):
    key = lax.broadcasted_iota(jnp.int32, (TILE, ROWS), 0)
    query = lax.broadcasted_iota(jnp.int32, (TILE, ROWS), 1)
    return key <= query + y * ROWS


def nt(a, b):
    return lax.dot_general(a, b, (((1,), (1,)), ((), ())), preferred_element_type=F32)


def tn(a, b):
    return lax.dot_general(a, b, (((0,), (0,)), ((), ())), preferred_element_type=F32)


def key_valid(length, t):
    pos = t * TILE + lax.broadcasted_iota(jnp.int32, (1, TILE), 1)
    return (pos < length).astype(F32)


def key_tile(ref, h, t):
    zz = t % 4
    return ref[h, worker(zz), zz // 2, t // 4].reshape(TILE, 128)


def columns(ref, k, half):
    return ref.at[:, pl.ds(pl.multiple_of(k * D + half * 640, 128), 640)]


def attend_kernel(
    length, q, kv, wo, w_up, w_gate,
    part, att, lse, kvb, wu, gz,
    kvt, low, sy, ry, ss, rs, lo, s1, r1, s2, r2, s3, r3, lw,
):
    x, c, z, y = here()
    sib = dev(x, 1 - c, z, y)
    half = pl.ds(pl.multiple_of(c * 640, 128), 640)
    other = pl.ds(pl.multiple_of((1 - c) * 640, 128), 640)
    greet(
        [sib]
        + [dev(x, c, step(z, d), y) for d in (1, 2, 3)]
        + [dev(x, c, z, step(y, d)) for d in (1, 2, 3)]
    )

    def send(h, carry):
        for d in (1, 3, 2):
            rcopy(kv.at[h], kvb.at[h, c, :, :, y], sy.at[h, d], ry.at[h, y], dev(x, c, z, step(y, d))).start()
        rcopy(kv.at[h], kvb.at[h, c, :, :, y], ss.at[h, 0], rs.at[h, y], sib).start()
        lcopy(kv.at[h], kvb.at[h, c, :, :, y], lo.at[h]).start()
        return carry

    lax.fori_loop(0, HG, send, 0)
    for d in (1, 3, 2):
        z2 = step(z, d)
        to = dev(x, c, z2, y)
        rcopy(columns(w_up, z2, c), wu.at[z, y, :, half], s1.at[0, d], r1.at[0, z], to).start()
        rcopy(columns(w_gate, z2, c), gz.at[z], s1.at[1, d], r1.at[1, z], to).start()
    lcopy(columns(w_up, z, c), wu.at[z, y, :, half], lw.at[0]).start()
    lcopy(columns(w_gate, z, c), gz.at[z], lw.at[1]).start()

    def forward(h):
        for d in (1, 3, 2):
            y2 = step(y, d)
            landed(kvb.at[h, c, :, :, y2], ry.at[h, y2])
            rcopy(kvb.at[h, c, :, :, y2], kvb.at[h, c, :, :, y2], ss.at[h, d], rs.at[h, y2], sib).start()

    def spread_up():
        for d in (1, 2, 3):
            landed(wu.at[step(z, d), y, :, half], r1.at[0, step(z, d)])
            landed(gz.at[step(z, d)], r1.at[1, step(z, d)])
        landed(wu.at[z, y, :, half], lw.at[0])
        landed(gz.at[z], lw.at[1])
        for d in (1, 3, 2):
            rcopy(wu.at[:, y, :, half], wu.at[:, y, :, half], s2.at[d], r2.at[y], dev(x, c, z, step(y, d))).start()
        rcopy(wu.at[:, y, :, half], wu.at[:, y, :, half], s3.at[0], r3.at[y], sib).start()

    tri = causal(y)
    forward(0)

    def per_head(h, carry):
        landed(kvb.at[h, c, :, :, y], lo.at[h])
        for k in range(4):
            landed(kvb.at[h, 1 - c, :, :, k], rs.at[h, k])

        def flip(t, carry):
            valid = key_valid(length[0], t)
            turned = key_tile(kvb, h, t).astype(F32).T * valid
            row = lax.broadcasted_iota(jnp.int32, (128, TILE), 0)
            kvt[t] = jnp.where(row < HDIM, valid, turned).astype(BF)
            return carry

        lax.fori_loop(0, 8, flip, 0)

        def per_block(j, carry):
            @pl.when(jnp.logical_and(j == 2, h < HG - 1))
            def _():
                forward(h + 1)

            @pl.when(jnp.logical_and(j == 2, h == 2))
            def _():
                spread_up()

            rows = pl.ds(pl.multiple_of(j * ROWS, ROWS), ROWS)
            qj = q[h, rows, :]
            last = tiles_of(c, j) - 1

            def full(t, acc):
                p = jnp.exp(nt(key_tile(kvb, h, t), qj)).astype(BF)
                return acc + jnp.dot(kvt[t], p, preferred_element_type=F32)

            acc = lax.fori_loop(0, last, full, jnp.zeros((128, ROWS), F32))
            p = jnp.where(tri, jnp.exp(nt(key_tile(kvb, h, last), qj)), 0.0).astype(BF)
            acc = acc + jnp.dot(kvt[last], p, preferred_element_type=F32)
            total = acc[0:1]
            lse[h, pl.ds(j, 1), :] = jnp.log(total)
            att[h, rows, :] = (acc[HDIM:] / total).T
            return carry

        lax.fori_loop(0, BLOCKS, per_block, 0)
        return carry

    lax.fori_loop(0, HG, per_head, 0)
    for h in range(HG):
        low[:, h * HDIM : (h + 1) * HDIM] = att[h].astype(BF)
    part[...] = jnp.dot(low[...], wo[...], preferred_element_type=F32).astype(BF)
    for d in (1, 3, 2):
        y2 = step(y, d)
        landed(wu.at[:, y2, :, half], r2.at[y2])
        rcopy(wu.at[:, y2, :, half], wu.at[:, y2, :, half], s3.at[d], r3.at[y2], sib).start()

    def sent(h, carry):
        for k in range(4):
            landed(kv.at[h], ss.at[h, k])
        for d in (1, 2, 3):
            landed(kv.at[h], sy.at[h, d])
        return carry

    lax.fori_loop(0, HG, sent, 0)
    for k in range(4):
        landed(wu.at[:, k, :, other], r3.at[k])
        landed(wu.at[:, k, :, half], s3.at[k])
    for d in (1, 2, 3):
        landed(gz.at[z], s1.at[0, d])
        landed(gz.at[z], s1.at[1, d])
        landed(wu.at[:, y, :, half], s2.at[d])


def attend(length, q, kv, wo, w_up, w_gate):
    n = BLOCKS * ROWS
    return remote_call(
        attend_kernel,
        [
            ((n, D), BF, "v"),
            ((HG, n, HDIM), F32, "v"),
            ((HG, BLOCKS, 128), F32, "v"),
            ((HG, 2, 2, 2, 4, ROWS, 128), BF, "v"),
            ((4, 4, 80, D), BF, "a"),
            ((4, 80, 640), BF, "a"),
        ],
        "svvvaa",
        [
            pltpu.VMEM((8, 128, TILE), BF), pltpu.VMEM((n, GROUP), BF),
            dma(HG, 4), dma(HG, 4), dma(HG, 4), dma(HG, 4), dma(HG),
            dma(2, 4), dma(2, 4), dma(4), dma(4), dma(4), dma(4), dma(2),
        ],
        1,
        "attend",
    )(length, q, kv, wo, w_up, w_gate)


def attend_back_kernel(
    length, q, kv, wo, dmix, att, lse, ha, hd,
    dq, dkv, gout, za, zd,
    qdo, delta, kt, acc, low, give, mine, got, got_y, oa, od, ra, rd, fa, fd,
    sg, rg, sy, ry, s1, r1, s2, r2, s3, r3, lo,
):
    x, c, z, y = here()
    sib = dev(x, 1 - c, z, y)
    to_y = [None] + [dev(x, c, z, step(y, d)) for d in (1, 2, 3)]
    to_x = [None] + [dev(step(x, d), c, z, y) for d in (1, 2, 3)]
    greet([sib] + to_y[1:] + to_x[1:])
    for d in (1, 3, 2):
        rcopy(ha.at[step(x, d)], ra.at[x], s1.at[0, d], r1.at[0, x], to_x[d]).start()
        rcopy(hd.at[step(y, d)], rd.at[y], s1.at[1, d], r1.at[1, y], to_y[d]).start()
    lcopy(ha.at[x], oa, lo.at[0]).start()
    lcopy(hd.at[y], od, lo.at[1]).start()

    def first_sums():
        landed(oa, lo.at[0])
        landed(od, lo.at[1])
        for d in (1, 2, 3):
            landed(ra.at[step(x, d)], r1.at[0, step(x, d)])
            landed(rd.at[step(y, d)], r1.at[1, step(y, d)])

        def body(k, carry):
            va = oa[k].astype(F32)
            vd = od[k].astype(F32)
            for d in (1, 2, 3):
                va = va + ra[step(x, d), k].astype(F32)
                vd = vd + rd[step(y, d), k].astype(F32)
            oa[k] = va.astype(BF)
            od[k] = vd.astype(BF)
            return carry

        lax.fori_loop(0, 4, body, 0)
        for d in (1, 3, 2):
            rcopy(oa.at[step(y, d)], fa.at[y], s2.at[0, d], r2.at[0, y], to_y[d]).start()
            rcopy(od.at[step(x, d)], fd.at[x], s2.at[1, d], r2.at[1, x], to_x[d]).start()

    def second_sums():
        for d in (1, 2, 3):
            landed(fa.at[step(y, d)], r2.at[0, step(y, d)])
            landed(fd.at[step(x, d)], r2.at[1, step(x, d)])
        va = oa[y].astype(F32)
        vd = od[x].astype(F32)
        for d in (1, 2, 3):
            va = va + fa[step(y, d)].astype(F32)
            vd = vd + fd[step(x, d)].astype(F32)
        fa[y] = va.astype(BF)
        fd[x] = vd.astype(BF)
        for d in (1, 3, 2):
            rcopy(fa.at[y], za.at[x], s3.at[0, d], r3.at[0, x], to_x[d]).start()
            rcopy(fd.at[x], zd.at[x], s3.at[1, d], r3.at[1, x], to_x[d]).start()
        lcopy(fa.at[y], za.at[x], lo.at[2]).start()
        lcopy(fd.at[x], zd.at[x], lo.at[3]).start()

    def settle(h):
        landed(got.at[h], rg.at[h])
        for i in range(2):
            for k in range(2):
                mine[h, i, k] = (mine[h, i, k].astype(F32) + got[h, i, k].astype(F32)).astype(BF)
        for d in (1, 3, 2):
            rcopy(mine.at[h, :, :, step(y, d)], got_y.at[h, y], sy.at[h, d], ry.at[h, y], to_y[d]).start()

    tri = causal(y)
    d_att = nt(dmix[...], wo[...]).astype(BF)
    for h in range(HG):
        low[:, h * HDIM : (h + 1) * HDIM] = att[h].astype(BF)
        dh = d_att[:, h * HDIM : (h + 1) * HDIM].astype(F32)
        wide = jnp.concatenate([jnp.zeros_like(dh), dh], axis=1).astype(BF)
        prod = dh * att[h]
        for j in range(BLOCKS):
            rows = slice(j * ROWS, (j + 1) * ROWS)
            qdo[h, j, :ROWS] = q[h, rows, :]
            qdo[h, j, ROWS:] = wide[rows]
            delta[h, j : j + 1, :] = jnp.sum(prod[rows].T, axis=0, keepdims=True)
    gout[...] = tn(low[...], dmix[...]).astype(BF)

    def per_head(h, carry):
        def flip(t, carry):
            kt[t] = (key_tile(kv, h, t).astype(F32).T * key_valid(length[0], t)).astype(BF)
            acc[t] = jnp.zeros((TILE, 128), F32)
            return carry

        lax.fori_loop(0, 8, flip, 0)

        def per_block(j, carry):
            @pl.when(jnp.logical_and(j == 2, h > 0))
            def _():
                settle(h - 1)

            @pl.when(jnp.logical_and(j == 0, h == 3))
            def _():
                first_sums()

            @pl.when(jnp.logical_and(j == 0, h == 4))
            def _():
                second_sums()

            rows = pl.ds(pl.multiple_of(j * ROWS, ROWS), ROWS)
            both = qdo[h, j]
            l_row = lse[h, pl.ds(j, 1), :]
            d_row = delta[h, pl.ds(j, 1), :]
            last = tiles_of(c, j) - 1

            def tile(t, dqt, mask):
                sd = nt(key_tile(kv, h, t), both)
                p = jnp.exp(sd[:, :ROWS] - l_row)
                if mask:
                    p = jnp.where(tri, p, 0.0)
                ds = (p * (sd[:, ROWS:] - d_row)).astype(BF)
                pair = jnp.concatenate([ds, p.astype(BF)], axis=1)
                acc[t] += jnp.dot(pair, both, preferred_element_type=F32)
                return dqt + jnp.dot(kt[t], ds, preferred_element_type=F32)

            dqt = lax.fori_loop(0, last, lambda t, s: tile(t, s, False), jnp.zeros((128, ROWS), F32))
            dqt = tile(last, dqt, True)
            dq[h, rows, :] = dqt[:HDIM].T * 0.125
            return carry

        lax.fori_loop(0, BLOCKS, per_block, 0)

        def store(i, carry):
            zi, k = i // 2, i % 2
            give[h, zi, k] = acc[k * 4 + owner_z(1 - c, zi)].astype(BF).reshape(4, ROWS, 128)
            mine[h, zi, k] = acc[k * 4 + owner_z(c, zi)].astype(BF).reshape(4, ROWS, 128)
            return carry

        lax.fori_loop(0, 4, store, 0)
        rcopy(give.at[h], got.at[h], sg.at[h], rg.at[h], sib).start()
        return carry

    lax.fori_loop(0, HG, per_head, 0)
    settle(HG - 1)

    def final(h, carry):
        for d in (1, 2, 3):
            landed(got_y.at[h, step(y, d)], ry.at[h, step(y, d)])
        for i in range(2):
            for k in range(2):
                v = mine[h, i, k, y].astype(F32)
                for d in (1, 2, 3):
                    v = v + got_y[h, step(y, d), i, k].astype(F32)
                dkv[h, i, k] = v.astype(BF)
        landed(give.at[h], sg.at[h])
        for d in (1, 2, 3):
            landed(got_y.at[h, y], sy.at[h, d])
        return carry

    lax.fori_loop(0, HG, final, 0)
    for d in (1, 2, 3):
        landed(za.at[step(x, d)], r3.at[0, step(x, d)])
        landed(zd.at[step(x, d)], r3.at[1, step(x, d)])
    landed(za.at[x], lo.at[2])
    landed(zd.at[x], lo.at[3])
    for d in (1, 2, 3):
        landed(ra.at[x], s1.at[0, d])
        landed(rd.at[y], s1.at[1, d])
        landed(fa.at[0], s2.at[0, d])
        landed(fd.at[0], s2.at[1, d])
        landed(fa.at[0], s3.at[0, d])
        landed(fd.at[0], s3.at[1, d])


def attend_back(length, q, kv, wo, dmix, att, lse, ha, hd):
    n = BLOCKS * ROWS
    V = pltpu.VMEM
    return remote_call(
        attend_back_kernel,
        [
            ((HG, n, HDIM), F32, "v"),
            ((HG, 2, 2, ROWS, 128), BF, "v"),
            ((GROUP, D), BF, "v"),
            ((4, 80, D), BF, "a"),
            ((4, 80, 640), BF, "a"),
        ],
        "svvvvvvaa",
        [
            V((HG, BLOCKS, 2 * ROWS, 128), BF),
            V((HG, BLOCKS, 128), F32),
            V((8, 128, TILE), BF),
            V((8, TILE, 128), F32),
            V((n, GROUP), BF),
            V((HG, 2, 2, 4, ROWS, 128), BF),
            V((HG, 2, 2, 4, ROWS, 128), BF),
            V((HG, 2, 2, 4, ROWS, 128), BF),
            V((HG, 4, 2, 2, ROWS, 128), BF),
            V((4, 80, D), BF), V((4, 80, 640), BF),
            V((4, 4, 80, D), BF), V((4, 4, 80, 640), BF),
            V((4, 80, D), BF), V((4, 80, 640), BF),
            dma(HG), dma(HG), dma(HG, 4), dma(HG, 4),
            dma(2, 4), dma(2, 4), dma(2, 4), dma(2, 4), dma(2, 4), dma(2, 4), dma(4),
        ],
        3,
        "attend_back",
    )(length, q, kv, wo, dmix, att, lse, ha, hd)


def inv_rms(v):
    return lax.rsqrt(jnp.mean(v * v, axis=-1, keepdims=True) + EPS)


def back_rms(dy, yy, inv):
    return (dy - yy * jnp.mean(dy * yy, axis=-1, keepdims=True)) * inv


def total_of(buf):
    return (buf[0].astype(F32) + buf[1].astype(F32)) + (buf[2].astype(F32) + buf[3].astype(F32))


def mix_of(res, part, rate):
    inv_p = inv_rms(part)
    unit = part * inv_p
    diff = unit - res
    u = res + rate * diff
    inv_u = inv_rms(u)
    return u * inv_u, unit, inv_p, inv_u, diff


def mix_back(dy, res, part, rate):
    yy, unit, inv_p, inv_u, diff = mix_of(res, part, rate)
    du = back_rms(dy, yy, inv_u)
    return du * (1.0 - rate), back_rms(du * rate, unit, inv_p), jnp.sum(du * diff, axis=0, keepdims=True)


def mid_kernel(
    part0, st, cot, rate_a, rate_m, su, sg, valid, wu_in, gz, w_down,
    result, d_st, dm, ha, hd, vec,
    buf, low, xg, dd, wu, wg, wd, up, gate, hid, dug, part, xt, ht, mixed, first, dfirst, ga, gd, ra, rd,
    ps, pr, gs, gr, s2, r2, s3, r3, sx, rx, lo,
):
    x, c, z, y = here()
    sib = dev(x, 1 - c, z, y)
    half = pl.ds(pl.multiple_of(c * 640, 128), 640)
    other = pl.ds(pl.multiple_of((1 - c) * 640, 128), 640)
    near = z // 2
    greet(z_peers(x, c, z, y) + [dev(x, c, z, step(y, d)) for d in (1, 2, 3)])
    z_scatter_start(part0, buf.at[0], ps.at[0], pr.at[0], x, c, z, y)

    def down_rows(k):
        return pl.ds(pl.multiple_of(k * 320, 16), 320)

    for d in (1, 3, 2):
        rcopy(gz, wg.at[:, y, :, half], s2.at[0, d], r2.at[0, y], dev(x, c, z, step(y, d))).start()
    rcopy(gz, wg.at[:, y, :, half], s3.at[0, 0], r3.at[0, y], sib).start()
    for d in (1, 3, 2):
        to = dev(x, c, z, step(y, d))
        rcopy(w_down.at[:, half], wd.at[down_rows(y), half], s2.at[1, d], r2.at[1, y], to).start()
    rcopy(w_down.at[:, half], wd.at[down_rows(y), half], s3.at[1, 0], r3.at[1, y], sib).start()
    lcopy(wu_in, wu, lo.at[0]).start()
    lcopy(gz, wg.at[:, y, :, half], lo.at[1]).start()
    lcopy(w_down.at[:, half], wd.at[down_rows(y), half], lo.at[2]).start()
    vec[...] = jnp.zeros_like(vec)

    z_scatter_take(buf.at[0], pr.at[0])
    total = total_of(buf.at[0])
    mixed[...] = total
    out = mix_of(st[...].astype(F32), total, rate_a[0:1])[0]
    first[...] = out
    low[0] = out.astype(BF)
    z_gather_start(low.at[0], xg, gs.at[0], gr.at[0], x, c, z, y)

    for d in (1, 3, 2):
        y2 = step(y, d)
        landed(wg.at[:, y2, :, half], r2.at[0, y2])
        rcopy(wg.at[:, y2, :, half], wg.at[:, y2, :, half], s3.at[0, d], r3.at[0, y2], sib).start()
    landed(wu, lo.at[0])
    landed(wg.at[:, y, :, half], lo.at[1])
    for k in range(4):
        landed(wg.at[:, k, :, other], r3.at[0, k])

    def rows_of(ref, p):
        return ref[p].reshape(2 * ROWS, D)

    def forward_cols(p):
        z_gather_take(xg, gr.at[0], p)

        def body(t, carry):
            cs = pl.ds(pl.multiple_of(t * 256, 256), 256)
            xs = rows_of(xg, p)
            u = jnp.dot(xs, wu[:, :, :, cs].reshape(D, 256), preferred_element_type=F32)
            g = jnp.dot(xs, wg[:, :, :, cs].reshape(D, 256), preferred_element_type=F32)
            tt = g * sg[0:1, cs]
            up[p, :, cs] = u
            gate[p, :, cs] = g
            hid[p, :, cs] = (u * su[0:1, cs] * (tt * jax.nn.sigmoid(tt))).astype(BF)
            return carry

        lax.fori_loop(0, 5, body, 0)

    def forward_down(p):
        def body(t, carry):
            cs = pl.ds(pl.multiple_of(t * 256, 256), 256)
            v = jnp.dot(hid[p], wd[:, cs], preferred_element_type=F32)
            part[0, p, :, :, cs] = v.astype(BF).reshape(2, ROWS, 256)
            return carry

        lax.fori_loop(0, 5, body, 0)
        z_scatter_pair(part.at[0], buf.at[1], ps.at[1], pr.at[1], p, x, c, z, y)

    forward_cols(near)
    for d in (1, 3, 2):
        y2 = step(y, d)
        landed(wd.at[down_rows(y2), half], r2.at[1, y2])
        rcopy(wd.at[down_rows(y2), half], wd.at[down_rows(y2), half], s3.at[1, d], r3.at[1, y2], sib).start()
    landed(wd.at[down_rows(y), half], lo.at[2])
    for k in range(4):
        landed(wd.at[down_rows(k), other], r3.at[1, k])
    forward_down(near)
    forward_cols(1 - near)
    forward_down(1 - near)

    def turn(dst, load):
        def body(t, carry):
            cs = pl.ds(pl.multiple_of(t * 256, 256), 256)
            for p in range(2):
                dst[cs, p * 256 : (p + 1) * 256] = load(p, cs).T
            return carry

        lax.fori_loop(0, 5, body, 0)

    turn(xt, lambda p, cs: xg[p, :, :, cs].reshape(256, 256))
    turn(ht, lambda p, cs: hid[p, :, cs])

    z_scatter_take(buf.at[1], pr.at[1])
    total = total_of(buf.at[1])
    live = valid[:, 0:1]
    base = first[...]
    d_base, d_part, g_am = mix_back(cot[...].astype(F32) * live, base, total, rate_m[0:1])
    low[1] = d_part.astype(BF)
    z_gather_start(low.at[1], dd, gs.at[1], gr.at[1], x, c, z, y)
    dfirst[...] = d_base
    vec[1:2] = g_am
    result[...] = (mix_of(base, total, rate_m[0:1])[0] * live).astype(BF)

    def backward_cols(p):
        z_gather_take(dd, gr.at[1], p)

        def body(t, carry):
            cs = pl.ds(pl.multiple_of(t * 256, 256), 256)
            dh = nt(rows_of(dd, p), wd[cs, :])
            u, g = up[p, :, cs], gate[p, :, cs]
            sc, sgc = su[0:1, cs], sg[0:1, cs]
            tt = g * sgc
            sig = jax.nn.sigmoid(tt)
            silu = tt * sig
            dsilu = sig * (1.0 + tt * (1.0 - sig))
            dhs = dh * sc
            dhu = dh * u
            both = dhu * dsilu * sc
            dug[0, p, :, cs] = (dhs * silu).astype(BF)
            dug[1, p, :, cs] = (both * sgc).astype(BF)
            vec[2:3, cs] += jnp.sum(dhu * silu, axis=0, keepdims=True)
            vec[3:4, cs] += jnp.sum(both * g, axis=0, keepdims=True)
            return carry

        lax.fori_loop(0, 5, body, 0)
        for t in range(2):
            v = nt(dug[0, p], wu[2 * t : 2 * t + 2].reshape(640, D)) + nt(
                dug[1, p], wg[2 * t : 2 * t + 2].reshape(640, D)
            )
            part[1, p, :, :, t * 640 : (t + 1) * 640] = v.astype(BF).reshape(2, ROWS, 640)
        z_scatter_pair(part.at[1], buf.at[2], ps.at[2], pr.at[2], p, x, c, z, y)

    backward_cols(near)
    backward_cols(1 - near)

    def gradients(w):
        cols = pl.ds(pl.multiple_of(w * 640, 128), 640)

        def body(k, carry):
            rows = pl.ds(pl.multiple_of(k * 320, 64), 320)
            for t in range(2):
                cs = slice(t * 640, (t + 1) * 640)
                v = jnp.dot(xt[rows, :], dug[w, :, :, cs].reshape(512, 640), preferred_element_type=F32)
                ga[w, k, :, :, cs] = v.astype(BF).reshape(4, 80, 640)
            v = jnp.dot(ht[rows, :], dd[:, :, :, cols].reshape(512, 640), preferred_element_type=F32)
            gd[w, k] = v.astype(BF).reshape(4, 80, 640)
            return carry

        lax.fori_loop(0, 4, body, 0)

    gradients(1 - c)
    rcopy(ga.at[1 - c], ra, sx.at[0], rx.at[0], sib).start()
    rcopy(gd.at[1 - c], rd, sx.at[1], rx.at[1], sib).start()

    z_scatter_take(buf.at[2], pr.at[2])
    dy = dfirst[...] + total_of(buf.at[2])
    d_res, d_part, g_aa = mix_back(dy, st[...].astype(F32), mixed[...], rate_a[0:1])
    low[2] = d_part.astype(BF)
    z_gather_start(low.at[2], dm, gs.at[2], gr.at[2], x, c, z, y)
    d_st[...] = d_res
    vec[0:1] = g_aa
    gradients(c)
    landed(ra, rx.at[0])
    landed(rd, rx.at[1])

    def add(k, carry):
        i, j = k // 4, k % 4
        ha[i, j] = (ga[c, i, j].astype(F32) + ra[i, j].astype(F32)).astype(BF)
        hd[i, j] = (gd[c, i, j].astype(F32) + rd[i, j].astype(F32)).astype(BF)
        return carry

    lax.fori_loop(0, 16, add, 0)
    for p in range(2):
        z_gather_take(dm, gr.at[2], p)
    for k in range(3):
        z_gather_sent(low.at[k], gs.at[k], c, z)
    z_scatter_sent(part0, ps.at[0], c, z)
    z_scatter_sent(part.at[0], ps.at[1], c, z)
    z_scatter_sent(part.at[1], ps.at[2], c, z)
    for k in range(4):
        landed(gz, s3.at[0, k])
        landed(w_down.at[:, half], s3.at[1, k])
    for d in (1, 2, 3):
        landed(gz, s2.at[0, d])
        landed(w_down.at[:, half], s2.at[1, d])
    landed(ra, sx.at[0])
    landed(rd, sx.at[1])


def middle(part0, st, cot, rate_a, rate_m, su, sg, valid, wu, gz, w_down):
    V = pltpu.VMEM
    return remote_call(
        mid_kernel,
        [
            ((ROWS, D), BF, "v"),
            ((ROWS, D), F32, "v"),
            ((2, 2, ROWS, D), BF, "a"),
            ((4, 4, 80, D), BF, "v"),
            ((4, 4, 80, 640), BF, "v"),
            ((8, D), F32, "v"),
        ],
        "avvvvvvvaaa",
        [
            V((3, 4, ROWS, D), BF), V((3, ROWS, D), BF), V((2, 2, ROWS, D), BF), V((2, 2, ROWS, D), BF),
            V((4, 4, 80, D), BF), V((4, 4, 80, D), BF), V((D, D), BF),
            V((2, 256, D), F32), V((2, 256, D), F32), V((2, 256, D), BF), V((2, 2, 256, D), BF),
            V((2, 2, 2, ROWS, D), BF), V((D, 512), BF), V((D, 512), BF),
            V((ROWS, D), F32), V((ROWS, D), F32), V((ROWS, D), F32),
            V((2, 4, 4, 80, D), BF), V((2, 4, 4, 80, 640), BF), V((4, 4, 80, D), BF), V((4, 4, 80, 640), BF),
            dma(3, 2, 2), dma(3, 4), dma(3, 4), dma(3, 2, 2),
            dma(2, 4), dma(2, 4), dma(2, 4), dma(2, 4), dma(2), dma(2), dma(3),
        ],
        2,
        "middle",
    )(part0, st, cot, rate_a, rate_m, su, sg, valid, wu, gz, w_down)


def qkv_back_kernel(length, dq, dkv, t, scale, inner, outer, xg, w, part, gw, gs, d0, d1):
    _, c, _, y = here()
    gs[...] = jnp.zeros_like(gs)
    d1[:, 448:] = jnp.zeros((BLOCKS * ROWS, 64), BF)

    def per_block(j, carry):
        rows = pl.ds(pl.multiple_of(j * ROWS, ROWS), ROWS)
        b = block_index(c, y, j)
        cosine, sine = turn_of(inner, outer, b)
        live = (b * ROWS + lax.broadcasted_iota(jnp.int32, (ROWS, 1), 0) < length[0]).astype(F32)
        for h in range(HG):
            cols = slice(h * HDIM, (h + 1) * HDIM)
            sc = scale[0:1, cols]
            both = t[h, rows, :]
            kv = dkv[h, rows, :].astype(F32) * live
            for k, dy in ((0, dq[h, rows, :]), (1, kv[:, :HDIM])):
                dy = dy.astype(BF).astype(F32)
                tt = both[:, k * HDIM : (k + 1) * HDIM]
                inv = inv_rms(tt)
                unit = tt * inv
                gs[0:1, cols] += jnp.sum(dy * unit, axis=0, keepdims=True)
                dt = back_rms(dy * sc, unit, inv)
                draw = (dt * cosine + swap(dt * sine)).astype(BF)
                if k == 0:
                    d0[rows, cols] = draw
                else:
                    d1[rows, cols] = draw
            dv = kv[:, HDIM:].astype(BF)
            if h < 3:
                d0[rows, GROUP + h * HDIM : GROUP + (h + 1) * HDIM] = dv
            else:
                d1[rows, GROUP + (h - 3) * HDIM : GROUP + (h - 2) * HDIM] = dv
        return carry

    lax.fori_loop(0, BLOCKS, per_block, 0)
    part[...] = (nt(d0[...], w[0]) + nt(d1[...], w[1])).astype(BF)
    gw[0] = tn(xg[...], d0[...]).astype(BF)
    gw[1] = tn(xg[...], d1[...]).astype(BF)


def qkv_back(length, dq, dkv, t, scale, inner, outer, xg, w):
    n = BLOCKS * ROWS
    return local_call(
        qkv_back_kernel,
        [((n, D), BF), ((2, D, 512), BF), ((8, GROUP), F32)],
        8,
        [pltpu.VMEM((n, 512), BF), pltpu.VMEM((n, 512), BF)],
        "qkv_back",
        smem=1,
    )(length, dq, dkv, t, scale, inner, outer, xg, w)


def close_kernel(
    part, d_st, za_in, zd_in, gq, go, vec,
    g_in, o_q, o_k, o_v, o_out, o_up, o_gate, o_down, o_vec,
    pbuf, za, zd, hq, rq, fq, zq, ob, oy, ox, o2, vs, vb,
    ps, pr, sc, rc, lo, s1, r1, s2, r2, s3, r3, sz, rz, sf, rf, so, ro, sv, rv,
):
    x, c, z, y = here()
    sib = dev(x, 1 - c, z, y)
    to_y = [None] + [dev(x, c, z, step(y, d)) for d in (1, 2, 3)]
    to_x = [None] + [dev(step(x, d), c, z, y) for d in (1, 2, 3)]
    to_z = [None] + [dev(x, c, step(z, d), y) for d in (1, 2, 3)]
    greet(z_peers(x, c, z, y) + to_y[1:] + to_x[1:])
    rcopy(gq.at[1 - c], hq.at[1], sc.at[0], rc.at[0], sib).start()
    rcopy(vec, vb.at[0], sv.at[0, 0], rv.at[0, 0], sib).start()
    rcopy(go, ob, sc.at[1], rc.at[1], sib).start()
    z_scatter_start(part, pbuf, ps, pr, x, c, z, y)
    lcopy(gq.at[c], hq.at[0], lo.at[0]).start()
    lcopy(go, oy, lo.at[1]).start()
    for d in (1, 3, 2):
        rcopy(za_in.at[step(z, d)], za.at[c, z], sz.at[1, d], rz.at[1, z], to_z[d]).start()
    lcopy(za_in.at[z], za.at[c, z], lo.at[2]).start()
    lcopy(zd_in, zd.at[c], lo.at[3]).start()
    rcopy(zd_in, zd.at[c], sf.at[2], rf.at[2], sib).start()

    landed(hq.at[0], lo.at[0])
    landed(hq.at[1], rc.at[0])

    def add(k, carry):
        i, j = k // 4, k % 4
        hq[0, i, j] = (hq[0, i, j].astype(F32) + hq[1, i, j].astype(F32)).astype(BF)
        return carry

    lax.fori_loop(0, 16, add, 0)
    for d in (1, 3, 2):
        rcopy(hq.at[0, step(x, d)], rq.at[x], s1.at[0, d], r1.at[0, x], to_x[d]).start()
    landed(oy, lo.at[1])
    landed(ob, rc.at[1])
    landed(vb.at[0], rv.at[0, 0])
    vs[...] = vec[...] + vb[0]
    for k in range(4):
        oy[k] = (oy[k].astype(F32) + ob[k].astype(F32)).astype(BF)
    for d in (1, 3, 2):
        rcopy(oy.at[step(y, d)], ox.at[y], s1.at[1, d], r1.at[1, y], to_y[d]).start()
        rcopy(vs, vb.at[d], sv.at[1, d], rv.at[1, d], to_y[d]).start()
    acc = oy[y].astype(F32)
    tot = vs[...]
    for d in (1, 2, 3):
        landed(ox.at[step(y, d)], r1.at[1, step(y, d)])
        landed(vb.at[d], rv.at[1, d])
        landed(vs, sv.at[1, d])
        acc = acc + ox[step(y, d)].astype(F32)
        tot = tot + vb[d]
    ox[y] = acc.astype(BF)
    vs[...] = tot
    for d in (1, 3, 2):
        rcopy(ox.at[y], o2.at[d], so.at[d], ro.at[d], to_x[d]).start()
        rcopy(vs, vb.at[3 + d], sv.at[2, d], rv.at[2, d], to_x[d]).start()
    for d in (1, 2, 3):
        landed(rq.at[step(x, d)], r1.at[0, step(x, d)])
    for k in range(4):
        v = hq[0, x, k].astype(F32)
        for d in (1, 2, 3):
            v = v + rq[step(x, d), k].astype(F32)
        fq[0, k] = v.astype(BF)
    for d in (1, 3, 2):
        rcopy(fq.at[0, step(y, d)], fq.at[1, y], s2.at[d], r2.at[y], to_y[d]).start()
    acc = ox[y].astype(F32)
    tot = vs[...]
    for d in (1, 2, 3):
        landed(o2.at[d], ro.at[d])
        landed(vb.at[3 + d], rv.at[2, d])
        landed(vs, sv.at[2, d])
        acc = acc + o2[d].astype(F32)
        tot = tot + vb[3 + d]
    o_out[...] = acc
    vs[...] = tot
    for d in (1, 3, 2):
        rcopy(vs, vb.at[6 + d], sv.at[3, d], rv.at[3, d], to_z[d]).start()
    landed(za.at[c, z], lo.at[2])
    for d in (1, 2, 3):
        landed(za.at[c, step(z, d)], rz.at[1, step(z, d)])
    rcopy(za.at[c], za.at[c], sf.at[1], rf.at[1], sib).start()
    for d in (1, 2, 3):
        landed(fq.at[1, step(y, d)], r2.at[step(y, d)])
    v = fq[0, y].astype(F32)
    for d in (1, 2, 3):
        v = v + fq[1, step(y, d)].astype(F32)
    zq[0, x] = v.astype(BF)
    for d in (1, 3, 2):
        rcopy(zq.at[0, x], zq.at[0, x], s3.at[d], r3.at[x], to_x[d]).start()
    z_scatter_take(pbuf, pr)
    g_in[...] = d_st[...] + total_of(pbuf)
    for d in (1, 2, 3):
        landed(zq.at[0, step(x, d)], r3.at[step(x, d)])
    for d in (1, 3, 2):
        rcopy(zq.at[0, step(z, d)], zq.at[1 + c, z], sz.at[0, d], rz.at[0, z], to_z[d]).start()
    zq[1 + c, z] = zq[0, z]
    landed(zd.at[c], lo.at[3])
    landed(zd.at[1 - c], rf.at[2])
    landed(za.at[1 - c], rf.at[1])
    for k in range(4):
        cols = slice(k * D, (k + 1) * D)
        o_up[:, cols] = za[0, k].astype(F32)
        o_gate[:, cols] = za[1, k].astype(F32)
        for h in range(2):
            o_down[k * 80 : (k + 1) * 80, h * 640 : (h + 1) * 640] = zd[h, k].astype(F32)
    for d in (1, 2, 3):
        landed(zq.at[1 + c, step(z, d)], rz.at[0, step(z, d)])
    rcopy(zq.at[1 + c], zq.at[1 + c], sf.at[0], rf.at[0], sib).start()
    tot = vs[...]
    for d in (1, 2, 3):
        landed(vb.at[6 + d], rv.at[3, d])
        landed(vs, sv.at[3, d])
        tot = tot + vb[6 + d]
    o_vec[0:2] = tot[0:2]
    o_vec[2:] = vs[2:]
    landed(zq.at[2 - c], rf.at[0])
    for k in range(4):
        a, b = zq[1, k].astype(F32), zq[2, k].astype(F32)
        at = k * GROUP
        o_q[:, at : at + GROUP] = a[:, :GROUP]
        o_k[:, at : at + GROUP] = b[:, :GROUP]
        o_v[:, at : at + GROUP] = jnp.concatenate([a[:, GROUP:], b[:, GROUP:448]], axis=1)
    z_scatter_sent(part, ps, c, z)
    landed(hq.at[1], sc.at[0])
    landed(go, sc.at[1])
    landed(vec, sv.at[0, 0])
    landed(zq.at[1], sf.at[0])
    landed(za.at[0], sf.at[1])
    landed(zd.at[0], sf.at[2])
    for d in (1, 2, 3):
        landed(rq.at[0], s1.at[0, d])
        landed(ox.at[0], s1.at[1, d])
        landed(fq.at[0, 0], s2.at[d])
        landed(zq.at[0, 0], s3.at[d])
        landed(zq.at[0, 0], sz.at[0, d])
        landed(za.at[0, 0], sz.at[1, d])
        landed(ox.at[0], so.at[d])


def close(part, d_st, za, zd, gq, go, vec):
    V = pltpu.VMEM
    return remote_call(
        close_kernel,
        [
            ((ROWS, D), F32, "v"),
            ((80, D), F32, "v"),
            ((80, D), F32, "v"),
            ((80, D), F32, "v"),
            ((80, D), F32, "v"),
            ((80, FF), F32, "v"),
            ((80, FF), F32, "v"),
            ((320, D), F32, "v"),
            ((8, D), F32, "v"),
        ],
        "avaaaav",
        [
            V((4, ROWS, D), BF), V((2, 4, 80, D), BF), V((2, 4, 80, 640), BF),
            V((2, 4, 4, 80, 512), BF), V((4, 4, 80, 512), BF), V((2, 4, 80, 512), BF), V((3, 4, 80, 512), BF),
            V((4, 80, D), BF), V((4, 80, D), BF), V((4, 80, D), BF), V((4, 80, D), BF), V((8, D), F32), V((10, 8, D), F32),
            dma(2, 2), dma(4), dma(2), dma(2), dma(4),
            dma(2, 4), dma(2, 4), dma(4), dma(4), dma(4), dma(4), dma(2, 4), dma(2, 4), dma(3), dma(3),
            dma(4), dma(4), dma(4, 4), dma(4, 4),
        ],
        4,
        "close",
    )(part, d_st, za, zd, gq, go, vec)


def shards(
    states, w_query, w_key, w_value, w_out, w_up, w_gate, w_down,
    scale_qk, alpha_attn, alpha_mlp, scale_up, scale_gate, lengths, cotangent,
):
    x, c, z, y = here()
    st = states[0]
    position = (c * 16 + z * 4 + y) * ROWS + jnp.arange(ROWS, dtype=jnp.int32)
    valid = jnp.broadcast_to((position < lengths[0]).astype(F32)[:, None], (ROWS, 128))

    def heads(w):
        return w.reshape(80, 4, HG, HDIM)

    q4, k4, v4 = heads(w_query), heads(w_key), heads(w_value)
    half0 = jnp.concatenate([q4, v4[:, :, :3]], axis=2)
    half1 = jnp.concatenate([k4, v4[:, :, 3:], jnp.zeros_like(v4[:, :, :1])], axis=2)
    wq = jnp.stack([half0, half1]).reshape(2, 80, 4, 512).transpose(0, 2, 1, 3)
    vec = jnp.concatenate([scale_qk, alpha_attn, alpha_mlp, scale_up, scale_gate, jnp.zeros((16,), BF)])
    vec = jnp.broadcast_to(vec.astype(F32)[None], (8, 896))
    xg, wqkv, vecs, wo = open_gather(st, wq, vec, w_out)
    rows = vecs[:, :, 0].reshape(16, 896)
    mine = lax.dynamic_slice_in_dim(rows, z * 4, 4, 0)

    def wide(v):
        return jnp.broadcast_to(v.reshape(1, -1), (8, v.size))

    scale_g = wide(mine[:, :80])
    rate_a = wide(rows[:, 80:160])
    rate_m = wide(rows[:, 160:240])
    su = wide(mine[:, 240:560])
    sg = wide(mine[:, 560:880])

    inner, outer = (jnp.asarray(t) for t in rope_tables())
    n = BLOCKS * ROWS
    xg2 = xg.reshape(n, D)
    wqkv2 = wqkv.reshape(2, D, 512)
    wo2 = wo.reshape(GROUP, D)
    q, kv, turned = make_qkv(xg2, wqkv2, scale_g, inner, outer)
    part, att, lse, kv_all, wu, gz = attend(lengths, q, kv.reshape(HG, 2, 2, ROWS, 128), wo2, w_up, w_gate)
    result, d_st, dm, ha, hd, vec = middle(
        part.reshape(2, 2, ROWS, D), st, cotangent[0], rate_a, rate_m, su, sg, valid, wu, gz, w_down
    )
    dq, dkv, go, za, zd = attend_back(lengths, q, kv_all, wo2, dm.reshape(n, D), att, lse, ha, hd)
    part, gq, g_sq = qkv_back(lengths, dq, dkv.reshape(HG, n, 128), turned, scale_g, inner, outer, xg2, wqkv2)
    vec = jnp.concatenate([vec[:4], jnp.pad(g_sq[0:1], ((0, 0), (0, D - GROUP))), vec[5:]])
    g_in, o_q, o_k, o_v, o_out, o_up, o_gate, o_down, o_vec = close(
        part.reshape(2, 2, ROWS, D), d_st, za, zd, gq.reshape(2, 4, 4, 80, 512), go.reshape(4, 80, D), vec
    )
    shard = z * 4 + y
    cut = lax.dynamic_slice_in_dim
    return (
        result[None],
        g_in[None],
        o_q,
        o_k,
        o_v,
        o_out,
        o_up,
        o_gate,
        o_down,
        cut(o_vec[4], y * 80, 80, 0),
        cut(o_vec[0], shard * 80, 80, 0),
        cut(o_vec[1], shard * 80, 80, 0),
        cut(o_vec[2], y * 320, 320, 0),
        cut(o_vec[3], y * 320, 320, 0),
    )


def solution(mesh):
    row = P("grp", ("seq", "shard"), None)
    mat = P("shard", None)
    one = P("shard")
    return jax.shard_map(
        shards,
        mesh=mesh,
        in_specs=(row,) + (mat,) * 7 + (one,) * 5 + (P("grp"), row),
        out_specs=(row, row) + (mat,) * 7 + (one,) * 5,
        check_vma=False,
    )
```

time: 606 us -> 410 us (0.68)
  Pallas kernels: 523 us -> 382 us
  matrix products: 31.6 us -> 0 us
  local copies, waits for them, and re-layouts: 35.9 us -> 23.9 us
  other arithmetic: 8.97 us -> 1.76 us
    pallas_call x10 -> x5, Pallas kernels: 492 us -> 352 us  [the longest x1 117 us: middle(): remote_call(mid_kernel, [((ROWS, D), BF, 'v'), ((ROWS, D), F32, 'v'), ((2...]
    dot_general x10 -> x0, matrix products: 31.6 us -> none  [the longest x1 7.22 us: shards(): lax.dot_general(dd, wdn, (((1,), (1,)), ((), ())), preferred_element_type...]
    slice x9 -> x3, local copies, waits for them, and re-layouts: 10.1 us -> 0.1 us  [the longest x1 0.09 us: shards(): sg = wide(mine[:, 560:880])]
    unnamed x54 -> x42, local copies, waits for them, and re-layouts: 14 us -> 13.6 us
where the time goes in v2:
time: 410 us; the launch traced here: 409 us
  Pallas kernels  382 us (93%)
  local copies, waits for them, and re-layouts  23.9 us (6%)
    pallas_call x1, Pallas kernels, middle(): remote_call(mid_kernel, [((ROWS, D), BF, 'v'), ((ROWS, D), F32, 'v'), ((2...  117 us
    pallas_call x1, Pallas kernels, attend_back(): remote_call(attend_back_kernel, [((HG, n, HDIM), F32, 'v'), ((HG, 2, 2, R...  80.7 us
    pallas_call x1, Pallas kernels, attend(): remote_call(attend_kernel, [((n, D), BF, 'v'), ((HG, n, HDIM), F32, 'v'),...  66.3 us
    pallas_call x1, Pallas kernels, close(): remote_call(close_kernel, [((ROWS, D), F32, 'v'), ((80, D), F32, 'v'), ((...  50.9 us
    pallas_call x1, Pallas kernels, open_gather(): remote_call(open_kernel, [((2, 2, ROWS, D), BF, 'a'), ((2, 4, 4, 80, 512)...  36.5 us
    pallas_call x1, Pallas kernels, qkv_back(): local_call(qkv_back_kernel, [((n, D), BF), ((2, D, 512), BF), ((8, GROUP)...  20.3 us
    unnamed x42, local copies, waits for them, and re-layouts  13.6 us
    pallas_call x1, Pallas kernels, make_qkv(): local_call(qkv_kernel, [((HG, n, 128), BF), ((HG, n, 128), BF), ((HG, n,...  10.2 us

profile of v2, /device:TPU:1, one launch (start us, length us, event | category | flops | bytes accessed | tf_op | source)
XLA Modules:
  0.0 409.3 jit_solution(10435580205932627801)
XLA Ops:
  0.7 1.1 copy.36
  1.9 1.2 copy.35
  3.1 0.1 pad_maximum_fusion
  3.2 0.2 copy.40
  3.4 0.2 copy.38
  3.7 0.1 pad.12.clone
  3.8 0.1 maximum_maximum_fusion
  3.9 0.2 copy.41
  4.1 0.9 maximum_bitcast_fusion.wq
  5.0 0.1 concatenate.22
  5.1 0.6 broadcast_in_dim.57.vec
  5.7 36.5 %open_gather.1 = (bf16[2,2,128,1280]{3,2,1,0:T(8,128)(2,1)}, bf16[2,4,4,80,512]{4,3,2,1,0:T(8,128)(2,1)}, f32[4,4,8,896]{3,2,1,0:T(8,128)}, bf16[4,80,1280]{2,1,0:T(8,128)(2,1)}) custom-call(bf16[128,1280]{1,0:T(8,128)(2,1)} %bitcast.39, bf16[2,4,80,512]{3,2,1,0:T(8,128)(2,1)} %maximum_bitcast_fusion.wq, f32[8,896]{1,0:T(8,128)} %broadcast_in_dim.57.vec, ...), custom_call_target="tpu_custom_call" | custom-call | tf_op jit(solution)/shard_map/open_gather/pallas_call | solution.py:230
  42.3 1.2 slice_reduce_fusion
  43.5 0.1 broadcast_in_dim.58
  43.6 0.6 broadcast_in_dim.59.scale
  44.2 10.2 %make_qkv.1 = (bf16[5,512,128]{2,1,0:T(8,128)(2,1)}, bf16[5,512,128]{2,1,0:T(8,128)(2,1)}, f32[5,512,128]{2,1,0:T(8,128)}) custom-call(bf16[512,1280]{1,0:T(8,128)(2,1)} %bitcast.32, bf16[2,1280,512]{2,1,0:T(8,128)(2,1)} %bitcast.30, f32[8,320]{1,0:T(8,128)} %broadcast_in_dim.59.scale, f32[2,128,64]{2,1,0:T(8,128)} %constant.60.clone.inner, ...), custom_call_target="tpu_custom_call" | custom-call | tf_op jit(solution)/shard_map/make_qkv/pallas_call | solution.py:306
  55.0 66.3 %attend.1 = (bf16[512,1280]{1,0:T(8,128)(2,1)}, f32[5,512,64]{2,1,0:T(8,128)}, f32[5,4,128]{2,1,0:T(4,128)}, bf16[5,2,2,2,4,128,128]{6,5,4,3,2,1,0:T(8,128)(2,1)...) custom-call(s32[1]{0:T(128)} %copy.52.length, bf16[5,512,128]{2,1,0:T(8,128)(2,1)} %get-tuple-element.53.q, ...), custom_call_target="tpu_custom_call" | custom-call | tf_op jit(solution)/shard_map/attend/pallas_call | solution.py:470
  121.3 0.1 fusion.5
  121.4 0.1 broadcast_in_dim.64
  121.5 0.6 broadcast_in_dim.65.su
  122.1 0.1 broadcast_in_dim.66
  122.2 0.6 broadcast_in_dim.67.sg
  122.8 0.7 broadcast_in_dim.68.valid
  123.6 0.1 broadcast_in_dim.60
  123.7 0.6 broadcast_in_dim.61.rate_a
  124.3 0.1 broadcast_in_dim.62
  124.4 0.6 broadcast_in_dim.63.rate_m
  125.0 117.0 %middle.1 = (bf16[128,1280]{1,0:T(8,128)(2,1)}, f32[128,1280]{1,0:T(8,128)}, bf16[2,2,128,1280]{3,2,1,0:T(8,128)(2,1)}, bf16[4,4,80,1280]{3,2,1,0:T(8,128)(2,1)}...) custom-call(bf16[2,2,128,1280]{3,2,1,0:T(8,128)(2,1)} %bitcast.41, bf16[128,1280]{1,0:T(8,128)(2,1)} %bitcast.40, ...), custom_call_target="tpu_custom_call" | custom-call | tf_op jit(solution)/shard_map/middle/pallas_call | solution.py:914
  242.1 80.7 %attend_back.1 = (f32[5,512,64]{2,1,0:T(8,128)}, bf16[5,2,2,128,128]{4,3,2,1,0:T(8,128)(2,1)}, bf16[320,1280]{1,0:T(8,128)(2,1)}, bf16[4,80,1280]{2,1,0:T(8,128)(2,1)}, bf16[4,80,640]{2,1,0:T(8,128)(2,1)}) custom-call(s32[1]{0:T(128)} %copy.52.length, bf16[5,512,128]{2,1,0:T(8,128)(2,1)} %get-tuple-element.53.q, ...), custom_call_target="tpu_custom_call" | custom-call | tf_op jit(solution)/shard_map/attend_back/pallas_call | solution.py:658
  322.8 20.3 %qkv_back.1 = (bf16[512,1280]{1,0:T(8,128)(2,1)}, bf16[2,1280,512]{2,1,0:T(8,128)(2,1)}, f32[8,320]{1,0:T(8,128)}) custom-call(s32[1]{0:T(128)} %copy.52.length, f32[5,512,64]{2,1,0:T(8,128)} %get-tuple-element.66.dq, bf16[5,512,128]{2,1,0:T(8,128)(2,1)} %bitcast.50, f32[5,512,128]{2,1,0:T(8,128)} %get-tuple-element.68.t, f32[8,320]{1,0:T(8,128)} %broadcast_in_dim.59.scale, ...), custom_call_target="tpu_custom_call" | custom-call | tf_op jit(solution)/shard_map/qkv_back/pallas_call | solution.py:982
  343.2 0.7 slice.57
  343.9 0.6 fusion.vec
  344.5 50.9 %close.1 = (f32[128,1280]{1,0:T(8,128)}, f32[80,1280]{1,0:T(8,128)}, f32[80,1280]{1,0:T(8,128)}, f32[80,1280]{1,0:T(8,128)}, f32[80,1280]{1,0:T(8,128)}, /*index...) custom-call(bf16[2,2,128,1280]{3,2,1,0:T(8,128)(2,1)} %bitcast.42, ...), custom_call_target="tpu_custom_call" | custom-call | tf_op jit(solution)/shard_map/close/pallas_call | solution.py:1134
  395.4 1.0 fusion.7
  396.4 0.7 dynamic-slice_reduce_fusion
  397.1 0.6 fusion.2
  397.7 0.6 fusion.4
  398.3 0.7 copy.53
  399.0 2.0 copy.54
  401.0 0.8 copy.55
  401.8 0.8 copy.56
  402.5 0.8 copy.57
  403.3 0.8 copy.58
  404.0 1.2 copy.59
  405.2 0.9 copy-done.1
  406.1 1.2 copy.60
  407.2 0.9 copy-done
  408.1 1.2 copy.61
  (37 shorter events, 0.2 us)
Async XLA Ops:
  1.8 1.6 copy-start.8
  3.6 1.4 copy-start.10
  3.6 1.4 copy-start.11
  3.6 1.4 copy-start.12
  3.7 1.4 copy-start.13
  3.7 1.4 copy-start.14
  322.8 21.0 %copy-start.9 = (f32[8,1280]{1,0:T(8,128)S(1)}, f32[8,1280]{1,0:T(8,128)}, u32[]{:S(2)}) copy-start(f32[8,1280]{1,0:T(8,128)} %get-tuple-element.75) | copy-start | bytes 122884
  344.5 53.8 %copy-start.7 = (bf16[128,1280]{1,0:T(8,128)(2,1)S(1)}, bf16[128,1280]{1,0:T(8,128)(2,1)}, u32[]{:S(2)}) copy-start(bf16[128,1280]{1,0:T(8,128)(2,1)} %get-tuple-element.59) | copy-start | bytes 983044
  395.4 5.6 %copy-start.6 = (f32[80,1280]{1,0:T(8,128)S(1)}, f32[80,1280]{1,0:T(8,128)}, u32[]{:S(2)}) copy-start(f32[80,1280]{1,0:T(8,128)} %get-tuple-element.115) | copy-start | bytes 1228804
  395.4 6.4 %copy-start.5 = (f32[80,1280]{1,0:T(8,128)S(1)}, f32[80,1280]{1,0:T(8,128)}, u32[]{:S(2)}) copy-start(f32[80,1280]{1,0:T(8,128)} %get-tuple-element.116) | copy-start | bytes 1228804
  398.3 4.3 %copy-start.4 = (f32[80,1280]{1,0:T(8,128)S(1)}, f32[80,1280]{1,0:T(8,128)}, u32[]{:S(2)}) copy-start(f32[80,1280]{1,0:T(8,128)} %get-tuple-element.117) | copy-start | bytes 1228804
  399.0 4.3 %copy-start.3 = (f32[80,1280]{1,0:T(8,128)S(1)}, f32[80,1280]{1,0:T(8,128)}, u32[]{:S(2)}) copy-start(f32[80,1280]{1,0:T(8,128)} %get-tuple-element.118) | copy-start | bytes 1228804
  401.0 3.0 copy-start.2
  404.0 2.0 copy-start.1
  406.1 2.0 copy-start

commit v3 on v2

v3 whole, which is shorter than its diff:
```python
import functools
import math

import jax
import jax.numpy as jnp
import numpy as np
from jax import lax
from jax.experimental import pallas as pl
from jax.experimental.pallas import tpu as pltpu
from jax.sharding import PartitionSpec as P


D, HEADS, HDIM, FF = 1280, 20, 64, 5120
ROWS, BLOCKS, HG = 128, 4, 5
GROUP = HG * HDIM
EPS = 1e-6
BF, F32 = jnp.bfloat16, jnp.float32
MESH = pl.DeviceIdType.MESH
VMEM_LIMIT = 60 << 20


def here():
    s = lax.axis_index("shard")
    return lax.axis_index("grp"), lax.axis_index("seq"), s // 4, s % 4


def dev(x, c, z, y):
    return (x, c, z * 4 + y)


def worker(z):
    return ((z + 1) // 2) % 2


def owner_z(w, i):
    return i * (3 - 2 * w) + w


def step(v, d):
    return (v + d) % 4


def rcopy(src, dst, ss, rs, to):
    return pltpu.make_async_remote_copy(
        src_ref=src, dst_ref=dst, send_sem=ss, recv_sem=rs, device_id=to, device_id_type=MESH
    )


def lcopy(src, dst, sem):
    return pltpu.make_async_copy(src, dst, sem)


def landed(dst, sem):
    pltpu.make_async_copy(dst, dst, sem).wait()


def greet(peers):
    bar = pltpu.get_barrier_semaphore()
    for p in peers:
        pl.semaphore_signal(bar, inc=1, device_id=p, device_id_type=MESH)
    pl.semaphore_wait(bar, len(peers))


def z_peers(x, c, z, y):
    far = [dev(x, cc, step(z, d), y) for d in (1, 2, 3) for cc in (0, 1)]
    return [dev(x, 1 - c, z, y)] + far


def z_gather_start(src, dst, ss, rs, x, c, z, y):
    w = worker(z)
    slot = (z // 2, c)
    for d in (1, 3, 2):
        rcopy(src, dst.at[slot], ss.at[d], rs.at[slot], dev(x, w, step(z, d), y)).start()

    @pl.when(c == w)
    def _():
        lcopy(src, dst.at[slot], rs.at[slot]).start()

    @pl.when(c != w)
    def _():
        rcopy(src, dst.at[slot], ss.at[0], rs.at[slot], dev(x, w, z, y)).start()


def z_gather_take(dst, rs, p):
    for k in range(2):
        landed(dst.at[p, k], rs.at[p, k])


def z_gather_sent(src, ss, c, z):
    for d in (1, 2, 3):
        landed(src, ss.at[d])

    @pl.when(c != worker(z))
    def _():
        landed(src, ss.at[0])


def z_gather_wait(src, dst, ss, rs, c, z):
    for p in range(2):
        z_gather_take(dst, rs, p)
    z_gather_sent(src, ss, c, z)


def z_scatter_pair(part, dst, ss, rs, p, x, c, z, y):
    oz = owner_z(c, p)
    for oc in range(2):
        mine = jnp.logical_and(c == oc, z == oz)

        @pl.when(mine)
        def _(oc=oc):
            lcopy(part.at[p, oc], dst.at[z], rs.at[z]).start()

        @pl.when(jnp.logical_not(mine))
        def _(oc=oc):
            rcopy(part.at[p, oc], dst.at[z], ss.at[p, oc], rs.at[z], dev(x, oc, oz, y)).start()


def z_scatter_start(part, dst, ss, rs, x, c, z, y):
    for p in range(2):
        z_scatter_pair(part, dst, ss, rs, p, x, c, z, y)


def z_scatter_take(dst, rs):
    for k in range(4):
        landed(dst.at[k], rs.at[k])


def z_scatter_sent(part, ss, c, z):
    for p in range(2):
        for oc in range(2):
            mine = jnp.logical_and(c == oc, z == owner_z(c, p))

            @pl.when(jnp.logical_not(mine))
            def _(p=p, oc=oc):
                landed(part.at[p, oc], ss.at[p, oc])


def remote_call(kernel, outs, ins_spaces, scratch, cid, name):
    spec = {
        "a": pl.BlockSpec(memory_space=pl.ANY),
        "v": pl.BlockSpec(memory_space=pltpu.VMEM),
        "s": pl.BlockSpec(memory_space=pltpu.SMEM),
    }
    return pl.pallas_call(
        kernel,
        out_shape=[jax.ShapeDtypeStruct(s, d) for s, d, _ in outs],
        in_specs=[spec[s] for s in ins_spaces],
        out_specs=[spec[s] for _, _, s in outs],
        scratch_shapes=scratch,
        compiler_params=pltpu.CompilerParams(
            collective_id=cid, has_side_effects=True, vmem_limit_bytes=VMEM_LIMIT
        ),
        name=name,
    )


def local_call(kernel, outs, n_in, scratch, name, smem=0):
    vmem = pl.BlockSpec(memory_space=pltpu.VMEM)
    sm = pl.BlockSpec(memory_space=pltpu.SMEM)
    return pl.pallas_call(
        kernel,
        out_shape=[jax.ShapeDtypeStruct(s, d) for s, d in outs],
        in_specs=[sm] * smem + [vmem] * n_in,
        out_specs=[vmem for _ in outs],
        scratch_shapes=scratch,
        compiler_params=pltpu.CompilerParams(vmem_limit_bytes=VMEM_LIMIT),
        name=name,
    )


def dma(*shape):
    return pltpu.SemaphoreType.DMA(shape)


def rope_tables():
    freqs = np.exp(np.arange(32) * (-2.0 * math.log(10000.0) / 64))
    freqs = np.tile(freqs, 4)
    sign = np.tile(np.concatenate([-np.ones(32), np.ones(32)]), 2)
    inner = np.arange(ROWS)[:, None] * freqs
    outer = (np.arange(32) * ROWS)[:, None] * freqs
    return (
        np.stack([np.cos(inner), np.sin(inner) * sign]).astype(np.float32),
        np.stack([np.cos(outer), np.sin(outer) * sign]).astype(np.float32),
    )


def block_index(c, y, j):
    return (j % 2) * 16 + owner_z(c, j // 2) * 4 + y


def turn_of(inner, outer, b):
    oc = outer[0, pl.ds(b, 1), :]
    os = outer[1, pl.ds(b, 1), :]
    return oc * inner[0] - os * inner[1], os * inner[0] + oc * inner[1]


def lanes():
    return lax.broadcasted_iota(jnp.int32, (ROWS, 128), 1)


def swap(v, lane):
    return jnp.where(lane % 64 < 32, pltpu.roll(v, 96, 1), pltpu.roll(v, 32, 1))


def half_means(v, lane):
    low = jnp.sum(jnp.where(lane < 64, v, 0.0), axis=-1, keepdims=True)
    high = jnp.sum(jnp.where(lane < 64, 0.0, v), axis=-1, keepdims=True)
    return jnp.where(lane < 64, low, high) * (1.0 / 64)


TILE = 512
STEP = 6


def tiles_of(c, j):
    return (j % 2) * 4 + owner_z(c, j // 2) + 1


def nt(a, b):
    return lax.dot_general(a, b, (((1,), (1,)), ((), ())), preferred_element_type=F32)


def tn(a, b):
    return lax.dot_general(a, b, (((0,), (0,)), ((), ())), preferred_element_type=F32)


def key_tile(ref, h, t):
    zz = t % 4
    return ref[h, worker(zz), zz // 2, t // 4].reshape(TILE, 128)


def work_items(c, y, length):
    n = [tiles_of(c, j) for j in range(BLOCKS)]
    starts = [n[0], n[0] + n[1], n[0] + n[1] + n[2]]
    query = lax.broadcasted_iota(jnp.int32, (1, ROWS), 1)

    def item(i):
        hits = [(i >= s).astype(jnp.int32) for s in starts]
        j = hits[0] + hits[1] + hits[2]
        t = i - hits[0] * n[0] - hits[1] * n[1] - hits[2] * n[2]
        last = query + y * ROWS + (tiles_of(c, j) - 1 - t) * TILE
        return j, t, jnp.minimum(last, length - 1 - t * TILE)

    return item


def columns(ref, k, half):
    return ref.at[:, pl.ds(pl.multiple_of(k * D + half * 640, 128), 640)]


def front_kernel(
    length, st, wq, vec, w_out, w_up, w_gate, w_down, inner, outer,
    part, att, lse, kv_o, q_o, t_o, xg_o, wqkv_o, wo_o, scale_o, rate_a, rate_m, su, sg, wu, wd, gy,
    xg, wqkv, vecs, wo, y0, y1, kv, kvb, q, tt, low, acc, tot, gz,
    xs, xr, w1s, w1r, w2s, w2r, w3s, w3r, vs, vr, os, orr, lo,
    f1s, f1r, f2s, f2r, f3s, f3r, f4s, f4r, fl, sy, ry, sf, rf, ss, rs, kl, ol,
):
    x, c, z, y = here()
    sib = dev(x, 1 - c, z, y)
    half = pl.ds(pl.multiple_of(c * 640, 128), 640)
    other = pl.ds(pl.multiple_of((1 - c) * 640, 128), 640)
    to_z = [None] + [dev(x, c, step(z, d), y) for d in (1, 2, 3)]
    to_y = [None] + [dev(x, c, z, step(y, d)) for d in (1, 2, 3)]
    to_x = [None] + [dev(step(x, d), c, z, y) for d in (1, 2, 3)]
    near_first = (1, 3, 2)
    greet(z_peers(x, c, z, y) + to_y[1:] + to_x[1:])

    for d in near_first:
        rcopy(wq.at[c, step(z, d)], wqkv.at[c, z, y], w1s.at[d], w1r.at[z], to_z[d]).start()
        rcopy(vec, vecs.at[z, y], vs.at[0, d], vr.at[0, z], to_z[d]).start()
    lcopy(wq.at[c, z], wqkv.at[c, z, y], lo.at[0]).start()
    lcopy(vec, vecs.at[z, y], lo.at[1]).start()
    z_gather_start(st, xg, xs, xr, x, c, z, y)
    for d in near_first:
        rcopy(w_out.at[:, half], wo.at[y, :, half], os.at[0, d], orr.at[0, y], to_y[d]).start()
    rcopy(w_out.at[:, half], wo.at[y, :, half], os.at[0, 0], orr.at[1, y], sib).start()
    lcopy(w_out.at[:, half], wo.at[y, :, half], lo.at[2]).start()
    down = w_down.at[pl.ds(pl.multiple_of(x * 80, 16), 80), half]
    for d in near_first:
        rcopy(down, wd.at[y, x, :, half], f2s.at[2, d], f2r.at[2, y], to_y[d]).start()
    lcopy(down, wd.at[y, x, :, half], fl.at[2]).start()

    @pl.when(z == x)
    def _():
        for d in near_first:
            z2 = step(z, d)
            rcopy(columns(w_up, z2, c), wu.at[x, y, :, half], f1s.at[0, d], f1r.at[0], to_z[d]).start()
            rcopy(columns(w_gate, z2, c), gz, f1s.at[1, d], f1r.at[1], to_z[d]).start()
        lcopy(columns(w_up, z, c), wu.at[x, y, :, half], f1r.at[0]).start()
        lcopy(columns(w_gate, z, c), gz, f1r.at[1]).start()

    for d in (1, 2, 3):
        landed(wqkv.at[c, step(z, d), y], w1r.at[step(z, d)])
        landed(vecs.at[step(z, d), y], vr.at[0, step(z, d)])
    landed(wqkv.at[c, z, y], lo.at[0])
    landed(vecs.at[z, y], lo.at[1])
    for d in near_first:
        rcopy(wqkv.at[c, :, y], wqkv.at[c, :, y], w2s.at[d], w2r.at[y], to_y[d]).start()
        rcopy(vecs.at[:, y], vecs.at[:, y], vs.at[1, d], vr.at[1, y], to_y[d]).start()
    rcopy(wqkv.at[c, :, y], wqkv.at[c, :, y], w3s.at[0], w3r.at[y], sib).start()
    landed(wd.at[y, x, :, half], fl.at[2])
    for d in (1, 2, 3):
        landed(wd.at[step(y, d), x, :, half], f2r.at[2, step(y, d)])
    for d in near_first:
        rcopy(wd.at[:, x, :, half], wd.at[:, x, :, half], f3s.at[1, d], f3r.at[1, x], to_x[d]).start()
    rcopy(wd.at[:, x, :, half], wd.at[:, x, :, half], f4s.at[1, 0], f4r.at[1, x], sib).start()
    landed(wu.at[x, y, :, half], f1r.at[0])
    landed(gz, f1r.at[1])
    for d in near_first:
        rcopy(wu.at[x, y, :, half], wu.at[x, y, :, half], f2s.at[0, d], f2r.at[0, y], to_y[d]).start()
        rcopy(gz, gy.at[y], f2s.at[1, d], f2r.at[1, y], to_y[d]).start()
    lcopy(gz, gy.at[y], fl.at[1]).start()
    for d in near_first:
        y2 = step(y, d)
        landed(wqkv.at[c, :, y2], w2r.at[y2])
        rcopy(wqkv.at[c, :, y2], wqkv.at[c, :, y2], w3s.at[d], w3r.at[y2], sib).start()
        landed(wo.at[y2, :, half], orr.at[0, y2])
        rcopy(wo.at[y2, :, half], wo.at[y2, :, half], os.at[1, d], orr.at[1, y2], sib).start()
        landed(vecs.at[:, y2], vr.at[1, y2])
    for zz in range(4):
        for yy in range(4):
            at = (zz * 4 + yy) * 80
            rate_a[:, at : at + 80] = vecs[zz, yy, :, 80:160]
            rate_m[:, at : at + 80] = vecs[zz, yy, :, 160:240]
    for yy in range(4):
        su[:, yy * 320 : (yy + 1) * 320] = vecs[z, yy, :, 240:560]
        sg[:, yy * 320 : (yy + 1) * 320] = vecs[z, yy, :, 560:880]
    scale = jnp.concatenate([vecs[z, yy, :, :80] for yy in range(4)], axis=1)
    for h in range(HG):
        sh = scale[:, h * HDIM : (h + 1) * HDIM]
        scale_o[:, h * 128 : (h + 1) * 128] = jnp.concatenate([sh, sh], axis=1)

    for d in (1, 2, 3):
        landed(wu.at[x, step(y, d), :, half], f2r.at[0, step(y, d)])
    for d in near_first:
        rcopy(wu.at[x, :, :, half], wu.at[x, :, :, half], f3s.at[0, d], f3r.at[0, x], to_x[d]).start()
    rcopy(wu.at[x, :, :, half], wu.at[x, :, :, half], f4s.at[0, 0], f4r.at[0, x], sib).start()

    for p in range(2):
        z_gather_take(xg, xr, p)
    for k in range(4):
        landed(wqkv.at[1 - c, :, k], w3r.at[k])
    lcopy(xg, xg_o, ol.at[0]).start()
    lcopy(wqkv, wqkv_o, ol.at[1]).start()

    def project(p, carry):
        rows = xg[p].reshape(2 * ROWS, D)
        y0[p] = jnp.dot(rows, wqkv[0].reshape(D, 512), preferred_element_type=F32)
        y1[p] = jnp.dot(rows, wqkv[1].reshape(D, 512), preferred_element_type=F32)
        return carry

    lax.fori_loop(0, 2, project, 0)
    lane = lanes()

    def send(h):
        rcopy(kv.at[h], kvb.at[h, c, :, :, y], sy.at[h, 0], ry.at[h, 0], to_y[1]).start()
        rcopy(kv.at[h], kvb.at[h, c, :, :, y], sy.at[h, 1], ry.at[h, 1], to_y[3]).start()
        rcopy(kv.at[h], kvb.at[h, c, :, :, y], ss.at[h, 0], rs.at[h, 0], sib).start()
        lcopy(kv.at[h], kvb.at[h, c, :, :, y], kl.at[h]).start()

    for h in range(HG):

        def per_block(j, carry, h=h):
            p, r = j // 2, pl.ds(pl.multiple_of((j % 2) * ROWS, ROWS), ROWS)
            cosine, sine = turn_of(inner, outer, block_index(c, y, j))
            raw = y0[p, r, h * 128 : (h + 1) * 128] if h < 4 else y1[p, r, 0:128]
            t = raw * cosine + swap(raw, lane) * sine
            unit = t * lax.rsqrt(half_means(t * t, lane) + EPS)
            both = unit * scale_o[0:1, h * 128 : (h + 1) * 128]
            pair = y1[p, r, 128 + (h // 2) * 128 : 256 + (h // 2) * 128]
            v = pair if h % 2 else pltpu.roll(pair, 64, 1)
            kv[h, p, j % 2] = jnp.where(lane < 64, pltpu.roll(both, 64, 1), v).astype(BF)
            rows = pl.ds(pl.multiple_of(j * ROWS, ROWS), ROWS)
            tt[h, rows, :] = t
            q[h, rows, :] = (jnp.where(lane < 64, both, 0.0).astype(BF).astype(F32) * 0.125).astype(BF)
            return carry

        lax.fori_loop(0, BLOCKS, per_block, 0)
        send(h)
    lcopy(q, q_o, ol.at[2]).start()
    lcopy(tt, t_o, ol.at[3]).start()

    def near(h):
        for k, src, to in ((0, step(y, 3), to_y[1]), (1, step(y, 1), to_y[3])):
            landed(kvb.at[h, c, :, :, src], ry.at[h, k])
            rcopy(kvb.at[h, c, k, :, src], kvb.at[h, c, k, :, src], sf.at[h, k], rf.at[h, k], to).start()
            rcopy(kvb.at[h, c, :, :, src], kvb.at[h, c, :, :, src], ss.at[h, 1 + k], rs.at[h, 1 + k], sib).start()

    def far(h):
        src = step(y, 2)
        for k in range(2):
            landed(kvb.at[h, c, k, :, src], rf.at[h, k])
            rcopy(kvb.at[h, c, k, :, src], kvb.at[h, c, k, :, src], ss.at[h, 3 + k], rs.at[h, 3 + k], sib).start()

    def ready(h):
        landed(kvb.at[h, c, :, :, y], kl.at[h])
        landed(kvb.at[h, 1 - c, :, :, y], rs.at[h, 0])
        landed(kvb.at[h, 1 - c, :, :, step(y, 3)], rs.at[h, 1])
        landed(kvb.at[h, 1 - c, :, :, step(y, 1)], rs.at[h, 2])
        for k in range(2):
            landed(kvb.at[h, 1 - c, k, :, step(y, 2)], rs.at[h, 3 + k])
        lcopy(kvb.at[h], kv_o.at[h], kl.at[h]).start()

    item = work_items(c, y, length[0])

    def compute(h):
        acc[...] = jnp.zeros_like(acc)
        tot[...] = jnp.zeros_like(tot)

        def body(g, carry):
            key = lax.broadcasted_iota(jnp.int32, (TILE, ROWS), 0)
            its = [item(g * STEP + u) for u in range(STEP)]
            ks = [key_tile(kvb, h, t) for _, t, _ in its]
            ss_ = [
                nt(k, q[h, pl.ds(pl.multiple_of(j * ROWS, ROWS), ROWS), :]) for k, (j, _, _) in zip(ks, its)
            ]
            ps = [jnp.where(key <= bound, jnp.exp(s), 0.0) for s, (_, _, bound) in zip(ss_, its)]
            for k, p, (j, _, _) in zip(ks, ps, its):
                tot[j] += jnp.sum(p.reshape(TILE // 8, 8, ROWS), axis=0)
                acc[j] += tn(k, p.astype(BF))
            return carry

        lax.fori_loop(0, 18 // STEP, body, 0)
        for j in range(BLOCKS):
            total = jnp.sum(tot[j], axis=0, keepdims=True)
            lse[h, j : j + 1, :] = jnp.log(total)
            att[h, j * ROWS : (j + 1) * ROWS, :] = (acc[j, HDIM:] / total).T

    near(0)

    def per_head(i, carry):
        @pl.when(i + 1 < HG)
        def _():
            near(i + 1)

        @pl.when(i < HG)
        def _():
            far(i)

        @pl.when(i > 0)
        def _():
            ready(i - 1)
            compute(i - 1)

        return carry

    lax.fori_loop(0, HG + 1, per_head, 0)
    for h in range(HG):
        low[:, h * HDIM : (h + 1) * HDIM] = att[h].astype(BF)
    landed(wo.at[y, :, half], lo.at[2])
    for k in range(4):
        landed(wo.at[k, :, other], orr.at[1, k])
    lcopy(wo, wo_o, ol.at[4]).start()
    for p in range(2):
        v = jnp.dot(low[p * 256 : (p + 1) * 256, :], wo[...].reshape(GROUP, D), preferred_element_type=F32)
        part[p] = v.astype(BF).reshape(2, ROWS, D)

    for d in near_first:
        x2 = step(x, d)
        landed(wd.at[:, x2, :, half], f3r.at[1, x2])
        rcopy(wd.at[:, x2, :, half], wd.at[:, x2, :, half], f4s.at[1, d], f4r.at[1, x2], sib).start()
    for d in near_first:
        x2 = step(x, d)
        landed(wu.at[x2, :, :, half], f3r.at[0, x2])
        rcopy(wu.at[x2, :, :, half], wu.at[x2, :, :, half], f4s.at[0, d], f4r.at[0, x2], sib).start()
    landed(gz, fl.at[1])
    for d in (1, 2, 3):
        landed(gy.at[step(y, d)], f2r.at[1, step(y, d)])

    def sent(h, carry):
        for k in range(2):
            landed(kv.at[h], sy.at[h, k])
            landed(kv.at[h, 0], sf.at[h, k])
            landed(kv.at[h, 0], ss.at[h, 3 + k])
        for k in range(3):
            landed(kv.at[h], ss.at[h, k])
        landed(kvb.at[h], kl.at[h])
        return carry

    lax.fori_loop(0, HG, sent, 0)
    z_gather_sent(st, xs, c, z)
    for k in range(4):
        landed(wd.at[:, k, :, other], f4r.at[1, k])
        landed(wu.at[k, :, :, other], f4r.at[0, k])
        landed(wd.at[:, k, :, half], f4s.at[1, k])
        landed(wu.at[k, :, :, half], f4s.at[0, k])
        landed(wqkv.at[c, :, k], w3s.at[k])
    landed(wo.at[0, :, half], os.at[0, 0])
    for d in (1, 2, 3):
        landed(wqkv.at[c, z, y], w1s.at[d])
        landed(vec, vs.at[0, d])
        landed(vecs.at[:, y], vs.at[1, d])
        landed(wqkv.at[c, :, y], w2s.at[d])
        landed(wo.at[0, :, half], os.at[0, d])
        landed(wo.at[0, :, half], os.at[1, d])
        landed(gz, f2s.at[0, d])
        landed(gz, f2s.at[1, d])
        landed(gz, f2s.at[2, d])
        landed(wu.at[x, :, :, half], f3s.at[0, d])
        landed(wd.at[:, x, :, half], f3s.at[1, d])

    @pl.when(z == x)
    def _():
        for d in (1, 2, 3):
            landed(gz, f1s.at[0, d])
            landed(gz, f1s.at[1, d])

    landed(xg, ol.at[0])
    landed(wqkv, ol.at[1])
    landed(q, ol.at[2])
    landed(tt, ol.at[3])
    landed(wo, ol.at[4])


def front(length, st, wq, vec, w_out, w_up, w_gate, w_down, inner, outer):
    n = BLOCKS * ROWS
    V = pltpu.VMEM
    return remote_call(
        front_kernel,
        [
            ((2, 2, ROWS, D), BF, "v"),
            ((HG, n, HDIM), F32, "v"),
            ((HG, BLOCKS, 128), F32, "v"),
            ((HG, 2, 2, 2, 4, ROWS, 128), BF, "a"),
            ((HG, n, 128), BF, "a"),
            ((HG, n, 128), F32, "a"),
            ((2, 2, ROWS, D), BF, "a"),
            ((2, 4, 4, 80, 512), BF, "a"),
            ((4, 80, D), BF, "a"),
            ((8, HG * 128), F32, "v"),
            ((8, D), F32, "v"),
            ((8, D), F32, "v"),
            ((8, D), F32, "v"),
            ((8, D), F32, "v"),
            ((4, 4, 80, D), BF, "a"),
            ((4, 4, 80, D), BF, "a"),
            ((4, 80, 640), BF, "a"),
        ],
        "saavaaaavv",
        [
            V((2, 2, ROWS, D), BF), V((2, 4, 4, 80, 512), BF), V((4, 4, 8, 896), F32), V((4, 80, D), BF),
            V((2, 256, 512), F32), V((2, 256, 512), F32),
            V((HG, 2, 2, ROWS, 128), BF), V((HG, 2, 2, 2, 4, ROWS, 128), BF), V((HG, n, 128), BF), V((HG, n, 128), F32),
            V((n, GROUP), BF), V((BLOCKS, 128, ROWS), F32), V((BLOCKS, 8, ROWS), F32), V((80, 640), BF),
            dma(4), dma(2, 2), dma(4), dma(4), dma(4), dma(4), dma(4), dma(4), dma(2, 4), dma(2, 4), dma(2, 4), dma(2, 4), dma(3),
            dma(2, 4), dma(2), dma(3, 4), dma(3, 4), dma(2, 4), dma(2, 4), dma(2, 4), dma(2, 4), dma(3),
            dma(HG, 2), dma(HG, 2), dma(HG, 2), dma(HG, 2), dma(HG, 5), dma(HG, 5), dma(HG), dma(5),
        ],
        0,
        "front",
    )(length, st, wq, vec, w_out, w_up, w_gate, w_down, inner, outer)


def attend_back_kernel(
    length, q, kv, wo, dmix, att, lse, ha, hd,
    dq, dkv, gout, za, zd,
    qdo, delta, dqt, acc, low, give, mine, got, got_y, oa, od, ra, rd, fa, fd,
    sg, rg, sy, ry, s1, r1, s2, r2, s3, r3, lo,
):
    x, c, z, y = here()
    sib = dev(x, 1 - c, z, y)
    to_y = [None] + [dev(x, c, z, step(y, d)) for d in (1, 2, 3)]
    to_x = [None] + [dev(step(x, d), c, z, y) for d in (1, 2, 3)]
    greet([sib] + to_y[1:] + to_x[1:])
    for d in (1, 3, 2):
        rcopy(ha.at[step(x, d)], ra.at[x], s1.at[0, d], r1.at[0, x], to_x[d]).start()
        rcopy(hd.at[step(y, d)], rd.at[y], s1.at[1, d], r1.at[1, y], to_y[d]).start()
    lcopy(ha.at[x], oa, lo.at[0]).start()
    lcopy(hd.at[y], od, lo.at[1]).start()

    def first_sums():
        landed(oa, lo.at[0])
        landed(od, lo.at[1])
        for d in (1, 2, 3):
            landed(ra.at[step(x, d)], r1.at[0, step(x, d)])
            landed(rd.at[step(y, d)], r1.at[1, step(y, d)])

        def body(k, carry):
            va = oa[k].astype(F32)
            vd = od[k].astype(F32)
            for d in (1, 2, 3):
                va = va + ra[step(x, d), k].astype(F32)
                vd = vd + rd[step(y, d), k].astype(F32)
            oa[k] = va.astype(BF)
            od[k] = vd.astype(BF)
            return carry

        lax.fori_loop(0, 4, body, 0)
        for d in (1, 3, 2):
            rcopy(oa.at[step(y, d)], fa.at[y], s2.at[0, d], r2.at[0, y], to_y[d]).start()
            rcopy(od.at[step(x, d)], fd.at[x], s2.at[1, d], r2.at[1, x], to_x[d]).start()

    def second_sums():
        for d in (1, 2, 3):
            landed(fa.at[step(y, d)], r2.at[0, step(y, d)])
            landed(fd.at[step(x, d)], r2.at[1, step(x, d)])
        va = oa[y].astype(F32)
        vd = od[x].astype(F32)
        for d in (1, 2, 3):
            va = va + fa[step(y, d)].astype(F32)
            vd = vd + fd[step(x, d)].astype(F32)
        fa[y] = va.astype(BF)
        fd[x] = vd.astype(BF)
        for d in (1, 3, 2):
            rcopy(fa.at[y], za.at[x], s3.at[0, d], r3.at[0, x], to_x[d]).start()
            rcopy(fd.at[x], zd.at[x], s3.at[1, d], r3.at[1, x], to_x[d]).start()
        lcopy(fa.at[y], za.at[x], lo.at[2]).start()
        lcopy(fd.at[x], zd.at[x], lo.at[3]).start()

    def settle(h):
        landed(got.at[h], rg.at[h])
        for i in range(2):
            for k in range(2):
                mine[h, i, k] = (mine[h, i, k].astype(F32) + got[h, i, k].astype(F32)).astype(BF)
        for d in (1, 3, 2):
            rcopy(mine.at[h, :, :, step(y, d)], got_y.at[h, y], sy.at[h, d], ry.at[h, y], to_y[d]).start()

    d_att = nt(dmix[...], wo[...]).astype(BF)
    for h in range(HG):
        low[:, h * HDIM : (h + 1) * HDIM] = att[h].astype(BF)
        dh = d_att[:, h * HDIM : (h + 1) * HDIM].astype(F32)
        wide = jnp.concatenate([jnp.zeros_like(dh), dh], axis=1).astype(BF)
        prod = dh * att[h]
        for j in range(BLOCKS):
            rows = slice(j * ROWS, (j + 1) * ROWS)
            qdo[h, j, :ROWS] = q[h, rows, :]
            qdo[h, j, ROWS:] = wide[rows]
            delta[h, j : j + 1, :] = jnp.sum(prod[rows].T, axis=0, keepdims=True)
    gout[...] = tn(low[...], dmix[...]).astype(BF)
    item = work_items(c, y, length[0])

    def per_head(h, carry):
        acc[...] = jnp.zeros_like(acc)
        dqt[...] = jnp.zeros_like(dqt)

        @pl.when(h == 3)
        def _():
            first_sums()

        @pl.when(h == 4)
        def _():
            second_sums()

        def body(g, carry):
            @pl.when(jnp.logical_and(g == 1, h > 0))
            def _():
                settle(h - 1)

            key = lax.broadcasted_iota(jnp.int32, (TILE, ROWS), 0)
            its = [item(g * STEP + u) for u in range(STEP)]
            ks = [key_tile(kv, h, t) for _, t, _ in its]
            bs = [qdo[h, j] for j, _, _ in its]
            sds = [nt(k, b) for k, b in zip(ks, bs)]
            dss, ps = [], []
            for sd, (j, _, bound) in zip(sds, its):
                p = jnp.where(key <= bound, jnp.exp(sd[:, :ROWS] - lse[h, pl.ds(j, 1), :]), 0.0)
                dss.append((p * (sd[:, ROWS:] - delta[h, pl.ds(j, 1), :])).astype(BF))
                ps.append(p.astype(BF))
            for ds, p, b, (_, t, _) in zip(dss, ps, bs, its):
                acc[t] += jnp.dot(jnp.concatenate([ds, p], axis=1), b, preferred_element_type=F32)
            for k, ds, (j, _, _) in zip(ks, dss, its):
                dqt[j] += tn(k, ds)
            return carry

        lax.fori_loop(0, 18 // STEP, body, 0)
        for j in range(BLOCKS):
            dq[h, j * ROWS : (j + 1) * ROWS, :] = dqt[j].T * 0.125

        def store(i, carry):
            zi, k = i // 2, i % 2
            give[h, zi, k] = acc[k * 4 + owner_z(1 - c, zi)].astype(BF).reshape(4, ROWS, 128)
            mine[h, zi, k] = acc[k * 4 + owner_z(c, zi)].astype(BF).reshape(4, ROWS, 128)
            return carry

        lax.fori_loop(0, 4, store, 0)
        rcopy(give.at[h], got.at[h], sg.at[h], rg.at[h], sib).start()
        return carry

    lax.fori_loop(0, HG, per_head, 0)
    settle(HG - 1)

    def final(h, carry):
        for d in (1, 2, 3):
            landed(got_y.at[h, step(y, d)], ry.at[h, step(y, d)])
        for i in range(2):
            for k in range(2):
                v = mine[h, i, k, y].astype(F32)
                for d in (1, 2, 3):
                    v = v + got_y[h, step(y, d), i, k].astype(F32)
                dkv[h, i, k] = v.astype(BF)
        landed(give.at[h], sg.at[h])
        for d in (1, 2, 3):
            landed(got_y.at[h, y], sy.at[h, d])
        return carry

    lax.fori_loop(0, HG, final, 0)
    for d in (1, 2, 3):
        landed(za.at[step(x, d)], r3.at[0, step(x, d)])
        landed(zd.at[step(x, d)], r3.at[1, step(x, d)])
    landed(za.at[x], lo.at[2])
    landed(zd.at[x], lo.at[3])
    for d in (1, 2, 3):
        landed(ra.at[x], s1.at[0, d])
        landed(rd.at[y], s1.at[1, d])
        landed(fa.at[0], s2.at[0, d])
        landed(fd.at[0], s2.at[1, d])
        landed(fa.at[0], s3.at[0, d])
        landed(fd.at[0], s3.at[1, d])


def attend_back(length, q, kv, wo, dmix, att, lse, ha, hd):
    n = BLOCKS * ROWS
    V = pltpu.VMEM
    return remote_call(
        attend_back_kernel,
        [
            ((HG, n, 128), F32, "v"),
            ((HG, 2, 2, ROWS, 128), BF, "v"),
            ((GROUP, D), BF, "v"),
            ((4, 80, D), BF, "a"),
            ((4, 80, 640), BF, "a"),
        ],
        "svvvvvvaa",
        [
            V((HG, BLOCKS, 2 * ROWS, 128), BF),
            V((HG, BLOCKS, 128), F32),
            V((BLOCKS, 128, ROWS), F32),
            V((8, TILE, 128), F32),
            V((n, GROUP), BF),
            V((HG, 2, 2, 4, ROWS, 128), BF),
            V((HG, 2, 2, 4, ROWS, 128), BF),
            V((HG, 2, 2, 4, ROWS, 128), BF),
            V((HG, 4, 2, 2, ROWS, 128), BF),
            V((4, 80, D), BF), V((4, 80, 640), BF),
            V((4, 4, 80, D), BF), V((4, 4, 80, 640), BF),
            V((4, 80, D), BF), V((4, 80, 640), BF),
            dma(HG), dma(HG), dma(HG, 4), dma(HG, 4),
            dma(2, 4), dma(2, 4), dma(2, 4), dma(2, 4), dma(2, 4), dma(2, 4), dma(4),
        ],
        3,
        "attend_back",
    )(length, q, kv, wo, dmix, att, lse, ha, hd)


def inv_rms(v):
    return lax.rsqrt(jnp.mean(v * v, axis=-1, keepdims=True) + EPS)


def back_rms(dy, yy, inv):
    return (dy - yy * jnp.mean(dy * yy, axis=-1, keepdims=True)) * inv


def total_of(buf):
    return (buf[0].astype(F32) + buf[1].astype(F32)) + (buf[2].astype(F32) + buf[3].astype(F32))


def mix_of(res, part, rate):
    inv_p = inv_rms(part)
    unit = part * inv_p
    diff = unit - res
    u = res + rate * diff
    inv_u = inv_rms(u)
    return u * inv_u, unit, inv_p, inv_u, diff


def mix_back(dy, res, part, rate):
    yy, unit, inv_p, inv_u, diff = mix_of(res, part, rate)
    du = back_rms(dy, yy, inv_u)
    return du * (1.0 - rate), back_rms(du * rate, unit, inv_p), jnp.sum(du * diff, axis=0, keepdims=True)


def mid_kernel(
    length, part0, st, cot, rate_a, rate_m, su, sg, wu_in, wd_in, gy,
    result, d_st, dm, ha, hd, vec,
    buf, low, xg, dd, wu, wg, wd, up, gate, hid, dug, part, xt, ht, mixed, first, dfirst, ga, gd, ra, rd,
    ps, pr, gs, gr, s2, r2, s3, r3, sx, rx, lo,
):
    x, c, z, y = here()
    sib = dev(x, 1 - c, z, y)
    half = pl.ds(pl.multiple_of(c * 640, 128), 640)
    other = pl.ds(pl.multiple_of((1 - c) * 640, 128), 640)
    near = z // 2
    greet(z_peers(x, c, z, y) + [dev(step(x, d), c, z, y) for d in (1, 2, 3)])
    z_scatter_start(part0, buf.at[0], ps.at[0], pr.at[0], x, c, z, y)
    for d in (1, 3, 2):
        rcopy(gy, wg.at[x, :, :, half], s2.at[d], r2.at[x], dev(step(x, d), c, z, y)).start()
    rcopy(gy, wg.at[x, :, :, half], s3.at[0], r3.at[x], sib).start()
    lcopy(gy, wg.at[x, :, :, half], lo.at[1]).start()
    lcopy(wu_in, wu, lo.at[0]).start()
    lcopy(wd_in, wd, lo.at[2]).start()
    vec[...] = jnp.zeros_like(vec)

    z_scatter_take(buf.at[0], pr.at[0])
    total = total_of(buf.at[0])
    mixed[...] = total
    out = mix_of(st[...].astype(F32), total, rate_a[0:1])[0]
    first[...] = out
    low[0] = out.astype(BF)
    z_gather_start(low.at[0], xg, gs.at[0], gr.at[0], x, c, z, y)

    for d in (1, 3, 2):
        x2 = step(x, d)
        landed(wg.at[x2, :, :, half], r2.at[x2])
        rcopy(wg.at[x2, :, :, half], wg.at[x2, :, :, half], s3.at[d], r3.at[x2], sib).start()
    landed(wu, lo.at[0])
    landed(wg.at[x, :, :, half], lo.at[1])
    landed(wd, lo.at[2])
    for k in range(4):
        landed(wg.at[k, :, :, other], r3.at[k])

    def rows_of(ref, p):
        return ref[p].reshape(2 * ROWS, D)

    def forward_cols(p):
        z_gather_take(xg, gr.at[0], p)

        def body(t, carry):
            cs = pl.ds(pl.multiple_of(t * 256, 256), 256)
            xs = rows_of(xg, p)
            u = jnp.dot(xs, wu[:, cs], preferred_element_type=F32)
            g = jnp.dot(xs, wg[:, :, :, cs].reshape(D, 256), preferred_element_type=F32)
            tt = g * sg[0:1, cs]
            up[p, :, cs] = u
            gate[p, :, cs] = g
            hid[p, :, cs] = (u * su[0:1, cs] * (tt * jax.nn.sigmoid(tt))).astype(BF)
            return carry

        lax.fori_loop(0, 5, body, 0)

    def forward_down(p):
        def body(t, carry):
            cs = pl.ds(pl.multiple_of(t * 256, 256), 256)
            v = jnp.dot(hid[p], wd[:, cs], preferred_element_type=F32)
            part[0, p, :, :, cs] = v.astype(BF).reshape(2, ROWS, 256)
            return carry

        lax.fori_loop(0, 5, body, 0)
        z_scatter_pair(part.at[0], buf.at[1], ps.at[1], pr.at[1], p, x, c, z, y)

    forward_cols(near)
    forward_down(near)
    forward_cols(1 - near)
    forward_down(1 - near)

    def turn(dst, load):
        def body(t, carry):
            cs = pl.ds(pl.multiple_of(t * 256, 256), 256)
            for p in range(2):
                dst[cs, p * 256 : (p + 1) * 256] = load(p, cs).T
            return carry

        lax.fori_loop(0, 5, body, 0)

    turn(xt, lambda p, cs: xg[p, :, :, cs].reshape(256, 256))
    turn(ht, lambda p, cs: hid[p, :, cs])

    z_scatter_take(buf.at[1], pr.at[1])
    total = total_of(buf.at[1])
    position = (c * 16 + z * 4 + y) * ROWS + lax.broadcasted_iota(jnp.int32, (ROWS, 1), 0)
    live = (position < length[0]).astype(F32)
    base = first[...]
    d_base, d_part, g_am = mix_back(cot[...].astype(F32) * live, base, total, rate_m[0:1])
    low[1] = d_part.astype(BF)
    z_gather_start(low.at[1], dd, gs.at[1], gr.at[1], x, c, z, y)
    dfirst[...] = d_base
    vec[1:2] = g_am
    result[...] = (mix_of(base, total, rate_m[0:1])[0] * live).astype(BF)

    def backward_cols(p):
        z_gather_take(dd, gr.at[1], p)

        def body(t, carry):
            cs = pl.ds(pl.multiple_of(t * 256, 256), 256)
            dh = nt(rows_of(dd, p), wd[cs, :])
            u, g = up[p, :, cs], gate[p, :, cs]
            sc, sgc = su[0:1, cs], sg[0:1, cs]
            tt = g * sgc
            sig = jax.nn.sigmoid(tt)
            silu = tt * sig
            dsilu = sig * (1.0 + tt * (1.0 - sig))
            dhs = dh * sc
            dhu = dh * u
            both = dhu * dsilu * sc
            dug[0, p, :, cs] = (dhs * silu).astype(BF)
            dug[1, p, :, cs] = (both * sgc).astype(BF)
            vec[2:3, cs] += jnp.sum(dhu * silu, axis=0, keepdims=True)
            vec[3:4, cs] += jnp.sum(both * g, axis=0, keepdims=True)
            return carry

        lax.fori_loop(0, 5, body, 0)
        for t in range(2):
            v = nt(dug[0, p], wu[t * 640 : (t + 1) * 640, :]) + nt(
                dug[1, p], wg[2 * t : 2 * t + 2].reshape(640, D)
            )
            part[1, p, :, :, t * 640 : (t + 1) * 640] = v.astype(BF).reshape(2, ROWS, 640)
        z_scatter_pair(part.at[1], buf.at[2], ps.at[2], pr.at[2], p, x, c, z, y)

    backward_cols(near)
    backward_cols(1 - near)

    def gradients(w):
        cols = pl.ds(pl.multiple_of(w * 640, 128), 640)

        def body(k, carry):
            rows = pl.ds(pl.multiple_of(k * 320, 64), 320)
            for t in range(2):
                cs = slice(t * 640, (t + 1) * 640)
                v = jnp.dot(xt[rows, :], dug[w, :, :, cs].reshape(512, 640), preferred_element_type=F32)
                ga[w, k, :, :, cs] = v.astype(BF).reshape(4, 80, 640)
            v = jnp.dot(ht[rows, :], dd[:, :, :, cols].reshape(512, 640), preferred_element_type=F32)
            gd[w, k] = v.astype(BF).reshape(4, 80, 640)
            return carry

        lax.fori_loop(0, 4, body, 0)

    gradients(1 - c)
    rcopy(ga.at[1 - c], ra, sx.at[0], rx.at[0], sib).start()
    rcopy(gd.at[1 - c], rd, sx.at[1], rx.at[1], sib).start()

    z_scatter_take(buf.at[2], pr.at[2])
    dy = dfirst[...] + total_of(buf.at[2])
    d_res, d_part, g_aa = mix_back(dy, st[...].astype(F32), mixed[...], rate_a[0:1])
    low[2] = d_part.astype(BF)
    z_gather_start(low.at[2], dm, gs.at[2], gr.at[2], x, c, z, y)
    d_st[...] = d_res
    vec[0:1] = g_aa
    gradients(c)
    landed(ra, rx.at[0])
    landed(rd, rx.at[1])

    def add(k, carry):
        i, j = k // 4, k % 4
        ha[i, j] = (ga[c, i, j].astype(F32) + ra[i, j].astype(F32)).astype(BF)
        hd[i, j] = (gd[c, i, j].astype(F32) + rd[i, j].astype(F32)).astype(BF)
        return carry

    lax.fori_loop(0, 16, add, 0)
    for p in range(2):
        z_gather_take(dm, gr.at[2], p)
    for k in range(3):
        z_gather_sent(low.at[k], gs.at[k], c, z)
    z_scatter_sent(part0, ps.at[0], c, z)
    z_scatter_sent(part.at[0], ps.at[1], c, z)
    z_scatter_sent(part.at[1], ps.at[2], c, z)
    for k in range(4):
        landed(gy, s3.at[k])
    for d in (1, 2, 3):
        landed(gy, s2.at[d])
    landed(ra, sx.at[0])
    landed(rd, sx.at[1])


def middle(length, part0, st, cot, rate_a, rate_m, su, sg, wu, wd, gy):
    V = pltpu.VMEM
    return remote_call(
        mid_kernel,
        [
            ((ROWS, D), BF, "v"),
            ((ROWS, D), F32, "v"),
            ((2, 2, ROWS, D), BF, "a"),
            ((4, 4, 80, D), BF, "v"),
            ((4, 4, 80, 640), BF, "v"),
            ((8, D), F32, "v"),
        ],
        "savvvvvvaaa",
        [
            V((3, 4, ROWS, D), BF), V((3, ROWS, D), BF), V((2, 2, ROWS, D), BF), V((2, 2, ROWS, D), BF),
            V((D, D), BF), V((4, 4, 80, D), BF), V((D, D), BF),
            V((2, 256, D), F32), V((2, 256, D), F32), V((2, 256, D), BF), V((2, 2, 256, D), BF),
            V((2, 2, 2, ROWS, D), BF), V((D, 512), BF), V((D, 512), BF),
            V((ROWS, D), F32), V((ROWS, D), F32), V((ROWS, D), F32),
            V((2, 4, 4, 80, D), BF), V((2, 4, 4, 80, 640), BF), V((4, 4, 80, D), BF), V((4, 4, 80, 640), BF),
            dma(3, 2, 2), dma(3, 4), dma(3, 4), dma(3, 2, 2),
            dma(4), dma(4), dma(4), dma(4), dma(2), dma(2), dma(3),
        ],
        2,
        "middle",
    )(length, part0, st, cot, rate_a, rate_m, su, sg, wu, wd, gy)


def qkv_back_kernel(dq, dkv, t, scale, inner, outer, xg, w, part, gw, gs, d0, d1, sums):
    _, c, _, y = here()
    sums[...] = jnp.zeros_like(sums)
    gs[...] = jnp.zeros_like(gs)
    lane = lanes()

    def per_block(j, carry):
        rows = pl.ds(pl.multiple_of(j * ROWS, ROWS), ROWS)
        cosine, sine = turn_of(inner, outer, block_index(c, y, j))
        pair = None
        for h in range(HG):
            cols = slice(h * 128, (h + 1) * 128)
            tt = t[h, rows, :]
            grads = dkv[h, rows, :].astype(F32)
            turned = pltpu.roll(grads, 64, 1)
            dy = jnp.where(lane < 64, dq[h, rows, :].astype(BF).astype(F32), turned)
            inv = lax.rsqrt(half_means(tt * tt, lane) + EPS)
            unit = tt * inv
            sums[:, cols] += jnp.sum((dy * unit).reshape(ROWS // 8, 8, 128), axis=0)
            dyh = dy * scale[0:1, cols]
            dt = (dyh - unit * half_means(dyh * unit, lane)) * inv
            draw = (dt * cosine + swap(dt * sine, lane)).astype(BF)
            if h < 4:
                d0[rows, cols] = draw
            else:
                d1[rows, 0:128] = draw
            if h % 2 == 0:
                pair = turned
            if h % 2 == 1 or h == 4:
                at = 128 + (h // 2) * 128
                d1[rows, at : at + 128] = jnp.where(lane < 64, pair, grads if h % 2 else 0.0).astype(BF)
        return carry

    lax.fori_loop(0, BLOCKS, per_block, 0)
    for h in range(HG):
        v = jnp.sum(sums[:, h * 128 : (h + 1) * 128], axis=0, keepdims=True)
        gs[0:1, h * HDIM : (h + 1) * HDIM] = v[:, :HDIM] + v[:, HDIM:]
    part[...] = (nt(d0[...], w[0]) + nt(d1[...], w[1])).astype(BF)
    gw[0] = tn(xg[...], d0[...]).astype(BF)
    gw[1] = tn(xg[...], d1[...]).astype(BF)


def qkv_back(dq, dkv, t, scale, inner, outer, xg, w):
    n = BLOCKS * ROWS
    return local_call(
        qkv_back_kernel,
        [((n, D), BF), ((2, D, 512), BF), ((8, D), F32)],
        8,
        [pltpu.VMEM((n, 512), BF), pltpu.VMEM((n, 512), BF), pltpu.VMEM((8, HG * 128), F32)],
        "qkv_back",
    )(dq, dkv, t, scale, inner, outer, xg, w)


def close_kernel(
    part, za_in, zd_in, gq, go, vec,
    pbuf, za, zd, zq, o_out, o_vec,
    hq, rq, fq, ob, oy, ox, o2, vs, vb,
    ps, pr, sc, rc, lo, s1, r1, s2, r2, s3, r3, sz, rz, sf, rf, so, ro, sv, rv,
):
    x, c, z, y = here()
    sib = dev(x, 1 - c, z, y)
    to_y = [None] + [dev(x, c, z, step(y, d)) for d in (1, 2, 3)]
    to_x = [None] + [dev(step(x, d), c, z, y) for d in (1, 2, 3)]
    to_z = [None] + [dev(x, c, step(z, d), y) for d in (1, 2, 3)]
    greet(z_peers(x, c, z, y) + to_y[1:] + to_x[1:])
    rcopy(gq.at[1 - c], hq.at[1], sc.at[0], rc.at[0], sib).start()
    rcopy(vec, vb.at[0], sv.at[0, 0], rv.at[0, 0], sib).start()
    rcopy(go, ob, sc.at[1], rc.at[1], sib).start()
    z_scatter_start(part, pbuf, ps, pr, x, c, z, y)
    lcopy(gq.at[c], hq.at[0], lo.at[0]).start()
    lcopy(go, oy, lo.at[1]).start()
    for d in (1, 3, 2):
        rcopy(za_in.at[step(z, d)], za.at[c, z], sz.at[1, d], rz.at[1, z], to_z[d]).start()
    lcopy(za_in.at[z], za.at[c, z], lo.at[2]).start()
    lcopy(zd_in, zd.at[c], lo.at[3]).start()
    rcopy(zd_in, zd.at[c], sf.at[2], rf.at[2], sib).start()

    landed(hq.at[0], lo.at[0])
    landed(hq.at[1], rc.at[0])

    def add(k, carry):
        i, j = k // 4, k % 4
        hq[0, i, j] = (hq[0, i, j].astype(F32) + hq[1, i, j].astype(F32)).astype(BF)
        return carry

    lax.fori_loop(0, 16, add, 0)
    for d in (1, 3, 2):
        rcopy(hq.at[0, step(x, d)], rq.at[x], s1.at[0, d], r1.at[0, x], to_x[d]).start()
    landed(oy, lo.at[1])
    landed(ob, rc.at[1])
    landed(vb.at[0], rv.at[0, 0])
    vs[...] = vec[...] + vb[0]
    for k in range(4):
        oy[k] = (oy[k].astype(F32) + ob[k].astype(F32)).astype(BF)
    for d in (1, 3, 2):
        rcopy(oy.at[step(y, d)], ox.at[y], s1.at[1, d], r1.at[1, y], to_y[d]).start()
        rcopy(vs, vb.at[d], sv.at[1, d], rv.at[1, d], to_y[d]).start()
    acc = oy[y].astype(F32)
    tot = vs[...]
    for d in (1, 2, 3):
        landed(ox.at[step(y, d)], r1.at[1, step(y, d)])
        landed(vb.at[d], rv.at[1, d])
        landed(vs, sv.at[1, d])
        acc = acc + ox[step(y, d)].astype(F32)
        tot = tot + vb[d]
    ox[y] = acc.astype(BF)
    vs[...] = tot
    for d in (1, 3, 2):
        rcopy(ox.at[y], o2.at[d], so.at[d], ro.at[d], to_x[d]).start()
        rcopy(vs, vb.at[3 + d], sv.at[2, d], rv.at[2, d], to_x[d]).start()
    for d in (1, 2, 3):
        landed(rq.at[step(x, d)], r1.at[0, step(x, d)])
    for k in range(4):
        v = hq[0, x, k].astype(F32)
        for d in (1, 2, 3):
            v = v + rq[step(x, d), k].astype(F32)
        fq[0, k] = v.astype(BF)
    for d in (1, 3, 2):
        rcopy(fq.at[0, step(y, d)], fq.at[1, y], s2.at[d], r2.at[y], to_y[d]).start()
    acc = ox[y].astype(F32)
    tot = vs[...]
    for d in (1, 2, 3):
        landed(o2.at[d], ro.at[d])
        landed(vb.at[3 + d], rv.at[2, d])
        landed(vs, sv.at[2, d])
        acc = acc + o2[d].astype(F32)
        tot = tot + vb[3 + d]
    o_out[...] = acc
    vs[...] = tot
    for d in (1, 3, 2):
        rcopy(vs, vb.at[6 + d], sv.at[3, d], rv.at[3, d], to_z[d]).start()
    landed(za.at[c, z], lo.at[2])
    for d in (1, 2, 3):
        landed(za.at[c, step(z, d)], rz.at[1, step(z, d)])
    rcopy(za.at[c], za.at[c], sf.at[1], rf.at[1], sib).start()
    for d in (1, 2, 3):
        landed(fq.at[1, step(y, d)], r2.at[step(y, d)])
    v = fq[0, y].astype(F32)
    for d in (1, 2, 3):
        v = v + fq[1, step(y, d)].astype(F32)
    zq[0, x] = v.astype(BF)
    for d in (1, 3, 2):
        rcopy(zq.at[0, x], zq.at[0, x], s3.at[d], r3.at[x], to_x[d]).start()
    z_scatter_take(pbuf, pr)
    for d in (1, 2, 3):
        landed(zq.at[0, step(x, d)], r3.at[step(x, d)])
    for d in (1, 3, 2):
        rcopy(zq.at[0, step(z, d)], zq.at[1 + c, z], sz.at[0, d], rz.at[0, z], to_z[d]).start()
    zq[1 + c, z] = zq[0, z]
    landed(zd.at[c], lo.at[3])
    landed(zd.at[1 - c], rf.at[2])
    landed(za.at[1 - c], rf.at[1])
    for d in (1, 2, 3):
        landed(zq.at[1 + c, step(z, d)], rz.at[0, step(z, d)])
    rcopy(zq.at[1 + c], zq.at[1 + c], sf.at[0], rf.at[0], sib).start()
    tot = vs[...]
    for d in (1, 2, 3):
        landed(vb.at[6 + d], rv.at[3, d])
        landed(vs, sv.at[3, d])
        tot = tot + vb[6 + d]
    o_vec[0:2] = tot[0:2]
    o_vec[2:] = vs[2:]
    landed(zq.at[2 - c], rf.at[0])
    z_scatter_sent(part, ps, c, z)
    landed(hq.at[1], sc.at[0])
    landed(go, sc.at[1])
    landed(vec, sv.at[0, 0])
    landed(zq.at[1], sf.at[0])
    landed(za.at[0], sf.at[1])
    landed(zd.at[0], sf.at[2])
    for d in (1, 2, 3):
        landed(rq.at[0], s1.at[0, d])
        landed(ox.at[0], s1.at[1, d])
        landed(fq.at[0, 0], s2.at[d])
        landed(zq.at[0, 0], s3.at[d])
        landed(zq.at[0, 0], sz.at[0, d])
        landed(za.at[0, 0], sz.at[1, d])
        landed(ox.at[0], so.at[d])


def close(part, za, zd, gq, go, vec):
    V = pltpu.VMEM
    return remote_call(
        close_kernel,
        [
            ((4, ROWS, D), BF, "v"),
            ((2, 4, 80, D), BF, "v"),
            ((2, 4, 80, 640), BF, "v"),
            ((3, 4, 80, 512), BF, "v"),
            ((80, D), F32, "v"),
            ((8, D), F32, "v"),
        ],
        "aaaaav",
        [
            V((2, 4, 4, 80, 512), BF), V((4, 4, 80, 512), BF), V((2, 4, 80, 512), BF),
            V((4, 80, D), BF), V((4, 80, D), BF), V((4, 80, D), BF), V((4, 80, D), BF), V((8, D), F32), V((10, 8, D), F32),
            dma(2, 2), dma(4), dma(2), dma(2), dma(4),
            dma(2, 4), dma(2, 4), dma(4), dma(4), dma(4), dma(4), dma(2, 4), dma(2, 4), dma(3), dma(3),
            dma(4), dma(4), dma(4, 4), dma(4, 4),
        ],
        4,
        "close",
    )(part, za, zd, gq, go, vec)


def finish_kernel(res, d_st, pbuf, za, zd, zq, out, vec, result, g_in, o_q, o_k, o_v, o_out, o_up, o_gate, o_down, o_vec):
    _, _, z, y = here()
    result[...] = res[...]
    g_in[...] = d_st[...] + total_of(pbuf)
    o_out[...] = out[...]
    for k in range(4):
        cols = slice(k * D, (k + 1) * D)
        o_up[:, cols] = za[0, k].astype(F32)
        o_gate[:, cols] = za[1, k].astype(F32)
        for h in range(2):
            o_down[k * 80 : (k + 1) * 80, h * 640 : (h + 1) * 640] = zd[h, k].astype(F32)
        a, b = zq[1, k].astype(F32), zq[2, k].astype(F32)
        at = k * GROUP
        pairs = [a[:, h * 128 : (h + 1) * 128] for h in range(4)] + [b[:, :128]]
        o_q[:, at : at + GROUP] = jnp.concatenate([v[:, :HDIM] for v in pairs], axis=1)
        o_k[:, at : at + GROUP] = jnp.concatenate([v[:, HDIM:] for v in pairs], axis=1)
        o_v[:, at : at + GROUP] = b[:, 128:448]
    v = vec[...]
    o_vec[0:2] = pltpu.roll(v, (16 - (z * 4 + y)) % 16 * 80, 1)[0:2]
    o_vec[2:4] = pltpu.roll(v, (4 - y) % 4 * 320, 1)[2:4]
    o_vec[4:] = pltpu.roll(v, (16 - y) % 16 * 80, 1)[4:]


def finish(res, d_st, pbuf, za, zd, zq, out, vec):
    return local_call(
        finish_kernel,
        [
            ((ROWS, D), BF),
            ((ROWS, D), F32),
            ((80, D), F32),
            ((80, D), F32),
            ((80, D), F32),
            ((80, D), F32),
            ((80, FF), F32),
            ((80, FF), F32),
            ((320, D), F32),
            ((8, D), F32),
        ],
        8,
        [],
        "finish",
    )(res, d_st, pbuf, za, zd, zq, out, vec)


def shards(
    states, w_query, w_key, w_value, w_out, w_up, w_gate, w_down,
    scale_qk, alpha_attn, alpha_mlp, scale_up, scale_gate, lengths, cotangent,
):
    x, c, z, y = here()
    st = states[0]

    def heads(w):
        return w.reshape(80, 4, HG, HDIM)

    q4, k4, v4 = heads(w_query), heads(w_key), heads(w_value)
    qk = jnp.stack([q4, k4], axis=3).reshape(80, 4, HG * 128)
    half1 = jnp.concatenate([qk[:, :, 512:], v4.reshape(80, 4, GROUP), jnp.zeros((80, 4, HDIM), BF)], axis=2)
    wq = jnp.stack([qk[:, :, :512], half1]).transpose(0, 2, 1, 3)
    vec = jnp.concatenate([scale_qk, alpha_attn, alpha_mlp, scale_up, scale_gate, jnp.zeros((16,), BF)])
    vec = jnp.broadcast_to(vec.astype(F32)[None], (8, 896))
    inner, outer = (jnp.asarray(t) for t in rope_tables())
    n = BLOCKS * ROWS
    part, att, lse, kv, q, turned, xg, wqkv, wo, scale, rate_a, rate_m, su, sg, wu, wd, gy = front(
        lengths, st, wq, vec, w_out, w_up, w_gate, w_down, inner, outer
    )
    result, d_st, dm, ha, hd, vec = middle(
        lengths, part, st, cotangent[0], rate_a, rate_m, su, sg, wu.reshape(D, D), wd.reshape(D, D), gy
    )
    dq, dkv, go, za, zd = attend_back(
        lengths, q, kv, wo.reshape(GROUP, D), dm.reshape(n, D), att, lse, ha, hd
    )
    part, gq, g_sq = qkv_back(
        dq, dkv.reshape(HG, n, 128), turned, scale, inner, outer, xg.reshape(n, D), wqkv.reshape(2, D, 512)
    )
    vec = jnp.concatenate([vec[:4], g_sq[0:1], vec[5:]])
    pbuf, za, zd, zq, out, vec = close(
        part.reshape(2, 2, ROWS, D), za, zd, gq.reshape(2, 4, 4, 80, 512), go.reshape(4, 80, D), vec
    )
    result, g_in, o_q, o_k, o_v, o_out, o_up, o_gate, o_down, o_vec = finish(
        result, d_st, pbuf, za, zd, zq, out, vec
    )
    return (
        result[None],
        g_in[None],
        o_q,
        o_k,
        o_v,
        o_out,
        o_up,
        o_gate,
        o_down,
        o_vec[4, :80],
        o_vec[0, :80],
        o_vec[1, :80],
        o_vec[2, :320],
        o_vec[3, :320],
    )


def solution(mesh):
    row = P("grp", ("seq", "shard"), None)
    mat = P("shard", None)
    one = P("shard")
    return jax.shard_map(
        shards,
        mesh=mesh,
        in_specs=(row,) + (mat,) * 7 + (one,) * 5 + (P("grp"), row),
        out_specs=(row, row) + (mat,) * 7 + (one,) * 5,
        check_vma=False,
    )
```

time: 410 us -> 360 us (0.88)
  Pallas kernels: 382 us -> 346 us
  local copies, waits for them, and re-layouts: 23.9 us -> 10.7 us
    pallas_call x6 -> x5, Pallas kernels: 265 us -> 236 us  [the longest x1 92.2 us: front(): remote_call(front_kernel, [((2, 2, ROWS, D), BF, 'v'), ((HG, n, HDIM), F3...]
    unnamed x42 -> x8, local copies, waits for them, and re-layouts: 13.6 us -> 1.69 us
    pallas_call x1, Pallas kernels: 117 us -> 110 us  [middle(): remote_call(mid_kernel, [((ROWS, D), BF, 'v'), ((ROWS, D), F32, 'v'), ((2...]
    broadcast_in_dim x11 -> x1, local copies, waits for them, and re-layouts: 4.21 us -> 0.01 us  [shards(): jnp.zeros((80, 4, HDIM), BF)]
where the time goes in v3:
time: 360 us
  Pallas kernels  346 us (96%)
  local copies, waits for them, and re-layouts  10.7 us (3%)
    pallas_call x1, Pallas kernels, middle(): remote_call(mid_kernel, [((ROWS, D), BF, 'v'), ((ROWS, D), F32, 'v'), ((2...  110 us
    pallas_call x1, Pallas kernels, front(): remote_call(front_kernel, [((2, 2, ROWS, D), BF, 'v'), ((HG, n, HDIM), F3...  92.2 us
    pallas_call x1, Pallas kernels, attend_back(): remote_call(attend_back_kernel, [((HG, n, 128), F32, 'v'), ((HG, 2, 2, RO...  73.9 us
    pallas_call x1, Pallas kernels, close(): remote_call(close_kernel, [((4, ROWS, D), BF, 'v'), ((2, 4, 80, D), BF, '...  49.7 us
    pallas_call x1, Pallas kernels, qkv_back(): local_call(qkv_back_kernel, [((n, D), BF), ((2, D, 512), BF), ((8, D), F3...  13.4 us

profile of v3, /device:TPU:1, one launch (start us, length us, event | category | flops | bytes accessed | tf_op | source)
XLA Modules:
  0.0 359.7 jit_solution(7211422481569095276)
XLA Ops:
  0.6 0.0 copy-start
  1.4 0.1 pad.7.clone
  1.4 3.5 concatenate.17
  4.9 0.6 broadcast_in_dim.16.vec
  5.5 1.2 reshape_reshape.3
  6.8 1.1 copy.33
  7.9 0.0 copy-done
  7.9 0.2 copy.34
  8.2 0.1 pad_maximum_fusion
  8.4 0.2 copy.39
  8.6 0.1 copy.40
  8.8 0.1 maximum_bitcast_fusion.1
  8.8 0.9 maximum_bitcast_fusion.wq
  9.7 92.2 %front.1 = (bf16[2,2,128,1280]{3,2,1,0:T(8,128)(2,1)}, f32[5,512,64]{2,1,0:T(8,128)}, f32[5,4,128]{2,1,0:T(4,128)}, bf16[5,2,2,2,4,128,128]{6,5,4,3,2,1,0:T(8,12...) custom-call(s32[1]{0:T(128)S(6)} %copy.41.length, ...), custom_call_target="tpu_custom_call" | custom-call | tf_op jit(solution)/shard_map/front/pallas_call | solution.py:518
  102.0 110.2 %middle.1 = (bf16[128,1280]{1,0:T(8,128)(2,1)}, f32[128,1280]{1,0:T(8,128)}, bf16[2,2,128,1280]{3,2,1,0:T(8,128)(2,1)}, bf16[4,4,80,1280]{3,2,1,0:T(8,128)(2,1)}...) custom-call(s32[1]{0:T(128)S(6)} %copy.41.length, bf16[2,2,128,1280]{3,2,1,0:T(8,128)(2,1)} %get-tuple-element.61.part0, ...), custom_call_target="tpu_custom_call" | custom-call | tf_op jit(solution)/shard_map/middle/pallas_call | solution.py:955
  212.2 73.9 %attend_back.1 = (f32[5,512,128]{2,1,0:T(8,128)}, bf16[5,2,2,128,128]{4,3,2,1,0:T(8,128)(2,1)}, bf16[320,1280]{1,0:T(8,128)(2,1)}, bf16[4,80,1280]{2,1,0:T(8,128)(2,1)}, bf16[4,80,640]{2,1,0:T(8,128)(2,1)}) custom-call(s32[1]{0:T(128)S(6)} %copy.41.length, bf16[5,512,128]{2,1,0:T(8,128)(2,1)} %get-tuple-element.71.q, ...), custom_call_target="tpu_custom_call" | custom-call | tf_op jit(solution)/shard_map/attend_back/pallas_call | solution.py:714
  286.1 0.0 copy-start.1
  286.1 13.4 %qkv_back.1 = (bf16[512,1280]{1,0:T(8,128)(2,1)}, bf16[2,1280,512]{2,1,0:T(8,128)(2,1)}, f32[8,1280]{1,0:T(8,128)}) custom-call(f32[5,512,128]{2,1,0:T(8,128)} %get-tuple-element.79.dq, bf16[5,512,128]{2,1,0:T(8,128)(2,1)} %bitcast.44, f32[5,512,128]{2,1,0:T(8,128)} %get-tuple-element.81.t, f32[8,640]{1,0:T(8,128)} %get-tuple-element.82.scale, ...), custom_call_target="tpu_custom_call" | custom-call | tf_op jit(solution)/shard_map/qkv_back/pallas_call | solution.py:1025
  299.5 0.8 slice.33
  300.3 0.0 copy-done.1
  300.4 0.6 pad_maximum_fusion.1.vec
  301.0 49.7 %close.1 = (bf16[4,128,1280]{2,1,0:T(8,128)(2,1)}, bf16[2,4,80,1280]{3,2,1,0:T(8,128)(2,1)}, bf16[2,4,80,640]{3,2,1,0:T(8,128)(2,1)}, bf16[3,4,80,512]{3,2,1,0:T...) custom-call(bf16[2,2,128,1280]{3,2,1,0:T(8,128)(2,1)} %bitcast.40, bf16[4,80,1280]{2,1,0:T(8,128)(2,1)} %get-tuple-element.86.za_in, ...), custom_call_target="tpu_custom_call" | custom-call | tf_op jit(solution)/shard_map/close/pallas_call | solution.py:1163
  350.7 6.3 %finish.1 = (bf16[128,1280]{1,0:T(8,128)(2,1)}, f32[128,1280]{1,0:T(8,128)}, f32[80,1280]{1,0:T(8,128)}, f32[80,1280]{1,0:T(8,128)}, f32[80,1280]{1,0:T(8,128)},...) custom-call(bf16[128,1280]{1,0:T(8,128)(2,1)} %get-tuple-element.69., ...), custom_call_target="tpu_custom_call" | custom-call | tf_op jit(solution)/shard_map/finish/pallas_call | solution.py:1210
  357.0 1.3 slice_bitcast_fusion
  358.3 1.4 slice_reduce_fusion
  (8 shorter events, 0.1 us)
Async XLA Ops:
  0.6 7.3 %copy-start = (bf16[80,1280]{1,0:T(8,128)(2,1)S(1)}, bf16[80,1280]{1,0:T(8,128)(2,1)}, u32[]{:S(2)}) copy-start(bf16[80,1280]{1,0:T(8,128)(2,1)} %param.19) | copy-start | bytes 614404
  286.1 14.2 %copy-start.1 = (f32[8,1280]{1,0:T(8,128)S(1)}, f32[8,1280]{1,0:T(8,128)}, u32[]{:S(2)}) copy-start(f32[8,1280]{1,0:T(8,128)} %get-tuple-element.90) | copy-start | bytes 122884

commit v4 on v3

v4 whole, which is shorter than its diff:
```python
import functools
import math

import jax
import jax.numpy as jnp
import numpy as np
from jax import lax
from jax.experimental import pallas as pl
from jax.experimental.pallas import tpu as pltpu
from jax.sharding import PartitionSpec as P


D, HEADS, HDIM, FF = 1280, 20, 64, 5120
ROWS, BLOCKS, HG = 128, 4, 5
GROUP = HG * HDIM
EPS = 1e-6
BF, F32 = jnp.bfloat16, jnp.float32
MESH = pl.DeviceIdType.MESH
VMEM_LIMIT = 60 << 20


def here():
    s = lax.axis_index("shard")
    return lax.axis_index("grp"), lax.axis_index("seq"), s // 4, s % 4


def dev(x, c, z, y):
    return (x, c, z * 4 + y)


def worker(z):
    return ((z + 1) // 2) % 2


def owner_z(w, i):
    return i * (3 - 2 * w) + w


def step(v, d):
    return (v + d) % 4


def rcopy(src, dst, ss, rs, to):
    return pltpu.make_async_remote_copy(
        src_ref=src, dst_ref=dst, send_sem=ss, recv_sem=rs, device_id=to, device_id_type=MESH
    )


def lcopy(src, dst, sem):
    return pltpu.make_async_copy(src, dst, sem)


def landed(dst, sem):
    pltpu.make_async_copy(dst, dst, sem).wait()


def greet(peers):
    bar = pltpu.get_barrier_semaphore()
    for p in peers:
        pl.semaphore_signal(bar, inc=1, device_id=p, device_id_type=MESH)
    pl.semaphore_wait(bar, len(peers))


def z_peers(x, c, z, y):
    far = [dev(x, cc, step(z, d), y) for d in (1, 2, 3) for cc in (0, 1)]
    return [dev(x, 1 - c, z, y)] + far


def z_gather_start(src, dst, ss, rs, x, c, z, y):
    w = worker(z)
    slot = (z // 2, c)
    for d in (1, 3, 2):
        rcopy(src, dst.at[slot], ss.at[d], rs.at[slot], dev(x, w, step(z, d), y)).start()

    @pl.when(c == w)
    def _():
        lcopy(src, dst.at[slot], rs.at[slot]).start()

    @pl.when(c != w)
    def _():
        rcopy(src, dst.at[slot], ss.at[0], rs.at[slot], dev(x, w, z, y)).start()


def z_gather_take(dst, rs, p):
    for k in range(2):
        landed(dst.at[p, k], rs.at[p, k])


def z_gather_sent(src, ss, c, z):
    for d in (1, 2, 3):
        landed(src, ss.at[d])

    @pl.when(c != worker(z))
    def _():
        landed(src, ss.at[0])


def z_gather_wait(src, dst, ss, rs, c, z):
    for p in range(2):
        z_gather_take(dst, rs, p)
    z_gather_sent(src, ss, c, z)


def z_scatter_pair(part, dst, ss, rs, p, x, c, z, y):
    oz = owner_z(c, p)
    for oc in range(2):
        mine = jnp.logical_and(c == oc, z == oz)

        @pl.when(mine)
        def _(oc=oc):
            lcopy(part.at[p, oc], dst.at[z], rs.at[z]).start()

        @pl.when(jnp.logical_not(mine))
        def _(oc=oc):
            rcopy(part.at[p, oc], dst.at[z], ss.at[p, oc], rs.at[z], dev(x, oc, oz, y)).start()


def z_scatter_start(part, dst, ss, rs, x, c, z, y):
    for p in range(2):
        z_scatter_pair(part, dst, ss, rs, p, x, c, z, y)


def z_scatter_take(dst, rs):
    for k in range(4):
        landed(dst.at[k], rs.at[k])


def z_scatter_sent(part, ss, c, z):
    for p in range(2):
        for oc in range(2):
            mine = jnp.logical_and(c == oc, z == owner_z(c, p))

            @pl.when(jnp.logical_not(mine))
            def _(p=p, oc=oc):
                landed(part.at[p, oc], ss.at[p, oc])


def remote_call(kernel, outs, ins_spaces, scratch, cid, name):
    spec = {
        "a": pl.BlockSpec(memory_space=pl.ANY),
        "v": pl.BlockSpec(memory_space=pltpu.VMEM),
        "s": pl.BlockSpec(memory_space=pltpu.SMEM),
    }
    return pl.pallas_call(
        kernel,
        out_shape=[jax.ShapeDtypeStruct(s, d) for s, d, _ in outs],
        in_specs=[spec[s] for s in ins_spaces],
        out_specs=[spec[s] for _, _, s in outs],
        scratch_shapes=scratch,
        compiler_params=pltpu.CompilerParams(
            collective_id=cid, has_side_effects=True, vmem_limit_bytes=VMEM_LIMIT
        ),
        name=name,
    )


def local_call(kernel, outs, n_in, scratch, name, smem=0):
    vmem = pl.BlockSpec(memory_space=pltpu.VMEM)
    sm = pl.BlockSpec(memory_space=pltpu.SMEM)
    return pl.pallas_call(
        kernel,
        out_shape=[jax.ShapeDtypeStruct(s, d) for s, d in outs],
        in_specs=[sm] * smem + [vmem] * n_in,
        out_specs=[vmem for _ in outs],
        scratch_shapes=scratch,
        compiler_params=pltpu.CompilerParams(vmem_limit_bytes=VMEM_LIMIT),
        name=name,
    )


def dma(*shape):
    return pltpu.SemaphoreType.DMA(shape)


def rope_tables():
    freqs = np.exp(np.arange(32) * (-2.0 * math.log(10000.0) / 64))
    freqs = np.tile(freqs, 4)
    sign = np.tile(np.concatenate([-np.ones(32), np.ones(32)]), 2)
    inner = np.arange(ROWS)[:, None] * freqs
    outer = (np.arange(32) * ROWS)[:, None] * freqs
    return (
        np.stack([np.cos(inner), np.sin(inner) * sign]).astype(np.float32),
        np.stack([np.cos(outer), np.sin(outer) * sign]).astype(np.float32),
    )


def block_index(c, y, j):
    return (j % 2) * 16 + owner_z(c, j // 2) * 4 + y


def turn_of(inner, outer, b):
    oc = outer[0, pl.ds(b, 1), :]
    os = outer[1, pl.ds(b, 1), :]
    return oc * inner[0] - os * inner[1], os * inner[0] + oc * inner[1]


def lanes():
    return lax.broadcasted_iota(jnp.int32, (ROWS, 128), 1)


def swap(v, lane):
    return jnp.where(lane % 64 < 32, pltpu.roll(v, 96, 1), pltpu.roll(v, 32, 1))


def half_means(v, lane):
    low = jnp.sum(jnp.where(lane < 64, v, 0.0), axis=-1, keepdims=True)
    high = jnp.sum(jnp.where(lane < 64, 0.0, v), axis=-1, keepdims=True)
    return jnp.where(lane < 64, low, high) * (1.0 / 64)


TILE = 512
STEP = 6


def tiles_of(c, j):
    return (j % 2) * 4 + owner_z(c, j // 2) + 1


def nt(a, b):
    return lax.dot_general(a, b, (((1,), (1,)), ((), ())), preferred_element_type=F32)


def tn(a, b):
    return lax.dot_general(a, b, (((0,), (0,)), ((), ())), preferred_element_type=F32)


def key_tile(ref, h, t):
    zz = t % 4
    return ref[h, worker(zz), zz // 2, t // 4].reshape(TILE, 128)


def work_items(c, y, length):
    n = [tiles_of(c, j) for j in range(BLOCKS)]
    starts = [n[0], n[0] + n[1], n[0] + n[1] + n[2]]
    query = lax.broadcasted_iota(jnp.int32, (1, ROWS), 1)

    def item(i):
        hits = [(i >= s).astype(jnp.int32) for s in starts]
        j = hits[0] + hits[1] + hits[2]
        t = i - hits[0] * n[0] - hits[1] * n[1] - hits[2] * n[2]
        last = query + y * ROWS + (tiles_of(c, j) - 1 - t) * TILE
        return j, t, jnp.minimum(last, length - 1 - t * TILE)

    return item


def columns(ref, k, half):
    return ref.at[:, pl.ds(pl.multiple_of(k * D + half * 640, 128), 640)]


def front_kernel(
    length, st, wq, vec, w_out, w_up, w_gate, w_down, inner, outer,
    part, att, lse, kv_o, q_o, t_o, xg_o, wqkv_o, wo_o, scale_o, rate_a, rate_m, su, sg, uq, wd, gz,
    xg, wqkv, vecs, wo, y0, y1, kv, kvb, q, tt, low, acc, tot, uz,
    xs, xr, w1s, w1r, w2s, w2r, w3s, w3r, vs, vr, os, orr, lo,
    f1s, f1r, f2s, f2r, f3s, f3r, f4s, f4r, fl, sy, ry, sf, rf, ss, rs, kl, ol,
):
    x, c, z, y = here()
    sib = dev(x, 1 - c, z, y)
    half = pl.ds(pl.multiple_of(c * 640, 128), 640)
    other = pl.ds(pl.multiple_of((1 - c) * 640, 128), 640)
    to_z = [None] + [dev(x, c, step(z, d), y) for d in (1, 2, 3)]
    to_y = [None] + [dev(x, c, z, step(y, d)) for d in (1, 2, 3)]
    to_x = [None] + [dev(step(x, d), c, z, y) for d in (1, 2, 3)]
    near_first = (1, 3, 2)
    greet(z_peers(x, c, z, y) + to_y[1:] + to_x[1:])

    for d in near_first:
        rcopy(wq.at[c, step(z, d)], wqkv.at[c, z, y], w1s.at[d], w1r.at[z], to_z[d]).start()
        rcopy(vec, vecs.at[z, y], vs.at[0, d], vr.at[0, z], to_z[d]).start()
    lcopy(wq.at[c, z], wqkv.at[c, z, y], lo.at[0]).start()
    lcopy(vec, vecs.at[z, y], lo.at[1]).start()
    for d in near_first:
        rcopy(w_out.at[:, half], wo.at[y, :, half], os.at[0, d], orr.at[0, y], to_y[d]).start()
    rcopy(w_out.at[:, half], wo.at[y, :, half], os.at[0, 0], orr.at[1, y], sib).start()
    lcopy(w_out.at[:, half], wo.at[y, :, half], lo.at[2]).start()

    for d in (1, 2, 3):
        landed(wqkv.at[c, step(z, d), y], w1r.at[step(z, d)])
        landed(vecs.at[step(z, d), y], vr.at[0, step(z, d)])
    landed(wqkv.at[c, z, y], lo.at[0])
    landed(vecs.at[z, y], lo.at[1])
    mine = wqkv.at[c, :, y]
    rcopy(mine, mine, w2s.at[0], w2r.at[0], to_y[1]).start()
    rcopy(mine, mine, w2s.at[1], w2r.at[1], to_y[3]).start()
    rcopy(mine, mine, w3s.at[0], w3r.at[0], sib).start()
    for d in near_first:
        rcopy(vecs.at[:, y], vecs.at[:, y], vs.at[1, d], vr.at[1, y], to_y[d]).start()
    z_gather_start(st, xg, xs, xr, x, c, z, y)
    for k, src, to in ((0, step(y, 3), to_y[1]), (1, step(y, 1), to_y[3])):
        block, piece = wqkv.at[c, :, src], wqkv.at[c, 2 * k : 2 * k + 2, src]
        landed(block, w2r.at[k])
        rcopy(piece, piece, w2s.at[2 + k], w2r.at[2 + k], to).start()
        rcopy(block, block, w3s.at[1 + k], w3r.at[1 + k], sib).start()
    for k in range(2):
        piece = wqkv.at[c, 2 * k : 2 * k + 2, step(y, 2)]
        landed(piece, w2r.at[2 + k])
        rcopy(piece, piece, w3s.at[3 + k], w3r.at[3 + k], sib).start()
    down = w_down.at[pl.ds(pl.multiple_of(x * 80, 16), 80), half]
    for d in near_first:
        rcopy(down, wd.at[y, x, :, half], f2s.at[1, d], f2r.at[1, y], to_y[d]).start()
    lcopy(down, wd.at[y, x, :, half], fl.at[2]).start()
    for d in (1, 2, 3):
        landed(vecs.at[:, step(y, d)], vr.at[1, step(y, d)])
    for zz in range(4):
        for yy in range(4):
            at = (zz * 4 + yy) * 80
            rate_a[:, at : at + 80] = vecs[zz, yy, :, 80:160]
            rate_m[:, at : at + 80] = vecs[zz, yy, :, 160:240]
    for yy in range(4):
        su[:, yy * 320 : (yy + 1) * 320] = vecs[z, yy, :, 240:560]
        sg[:, yy * 320 : (yy + 1) * 320] = vecs[z, yy, :, 560:880]
    scale = jnp.concatenate([vecs[z, yy, :, :80] for yy in range(4)], axis=1)
    for h in range(HG):
        sh = scale[:, h * HDIM : (h + 1) * HDIM]
        scale_o[:, h * 128 : (h + 1) * 128] = jnp.concatenate([sh, sh], axis=1)

    for p in range(2):
        z_gather_take(xg, xr, p)
    for d in near_first:
        rcopy(columns(w_gate, step(z, d), c), gz.at[z], f1s.at[1, d], f1r.at[1 + z], to_z[d]).start()
    lcopy(columns(w_gate, z, c), gz.at[z], fl.at[0]).start()

    @pl.when(z == x)
    def _():
        for d in near_first:
            rcopy(columns(w_up, step(z, d), c), uz, f1s.at[0, d], f1r.at[0], to_z[d]).start()
        lcopy(columns(w_up, z, c), uz, f1r.at[0]).start()

    for k, src in ((0, y), (1, step(y, 3)), (2, step(y, 1))):
        landed(wqkv.at[1 - c, :, src], w3r.at[k])
    for k in range(2):
        landed(wqkv.at[1 - c, 2 * k : 2 * k + 2, step(y, 2)], w3r.at[3 + k])
    lcopy(xg, xg_o, ol.at[0]).start()
    lcopy(wqkv, wqkv_o, ol.at[1]).start()

    def project(p, carry):
        rows = xg[p].reshape(2 * ROWS, D)
        y0[p] = jnp.dot(rows, wqkv[0].reshape(D, 512), preferred_element_type=F32)
        y1[p] = jnp.dot(rows, wqkv[1].reshape(D, 512), preferred_element_type=F32)
        return carry

    lax.fori_loop(0, 2, project, 0)
    lane = lanes()

    def send(h):
        rcopy(kv.at[h], kvb.at[h, c, :, :, y], sy.at[h, 0], ry.at[h, 0], to_y[1]).start()
        rcopy(kv.at[h], kvb.at[h, c, :, :, y], sy.at[h, 1], ry.at[h, 1], to_y[3]).start()
        rcopy(kv.at[h], kvb.at[h, c, :, :, y], ss.at[h, 0], rs.at[h, 0], sib).start()
        lcopy(kv.at[h], kvb.at[h, c, :, :, y], kl.at[h]).start()

    for h in range(HG):

        def per_block(j, carry, h=h):
            p, r = j // 2, pl.ds(pl.multiple_of((j % 2) * ROWS, ROWS), ROWS)
            cosine, sine = turn_of(inner, outer, block_index(c, y, j))
            raw = y0[p, r, h * 128 : (h + 1) * 128] if h < 4 else y1[p, r, 0:128]
            t = raw * cosine + swap(raw, lane) * sine
            unit = t * lax.rsqrt(half_means(t * t, lane) + EPS)
            both = unit * scale_o[0:1, h * 128 : (h + 1) * 128]
            pair = y1[p, r, 128 + (h // 2) * 128 : 256 + (h // 2) * 128]
            v = pair if h % 2 else pltpu.roll(pair, 64, 1)
            kv[h, p, j % 2] = jnp.where(lane < 64, pltpu.roll(both, 64, 1), v).astype(BF)
            rows = pl.ds(pl.multiple_of(j * ROWS, ROWS), ROWS)
            tt[h, rows, :] = t
            q[h, rows, :] = (jnp.where(lane < 64, both, 0.0).astype(BF).astype(F32) * 0.125).astype(BF)
            return carry

        lax.fori_loop(0, BLOCKS, per_block, 0)
        send(h)
    landed(wd.at[y, x, :, half], fl.at[2])
    for d in (1, 2, 3):
        landed(wd.at[step(y, d), x, :, half], f2r.at[1, step(y, d)])
    for d in near_first:
        rcopy(wd.at[:, x, :, half], wd.at[:, x, :, half], f3s.at[d], f3r.at[x], to_x[d]).start()
    rcopy(wd.at[:, x, :, half], wd.at[:, x, :, half], f4s.at[0], f4r.at[x], sib).start()
    lcopy(q, q_o, ol.at[2]).start()
    lcopy(tt, t_o, ol.at[3]).start()

    def near(h):
        for k, src, to in ((0, step(y, 3), to_y[1]), (1, step(y, 1), to_y[3])):
            landed(kvb.at[h, c, :, :, src], ry.at[h, k])
            rcopy(kvb.at[h, c, k, :, src], kvb.at[h, c, k, :, src], sf.at[h, k], rf.at[h, k], to).start()
            rcopy(kvb.at[h, c, :, :, src], kvb.at[h, c, :, :, src], ss.at[h, 1 + k], rs.at[h, 1 + k], sib).start()

    def far(h):
        src = step(y, 2)
        for k in range(2):
            landed(kvb.at[h, c, k, :, src], rf.at[h, k])
            rcopy(kvb.at[h, c, k, :, src], kvb.at[h, c, k, :, src], ss.at[h, 3 + k], rs.at[h, 3 + k], sib).start()

    def ready(h):
        landed(kvb.at[h, c, :, :, y], kl.at[h])
        landed(kvb.at[h, 1 - c, :, :, y], rs.at[h, 0])
        landed(kvb.at[h, 1 - c, :, :, step(y, 3)], rs.at[h, 1])
        landed(kvb.at[h, 1 - c, :, :, step(y, 1)], rs.at[h, 2])
        for k in range(2):
            landed(kvb.at[h, 1 - c, k, :, step(y, 2)], rs.at[h, 3 + k])
        lcopy(kvb.at[h], kv_o.at[h], kl.at[h]).start()

    item = work_items(c, y, length[0])

    def compute(h):
        acc[...] = jnp.zeros_like(acc)
        tot[...] = jnp.zeros_like(tot)

        def body(g, carry):
            key = lax.broadcasted_iota(jnp.int32, (TILE, ROWS), 0)
            its = [item(g * STEP + u) for u in range(STEP)]
            ks = [key_tile(kvb, h, t) for _, t, _ in its]
            ss_ = [
                nt(k, q[h, pl.ds(pl.multiple_of(j * ROWS, ROWS), ROWS), :]) for k, (j, _, _) in zip(ks, its)
            ]
            ps = [jnp.where(key <= bound, jnp.exp(s), 0.0) for s, (_, _, bound) in zip(ss_, its)]
            for k, p, (j, _, _) in zip(ks, ps, its):
                tot[j] += jnp.sum(p.reshape(TILE // 8, 8, ROWS), axis=0)
                acc[j] += tn(k, p.astype(BF))
            return carry

        lax.fori_loop(0, 18 // STEP, body, 0)
        for j in range(BLOCKS):
            total = jnp.sum(tot[j], axis=0, keepdims=True)
            lse[h, j : j + 1, :] = jnp.log(total)
            att[h, j * ROWS : (j + 1) * ROWS, :] = (acc[j, HDIM:] / total).T

    def spread_up():
        landed(uz, f1r.at[0])
        for d in near_first:
            rcopy(uz, uq.at[y], f2s.at[0, d], f2r.at[0, y], to_y[d]).start()
        lcopy(uz, uq.at[y], fl.at[1]).start()

    near(0)

    def per_head(i, carry):
        @pl.when(i + 1 < HG)
        def _():
            near(i + 1)

        @pl.when(i == HG)
        def _():
            spread_up()

        @pl.when(i > 0)
        def _():
            ready(i - 1)
            compute(i - 1)

        @pl.when(i < HG)
        def _():
            far(i)

        return carry

    lax.fori_loop(0, HG + 1, per_head, 0)
    for h in range(HG):
        low[:, h * HDIM : (h + 1) * HDIM] = att[h].astype(BF)
    for d in near_first:
        y2 = step(y, d)
        landed(wo.at[y2, :, half], orr.at[0, y2])
        rcopy(wo.at[y2, :, half], wo.at[y2, :, half], os.at[1, d], orr.at[1, y2], sib).start()
    landed(wo.at[y, :, half], lo.at[2])
    for k in range(4):
        landed(wo.at[k, :, other], orr.at[1, k])
    lcopy(wo, wo_o, ol.at[4]).start()
    for p in range(2):
        v = jnp.dot(low[p * 256 : (p + 1) * 256, :], wo[...].reshape(GROUP, D), preferred_element_type=F32)
        part[p] = v.astype(BF).reshape(2, ROWS, D)

    for d in near_first:
        x2 = step(x, d)
        landed(wd.at[:, x2, :, half], f3r.at[x2])
        rcopy(wd.at[:, x2, :, half], wd.at[:, x2, :, half], f4s.at[d], f4r.at[x2], sib).start()
    landed(uz, fl.at[1])
    landed(uz, fl.at[0])
    for d in (1, 2, 3):
        landed(uq.at[step(y, d)], f2r.at[0, step(y, d)])
        landed(gz.at[step(z, d)], f1r.at[1 + step(z, d)])

    def sent(h, carry):
        for k in range(2):
            landed(kv.at[h], sy.at[h, k])
            landed(kv.at[h, 0], sf.at[h, k])
            landed(kv.at[h, 0], ss.at[h, 3 + k])
        for k in range(3):
            landed(kv.at[h], ss.at[h, k])
        landed(kvb.at[h], kl.at[h])
        return carry

    lax.fori_loop(0, HG, sent, 0)
    z_gather_sent(st, xs, c, z)
    for k in range(4):
        landed(wd.at[:, k, :, other], f4r.at[k])
        landed(wd.at[:, k, :, half], f4s.at[k])
    landed(wo.at[0, :, half], os.at[0, 0])
    for k in range(2):
        landed(mine, w2s.at[k])
        landed(wqkv.at[c, 0:2, y], w2s.at[2 + k])
        landed(wqkv.at[c, 0:2, y], w3s.at[3 + k])
    for k in range(3):
        landed(mine, w3s.at[k])
    for d in (1, 2, 3):
        landed(wqkv.at[c, z, y], w1s.at[d])
        landed(vec, vs.at[0, d])
        landed(vecs.at[:, y], vs.at[1, d])
        landed(wo.at[0, :, half], os.at[0, d])
        landed(wo.at[0, :, half], os.at[1, d])
        landed(uz, f1s.at[1, d])
        landed(uz, f2s.at[0, d])
        landed(uz, f2s.at[1, d])
        landed(wd.at[:, x, :, half], f3s.at[d])

    @pl.when(z == x)
    def _():
        for d in (1, 2, 3):
            landed(uz, f1s.at[0, d])

    landed(xg, ol.at[0])
    landed(wqkv, ol.at[1])
    landed(q, ol.at[2])
    landed(tt, ol.at[3])
    landed(wo, ol.at[4])


def front(length, st, wq, vec, w_out, w_up, w_gate, w_down, inner, outer):
    n = BLOCKS * ROWS
    V = pltpu.VMEM
    return remote_call(
        front_kernel,
        [
            ((2, 2, ROWS, D), BF, "v"),
            ((HG, n, HDIM), F32, "v"),
            ((HG, BLOCKS, 128), F32, "v"),
            ((HG, 2, 2, 2, 4, ROWS, 128), BF, "a"),
            ((HG, n, 128), BF, "a"),
            ((HG, n, 128), F32, "a"),
            ((2, 2, ROWS, D), BF, "a"),
            ((2, 4, 4, 80, 512), BF, "a"),
            ((4, 80, D), BF, "a"),
            ((8, HG * 128), F32, "v"),
            ((8, D), F32, "v"),
            ((8, D), F32, "v"),
            ((8, D), F32, "v"),
            ((8, D), F32, "v"),
            ((4, 80, 640), BF, "a"),
            ((4, 4, 80, D), BF, "a"),
            ((4, 80, 640), BF, "a"),
        ],
        "saavaaaavv",
        [
            V((2, 2, ROWS, D), BF), V((2, 4, 4, 80, 512), BF), V((4, 4, 8, 896), F32), V((4, 80, D), BF),
            V((2, 256, 512), F32), V((2, 256, 512), F32),
            V((HG, 2, 2, ROWS, 128), BF), V((HG, 2, 2, 2, 4, ROWS, 128), BF), V((HG, n, 128), BF), V((HG, n, 128), F32),
            V((n, GROUP), BF), V((BLOCKS, 128, ROWS), F32), V((BLOCKS, 8, ROWS), F32), V((80, 640), BF),
            dma(4), dma(2, 2), dma(4), dma(4), dma(4), dma(4), dma(5), dma(5), dma(2, 4), dma(2, 4), dma(2, 4), dma(2, 4), dma(3),
            dma(2, 4), dma(5), dma(2, 4), dma(2, 4), dma(4), dma(4), dma(4), dma(4), dma(3),
            dma(HG, 2), dma(HG, 2), dma(HG, 2), dma(HG, 2), dma(HG, 5), dma(HG, 5), dma(HG), dma(5),
        ],
        0,
        "front",
    )(length, st, wq, vec, w_out, w_up, w_gate, w_down, inner, outer)


def inv_rms(v):
    return lax.rsqrt(jnp.mean(v * v, axis=-1, keepdims=True) + EPS)


def back_rms(dy, yy, inv):
    return (dy - yy * jnp.mean(dy * yy, axis=-1, keepdims=True)) * inv


def total_of(buf):
    return (buf[0].astype(F32) + buf[1].astype(F32)) + (buf[2].astype(F32) + buf[3].astype(F32))


def mix_of(res, part, rate):
    inv_p = inv_rms(part)
    unit = part * inv_p
    diff = unit - res
    u = res + rate * diff
    inv_u = inv_rms(u)
    return u * inv_u, unit, inv_p, inv_u, diff


def mix_back(dy, res, part, rate):
    yy, unit, inv_p, inv_u, diff = mix_of(res, part, rate)
    du = back_rms(dy, yy, inv_u)
    return du * (1.0 - rate), back_rms(du * rate, unit, inv_p), jnp.sum(du * diff, axis=0, keepdims=True)


HALF = ROWS // 2


def mid_kernel(
    length, part0, st, cot, rate_a, rate_m, su, sg, uq, wd_in, gz,
    result, d_st, dm, ha, hd, vec,
    buf, low, xg, dd, wu, wg, wd, up, gate, hid, dug, part, xt, ht, mixed, first, dfirst, ga, gd, ra, rd, rdy,
    ps, pr, gs, gr, s2, r2, s3, r3, sx, rx, sy, ry, lo,
):
    x, c, z, y = here()
    sib = dev(x, 1 - c, z, y)
    half = pl.ds(pl.multiple_of(c * 640, 128), 640)
    other = pl.ds(pl.multiple_of((1 - c) * 640, 128), 640)
    to_x = [None] + [dev(step(x, d), c, z, y) for d in (1, 2, 3)]
    to_y = [None] + [dev(x, c, z, step(y, d)) for d in (1, 2, 3)]

    def cut(k):
        return pl.ds(k * HALF, HALF)

    def scatter(n, src, k):
        for p in range(2):
            oz = owner_z(c, p)
            for oc in range(2):
                mine = jnp.logical_and(c == oc, z == oz)
                piece, to = src.at[p, oc, cut(k)], buf.at[n, z, cut(k)]

                @pl.when(mine)
                def _(piece=piece, to=to):
                    lcopy(piece, to, pr.at[n, k, z]).start()

                @pl.when(jnp.logical_not(mine))
                def _(piece=piece, to=to, p=p, oc=oc, oz=oz):
                    rcopy(piece, to, ps.at[n, k, p, oc], pr.at[n, k, z], dev(x, oc, oz, y)).start()

    def scatter_take(n, k):
        for i in range(4):
            landed(buf.at[n, i, cut(k)], pr.at[n, k, i])
        return total_of(buf.at[n, :, cut(k)])

    def scatter_sent(n, src):
        for k in range(2):
            for p in range(2):
                for oc in range(2):
                    mine = jnp.logical_and(c == oc, z == owner_z(c, p))

                    @pl.when(jnp.logical_not(mine))
                    def _(k=k, p=p, oc=oc):
                        landed(src.at[p, oc, cut(k)], ps.at[n, k, p, oc])

    def gather(n, dst, k):
        w = worker(z)
        piece, to, sem = low.at[n, cut(k)], dst.at[z // 2, c, cut(k)], gr.at[n, k, z // 2, c]
        for d in (1, 3, 2):
            rcopy(piece, to, gs.at[n, k, d], sem, dev(x, w, step(z, d), y)).start()

        @pl.when(c == w)
        def _():
            lcopy(piece, to, sem).start()

        @pl.when(c != w)
        def _():
            rcopy(piece, to, gs.at[n, k, 0], sem, dev(x, w, z, y)).start()

    def gather_take(n, dst, k):
        for p in range(2):
            for i in range(2):
                landed(dst.at[p, i, cut(k)], gr.at[n, k, p, i])

    def gather_sent(n):
        for k in range(2):
            for d in (1, 2, 3):
                landed(low.at[n, cut(k)], gs.at[n, k, d])

            @pl.when(c != worker(z))
            def _(k=k):
                landed(low.at[n, cut(k)], gs.at[n, k, 0])

    greet(z_peers(x, c, z, y) + to_x[1:] + to_y[1:])
    for k in range(2):
        scatter(0, part0, k)
    for d in (1, 3, 2):
        rcopy(uq, wu.at[x, :, :, half], s2.at[0, d], r2.at[0, x], to_x[d]).start()
        rcopy(gz, wg.at[:, y, :, half], s2.at[1, d], r2.at[1, y], to_y[d]).start()
    rcopy(uq, wu.at[x, :, :, half], s3.at[0, 0], r3.at[0, x], sib).start()
    rcopy(gz, wg.at[:, y, :, half], s3.at[1, 0], r3.at[1, y], sib).start()
    lcopy(uq, wu.at[x, :, :, half], lo.at[0]).start()
    lcopy(gz, wg.at[:, y, :, half], lo.at[1]).start()
    lcopy(wd_in, wd, lo.at[2]).start()
    vec[...] = jnp.zeros_like(vec)

    for k in range(2):
        total = scatter_take(0, k)
        out = mix_of(st[cut(k)].astype(F32), total, rate_a[0:1])[0]
        low[0, cut(k)] = out.astype(BF)
        gather(0, xg, k)
        mixed[cut(k)] = total
        first[cut(k)] = out

    for d in (1, 3, 2):
        x2, y2 = step(x, d), step(y, d)
        landed(wu.at[x2, :, :, half], r2.at[0, x2])
        rcopy(wu.at[x2, :, :, half], wu.at[x2, :, :, half], s3.at[0, d], r3.at[0, x2], sib).start()
        landed(wg.at[:, y2, :, half], r2.at[1, y2])
        rcopy(wg.at[:, y2, :, half], wg.at[:, y2, :, half], s3.at[1, d], r3.at[1, y2], sib).start()
    landed(wu.at[x, :, :, half], lo.at[0])
    landed(wg.at[:, y, :, half], lo.at[1])
    landed(wd, lo.at[2])
    for k in range(4):
        landed(wu.at[k, :, :, other], r3.at[0, k])
        landed(wg.at[:, k, :, other], r3.at[1, k])

    def rows_of(ref, k):
        return ref[:, :, cut(k)].reshape(4 * HALF, D)

    def forward(k):
        gather_take(0, xg, k)

        def cols(t, carry):
            cs = pl.ds(pl.multiple_of(t * 256, 256), 256)
            xs = rows_of(xg, k)
            u = jnp.dot(xs, wu[:, :, :, cs].reshape(D, 256), preferred_element_type=F32)
            g = jnp.dot(xs, wg[:, :, :, cs].reshape(D, 256), preferred_element_type=F32)
            tt = g * sg[0:1, cs]
            up[k, :, cs] = u
            gate[k, :, cs] = g
            hid[k, :, cs] = (u * su[0:1, cs] * (tt * jax.nn.sigmoid(tt))).astype(BF)
            return carry

        lax.fori_loop(0, 5, cols, 0)

        def down(t, carry):
            cs = pl.ds(pl.multiple_of(t * 256, 256), 256)
            v = jnp.dot(hid[k], wd[:, cs], preferred_element_type=F32)
            part[0, :, :, cut(k), cs] = v.astype(BF).reshape(2, 2, HALF, 256)
            return carry

        lax.fori_loop(0, 5, down, 0)
        scatter(1, part.at[0], k)

    for k in range(2):
        forward(k)

    def turn(dst, load):
        def body(t, carry):
            cs = pl.ds(pl.multiple_of(t * 256, 256), 256)
            for k in range(2):
                dst[cs, k * 256 : (k + 1) * 256] = load(k, cs).T
            return carry

        lax.fori_loop(0, 5, body, 0)

    turn(ht, lambda k, cs: hid[k, :, cs])
    am = rate_m[0:1]
    at = (c * 16 + z * 4 + y) * ROWS
    for k in range(2):
        total = scatter_take(1, k)
        position = at + k * HALF + lax.broadcasted_iota(jnp.int32, (HALF, 1), 0)
        live = (position < length[0]).astype(F32)
        base = first[cut(k)]
        d_base, d_part, g_am = mix_back(cot[cut(k)].astype(F32) * live, base, total, am)
        low[1, cut(k)] = d_part.astype(BF)
        gather(1, dd, k)
        dfirst[cut(k)] = d_base
        vec[1:2] += g_am
        result[cut(k)] = (mix_of(base, total, am)[0] * live).astype(BF)
    turn(xt, lambda k, cs: xg[:, :, cut(k), cs].reshape(256, 256))

    def backward(k):
        gather_take(1, dd, k)

        def cols(t, carry):
            cs = pl.ds(pl.multiple_of(t * 256, 256), 256)
            dh = nt(rows_of(dd, k), wd[cs, :])
            u, g = up[k, :, cs], gate[k, :, cs]
            sc, sgc = su[0:1, cs], sg[0:1, cs]
            tt = g * sgc
            sig = jax.nn.sigmoid(tt)
            silu = tt * sig
            dsilu = sig * (1.0 + tt * (1.0 - sig))
            dhs = dh * sc
            dhu = dh * u
            both = dhu * dsilu * sc
            dug[0, k, :, cs] = (dhs * silu).astype(BF)
            dug[1, k, :, cs] = (both * sgc).astype(BF)
            vec[2:3, cs] += jnp.sum(dhu * silu, axis=0, keepdims=True)
            vec[3:4, cs] += jnp.sum(both * g, axis=0, keepdims=True)
            return carry

        lax.fori_loop(0, 5, cols, 0)
        for t in range(2):
            v = nt(dug[0, k], wu[2 * t : 2 * t + 2].reshape(640, D)) + nt(
                dug[1, k], wg[2 * t : 2 * t + 2].reshape(640, D)
            )
            part[1, :, :, cut(k), t * 640 : (t + 1) * 640] = v.astype(BF).reshape(2, 2, HALF, 640)
        scatter(2, part.at[1], k)

    for k in range(2):
        backward(k)

    def meet(k):
        dy = dfirst[cut(k)] + scatter_take(2, k)
        d_res, d_part, g_aa = mix_back(dy, st[cut(k)].astype(F32), mixed[cut(k)], rate_a[0:1])
        low[2, cut(k)] = d_part.astype(BF)
        gather(2, dm, k)
        d_st[cut(k)] = d_res
        vec[0:1] += g_aa

    def grad_down(i, carry):
        w = jnp.where(i == 0, 1 - c, c)
        cols = pl.ds(pl.multiple_of(w * 640, 128), 640)
        for k in range(4):
            rhs = jnp.concatenate([dd[:, :, cut(j), cols].reshape(256, 640) for j in range(2)], axis=0)
            v = jnp.dot(ht[k * 320 : (k + 1) * 320, :], rhs, preferred_element_type=F32)
            gd[w, k] = v.astype(BF).reshape(4, 80, 640)

        @pl.when(i == 0)
        def _():
            rcopy(gd.at[1 - c], rd, sx.at[1], rx.at[1], sib).start()

        return carry

    def grad_up(w):
        def body(k, carry):
            rows = pl.ds(pl.multiple_of(k * 320, 64), 320)
            for t in range(2):
                cs = slice(t * 640, (t + 1) * 640)
                v = jnp.dot(xt[rows, :], dug[w, :, :, cs].reshape(512, 640), preferred_element_type=F32)
                ga[w, k, :, :, cs] = v.astype(BF).reshape(4, 80, 640)
            return carry

        lax.fori_loop(0, 4, body, 0)

    lax.fori_loop(0, 2, grad_down, 0)
    meet(0)
    landed(rd, rx.at[1])

    def add_d(k, carry):
        i, j = k // 4, k % 4
        rd[i, j] = (gd[c, i, j].astype(F32) + rd[i, j].astype(F32)).astype(BF)
        return carry

    lax.fori_loop(0, 16, add_d, 0)
    for d in (1, 3, 2):
        rcopy(rd.at[step(y, d)], rdy.at[y], sy.at[d], ry.at[y], to_y[d]).start()
    grad_up(1 - c)
    rcopy(ga.at[1 - c], ra, sx.at[0], rx.at[0], sib).start()
    meet(1)
    grad_up(c)
    landed(ra, rx.at[0])

    def add_a(k, carry):
        i, j = k // 4, k % 4
        ha[i, j] = (ga[c, i, j].astype(F32) + ra[i, j].astype(F32)).astype(BF)
        return carry

    lax.fori_loop(0, 16, add_a, 0)
    for d in (1, 2, 3):
        landed(rdy.at[step(y, d)], ry.at[step(y, d)])

    def sum_d(k, carry):
        v = rd[y, k].astype(F32)
        for d in (1, 2, 3):
            v = v + rdy[step(y, d), k].astype(F32)
        hd[k] = v.astype(BF)
        return carry

    lax.fori_loop(0, 4, sum_d, 0)
    for k in range(2):
        gather_take(2, dm, k)
    for n in range(3):
        gather_sent(n)
    for n, src in ((0, part0), (1, part.at[0]), (2, part.at[1])):
        scatter_sent(n, src)
    for i in range(2):
        for k in range(4):
            landed(gz, s3.at[i, k])
        for d in (1, 2, 3):
            landed(gz, s2.at[i, d])
    landed(ra, sx.at[0])
    landed(rd, sx.at[1])
    for d in (1, 2, 3):
        landed(rdy.at[y], sy.at[d])


def middle(length, part0, st, cot, rate_a, rate_m, su, sg, uq, wd, gz):
    V = pltpu.VMEM
    return remote_call(
        mid_kernel,
        [
            ((ROWS, D), BF, "v"),
            ((ROWS, D), F32, "v"),
            ((2, 2, ROWS, D), BF, "a"),
            ((4, 4, 80, D), BF, "v"),
            ((4, 80, 640), BF, "v"),
            ((8, D), F32, "v"),
        ],
        "savvvvvvaaa",
        [
            V((3, 4, ROWS, D), BF), V((3, ROWS, D), BF), V((2, 2, ROWS, D), BF), V((2, 2, ROWS, D), BF),
            V((4, 4, 80, D), BF), V((4, 4, 80, D), BF), V((D, D), BF),
            V((2, 256, D), F32), V((2, 256, D), F32), V((2, 256, D), BF), V((2, 2, 256, D), BF),
            V((2, 2, 2, ROWS, D), BF), V((D, 512), BF), V((D, 512), BF),
            V((ROWS, D), F32), V((ROWS, D), F32), V((ROWS, D), F32),
            V((2, 4, 4, 80, D), BF), V((2, 4, 4, 80, 640), BF), V((4, 4, 80, D), BF), V((4, 4, 80, 640), BF),
            V((4, 4, 80, 640), BF),
            dma(3, 2, 2, 2), dma(3, 2, 4), dma(3, 2, 4), dma(3, 2, 2, 2),
            dma(2, 4), dma(2, 4), dma(2, 4), dma(2, 4), dma(2), dma(2), dma(4), dma(4), dma(3),
        ],
        2,
        "middle",
    )(length, part0, st, cot, rate_a, rate_m, su, sg, uq, wd, gz)


CUT = 768


def back_kernel(
    length, q, kv_in, wo, dmix, att, lse, ha, hd, tt_in, xg_in, wq_in, scale, inner, outer, vec,
    pbuf, za, zd, zq, o_out, o_vec,
    kv, tt, xg, wq,
    qdo, delta, dqt, acc, low, give, mine, got, got_y, dq, dd, sums, part, gq, go,
    oax, oay, rax, ray, fax, fay, fd, hq, rqx, rqy, fqx, fqy, ob, ox, o2, vs, vb, ws, wb,
    lo, sg, rg, sy, ry, s1, r1, s2, r2, s3, r3, sz, rz, sc, rc, q1, p1, q2, p2, q3, p3, so, ro, sv, rv, sw, rw, ps, pr, sf, rf,
):
    x, c, z, y = here()
    sib = dev(x, 1 - c, z, y)
    to_y = [None] + [dev(x, c, z, step(y, d)) for d in (1, 2, 3)]
    to_x = [None] + [dev(step(x, d), c, z, y) for d in (1, 2, 3)]
    to_z = [None] + [dev(x, c, step(z, d), y) for d in (1, 2, 3)]
    near_first = (1, 3, 2)
    lcopy(kv_in, kv, lo.at[0]).start()
    lcopy(ha.at[x, :, :, 0:CUT], oax, lo.at[1]).start()
    lcopy(ha.at[:, y, :, CUT:D], oay, lo.at[2]).start()
    lcopy(tt_in, tt, lo.at[3]).start()
    lcopy(xg_in, xg, lo.at[4]).start()
    lcopy(wq_in, wq, lo.at[5]).start()
    greet(z_peers(x, c, z, y) + to_y[1:] + to_x[1:])
    for d in near_first:
        rcopy(hd.at[step(x, d)], fd.at[x], s2.at[1, d], r2.at[1, x], to_x[d]).start()
    for d in near_first:
        rcopy(ha.at[step(x, d), :, :, 0:CUT], rax.at[x], s1.at[0, d], r1.at[0, x], to_x[d]).start()
        rcopy(ha.at[:, step(y, d), :, CUT:D], ray.at[y], s1.at[1, d], r1.at[1, y], to_y[d]).start()

    def settle(h):
        landed(got.at[h], rg.at[h])
        for i in range(2):
            for k in range(2):
                mine[h, i, k] = (mine[h, i, k].astype(F32) + got[h, i, k].astype(F32)).astype(BF)
        for d in near_first:
            rcopy(mine.at[h, :, :, step(y, d)], got_y.at[h, y], sy.at[h, d], ry.at[h, y], to_y[d]).start()

    d_att = nt(dmix[...], wo[...]).astype(BF)
    for h in range(HG):
        low[:, h * HDIM : (h + 1) * HDIM] = att[h].astype(BF)
        dh = d_att[:, h * HDIM : (h + 1) * HDIM].astype(F32)
        wide = jnp.concatenate([jnp.zeros_like(dh), dh], axis=1).astype(BF)
        prod = dh * att[h]
        for j in range(BLOCKS):
            rows = slice(j * ROWS, (j + 1) * ROWS)
            qdo[h, j, :ROWS] = q[h, rows, :]
            qdo[h, j, ROWS:] = wide[rows]
            delta[h, j : j + 1, :] = jnp.sum(prod[rows].T, axis=0, keepdims=True)
    for k in range(2):
        g = tn(low[...], dmix[:, k * 640 : (k + 1) * 640])
        go[k] = g.astype(BF).reshape(4, 80, 640)
    rcopy(go.at[1 - c], ob, sc.at[1], rc.at[1], sib).start()
    rcopy(vec, vb.at[0], sv.at[0, 0], rv.at[0, 0], sib).start()

    def small_cores():
        landed(ob, rc.at[1])
        landed(vb.at[0], rv.at[0, 0])
        vs[...] = vec[...] + vb[0]
        for k in range(4):
            ob[k] = (go[c, k].astype(F32) + ob[k].astype(F32)).astype(BF)
        for d in near_first:
            rcopy(ob.at[step(y, d)], ox.at[y], so.at[0, d], ro.at[0, y], to_y[d]).start()
            rcopy(vs, vb.at[d], sv.at[1, d], rv.at[1, d], to_y[d]).start()

    def small_y():
        v, tot = ob[y].astype(F32), vs[...]
        for d in (1, 2, 3):
            landed(ox.at[step(y, d)], ro.at[0, step(y, d)])
            landed(vb.at[d], rv.at[1, d])
            landed(vs, sv.at[1, d])
            v = v + ox[step(y, d)].astype(F32)
            tot = tot + vb[d]
        ox[y] = v.astype(BF)
        vs[...] = tot
        for d in near_first:
            rcopy(ox.at[y], o2.at[d], so.at[1, d], ro.at[1, d], to_x[d]).start()
            rcopy(vs, vb.at[3 + d], sv.at[2, d], rv.at[2, d], to_x[d]).start()

    def small_x():
        v, tot = ox[y].astype(F32), vs[...]
        for d in (1, 2, 3):
            landed(o2.at[d], ro.at[1, d])
            landed(vb.at[3 + d], rv.at[2, d])
            landed(vs, sv.at[2, d])
            v = v + o2[d].astype(F32)
            tot = tot + vb[3 + d]
        o_out[c] = v.astype(BF)
        vs[...] = tot
        rcopy(o_out.at[c], o_out.at[c], sf.at[3], rf.at[3], sib).start()
        for d in near_first:
            rcopy(vs, vb.at[6 + d], sv.at[3, d], rv.at[3, d], to_z[d]).start()

    def small_z():
        tot = vs[...]
        for d in (1, 2, 3):
            landed(vb.at[6 + d], rv.at[3, d])
            landed(vs, sv.at[3, d])
            tot = tot + vb[6 + d]
        o_vec[0:2] = tot[0:2]
        o_vec[2:] = vs[2:]

    def down_x():
        v = hd[x].astype(F32)
        for d in (1, 2, 3):
            landed(fd.at[step(x, d)], r2.at[1, step(x, d)])
            v = v + fd[step(x, d)].astype(F32)
        zd[c, x] = v.astype(BF)
        for d in near_first:
            rcopy(zd.at[c, x], zd.at[c, x], s3.at[1, d], r3.at[1, x], to_x[d]).start()

    def down_done():
        for d in (1, 2, 3):
            landed(zd.at[c, step(x, d)], r3.at[1, step(x, d)])
        rcopy(zd.at[c], zd.at[c], sf.at[1], rf.at[1], sib).start()

    def up_first():
        landed(oax, lo.at[1])
        landed(oay, lo.at[2])
        for d in (1, 2, 3):
            landed(rax.at[step(x, d)], r1.at[0, step(x, d)])
            landed(ray.at[step(y, d)], r1.at[1, step(y, d)])

        def body(k, carry):
            v, w = oax[k].astype(F32), oay[k].astype(F32)
            for d in (1, 2, 3):
                v = v + rax[step(x, d), k].astype(F32)
                w = w + ray[step(y, d), k].astype(F32)
            oax[k] = v.astype(BF)
            oay[k] = w.astype(BF)
            return carry

        lax.fori_loop(0, 4, body, 0)
        for d in near_first:
            rcopy(oax.at[step(y, d)], fax.at[y], s2.at[0, d], r2.at[0, y], to_y[d]).start()
            rcopy(oay.at[step(x, d)], fay.at[x], s2.at[2, d], r2.at[2, x], to_x[d]).start()

    landed(kv, lo.at[0])
    item = work_items(c, y, length[0])

    def per_head(h, carry):
        acc[...] = jnp.zeros_like(acc)
        dqt[...] = jnp.zeros_like(dqt)
        for k, f in ((1, small_cores), (2, small_y), (2, down_x), (3, small_x), (4, small_z), (4, down_done)):
            pl.when(h == k)(f)

        def body(g, carry):
            @pl.when(jnp.logical_and(g == 1, h > 0))
            def _():
                settle(h - 1)

            pl.when(jnp.logical_and(g == 2, h == HG - 1))(up_first)
            key = lax.broadcasted_iota(jnp.int32, (TILE, ROWS), 0)
            its = [item(g * STEP + u) for u in range(STEP)]
            ks = [key_tile(kv, h, t) for _, t, _ in its]
            bs = [qdo[h, j] for j, _, _ in its]
            sds = [nt(k, b) for k, b in zip(ks, bs)]
            dss, pp = [], []
            for sd, (j, _, bound) in zip(sds, its):
                p = jnp.where(key <= bound, jnp.exp(sd[:, :ROWS] - lse[h, pl.ds(j, 1), :]), 0.0)
                dss.append((p * (sd[:, ROWS:] - delta[h, pl.ds(j, 1), :])).astype(BF))
                pp.append(p.astype(BF))
            for ds, p, b, (_, t, _) in zip(dss, pp, bs, its):
                acc[t] += jnp.dot(jnp.concatenate([ds, p], axis=1), b, preferred_element_type=F32)
            for k, ds, (j, _, _) in zip(ks, dss, its):
                dqt[j] += tn(k, ds)
            return carry

        lax.fori_loop(0, 18 // STEP, body, 0)

        def store(i, carry):
            zi, k = i // 2, i % 2
            give[h, zi, k] = acc[k * 4 + owner_z(1 - c, zi)].astype(BF).reshape(4, ROWS, 128)
            mine[h, zi, k] = acc[k * 4 + owner_z(c, zi)].astype(BF).reshape(4, ROWS, 128)
            return carry

        lax.fori_loop(0, 4, store, 0)
        rcopy(give.at[h], got.at[h], sg.at[h], rg.at[h], sib).start()
        for j in range(BLOCKS):
            dq[h, j * ROWS : (j + 1) * ROWS, :] = dqt[j].T * 0.125
        return carry

    lax.fori_loop(0, HG, per_head, 0)
    settle(HG - 1)
    ws[...] = jnp.zeros_like(ws)
    landed(tt, lo.at[3])
    landed(xg, lo.at[4])
    landed(wq, lo.at[5])
    sums[...] = jnp.zeros_like(sums)
    lane = lanes()

    def through(h, carry):
        for d in (1, 2, 3):
            landed(got_y.at[h, step(y, d)], ry.at[h, step(y, d)])
        cols = pl.ds(pl.multiple_of(h * 128, 128), 128)
        pair = pl.ds(pl.multiple_of(640 + (h // 2) * 128, 128), 128)
        odd = h % 2 == 1

        def per_block(j, carry):
            i, k = j // 2, j % 2
            rows = pl.ds(pl.multiple_of(j * ROWS, ROWS), ROWS)
            cosine, sine = turn_of(inner, outer, block_index(c, y, j))
            grads = mine[h, i, k, y].astype(F32)
            for d in (1, 2, 3):
                grads = grads + got_y[h, step(y, d), i, k].astype(F32)
            grads = grads.astype(BF).astype(F32)
            turned = pltpu.roll(grads, 64, 1)
            t = tt[h, rows, :]
            dy = jnp.where(lane < 64, dq[h, rows, :].astype(BF).astype(F32), turned)
            inv = lax.rsqrt(half_means(t * t, lane) + EPS)
            unit = t * inv
            sums[:, cols] += jnp.sum((dy * unit).reshape(ROWS // 8, 8, 128), axis=0)
            dyh = dy * scale[0:1, cols]
            dt = (dyh - unit * half_means(dyh * unit, lane)) * inv
            dd[rows, cols] = (dt * cosine + swap(dt * sine, lane)).astype(BF)
            before = jnp.where(odd, dd[rows, pair].astype(F32), turned)
            dd[rows, pair] = jnp.where(lane < 64, before, jnp.where(odd, grads, 0.0)).astype(BF)
            return carry

        lax.fori_loop(0, BLOCKS, per_block, 0)
        return carry

    lax.fori_loop(0, HG - 1, through, 0)
    for d in (1, 2, 3):
        landed(fax.at[step(y, d)], r2.at[0, step(y, d)])
        landed(fay.at[step(x, d)], r2.at[2, step(x, d)])
    v, w = oax[y].astype(F32), oay[x].astype(F32)
    for d in (1, 2, 3):
        v = v + fax[step(y, d)].astype(F32)
        w = w + fay[step(x, d)].astype(F32)
    za[2, x, :, 0:CUT] = v.astype(BF)
    za[2, x, :, CUT:D] = w.astype(BF)
    for d in near_first:
        rcopy(za.at[2, x], za.at[2, x], s3.at[0, d], r3.at[0, x], to_x[d]).start()
    through(HG - 1, 0)

    def weights(i, carry):
        h = jnp.where(i == 0, 1 - c, c)
        cols = pl.ds(pl.multiple_of(h * 512, 128), 512)
        gq[h] = tn(xg[...].reshape(512, D), dd[:, cols]).astype(BF).reshape(4, 4, 80, 512)

        @pl.when(i == 0)
        def _():
            rcopy(gq.at[1 - c], hq, sc.at[0], rc.at[0], sib).start()

        return carry

    def inputs(p, carry):
        rows = pl.ds(pl.multiple_of(p * 256, 256), 256)
        v = nt(dd[rows, 0:512], wq[0].reshape(D, 512)) + nt(dd[rows, 512:1024], wq[1].reshape(D, 512))
        part[p] = v.astype(BF).reshape(2, ROWS, D)
        z_scatter_pair(part, pbuf, ps, pr, p, x, c, z, y)
        return carry

    lax.fori_loop(0, 2, weights, 0)
    for h in range(HG):
        v = jnp.sum(sums[:, h * 128 : (h + 1) * 128], axis=0, keepdims=True)
        ws[:, h * HDIM : (h + 1) * HDIM] = jnp.broadcast_to(v[:, :HDIM] + v[:, HDIM:], (8, HDIM))
    rcopy(ws, wb.at[0], sw.at[0, 0], rw.at[0, 0], sib).start()

    landed(hq, rc.at[0])

    def add_q(k, carry):
        i, j = k // 4, k % 4
        v = (gq[c, i, j].astype(F32) + hq[i, j].astype(F32)).astype(BF)
        fqx[i, j] = v[:, :256]
        fqy[j, i] = v[:, 256:]
        return carry

    lax.fori_loop(0, 16, add_q, 0)
    for d in near_first:
        rcopy(fqx.at[step(x, d)], rqx.at[x], q1.at[0, d], p1.at[0, x], to_x[d]).start()
        rcopy(fqy.at[step(y, d)], rqy.at[y], q1.at[1, d], p1.at[1, y], to_y[d]).start()
    landed(wb.at[0], rw.at[0, 0])
    landed(ws, sw.at[0, 0])
    ws[...] = ws[...] + wb[0]
    for d in near_first:
        rcopy(ws, wb.at[d], sw.at[1, d], rw.at[1, d], to_y[d]).start()
    for d in (1, 2, 3):
        landed(za.at[2, step(x, d)], r3.at[0, step(x, d)])
    for d in near_first:
        rcopy(za.at[2, step(z, d)], za.at[c, z], sz.at[0, d], rz.at[0, z], to_z[d]).start()
    za[c, z] = za[2, z]
    lax.fori_loop(0, 2, inputs, 0)
    for d in (1, 2, 3):
        landed(rqx.at[step(x, d)], p1.at[0, step(x, d)])
        landed(rqy.at[step(y, d)], p1.at[1, step(y, d)])

    def add_q1(k, carry):
        a, b = fqx[x, k].astype(F32), fqy[y, k].astype(F32)
        for d in (1, 2, 3):
            a = a + rqx[step(x, d), k].astype(F32)
            b = b + rqy[step(y, d), k].astype(F32)
        rqx[x, k] = a.astype(BF)
        rqy[y, k] = b.astype(BF)
        return carry

    lax.fori_loop(0, 4, add_q1, 0)
    for d in near_first:
        rcopy(rqx.at[x, step(y, d)], fqx.at[4, y], q2.at[0, d], p2.at[0, y], to_y[d]).start()
        rcopy(rqy.at[y, step(x, d)], fqy.at[4, x], q2.at[1, d], p2.at[1, x], to_x[d]).start()
    tot = ws[...]
    for d in (1, 2, 3):
        landed(wb.at[d], rw.at[1, d])
        landed(ws, sw.at[1, d])
        tot = tot + wb[d]
    ws[...] = tot
    for d in near_first:
        rcopy(ws, wb.at[3 + d], sw.at[2, d], rw.at[2, d], to_x[d]).start()
    for d in (1, 2, 3):
        landed(fqx.at[4, step(y, d)], p2.at[0, step(y, d)])
        landed(fqy.at[4, step(x, d)], p2.at[1, step(x, d)])
    a, b = rqx[x, y].astype(F32), rqy[y, x].astype(F32)
    for d in (1, 2, 3):
        a = a + fqx[4, step(y, d)].astype(F32)
        b = b + fqy[4, step(x, d)].astype(F32)
    zq[0, x] = jnp.concatenate([a, b], axis=1).astype(BF)
    for d in near_first:
        rcopy(zq.at[0, x], zq.at[0, x], q3.at[d], p3.at[x], to_x[d]).start()
    tot = ws[...]
    for d in (1, 2, 3):
        landed(wb.at[3 + d], rw.at[2, d])
        landed(ws, sw.at[2, d])
        tot = tot + wb[3 + d]
    o_vec[4:5, 0:384] = tot[0:1]
    for d in (1, 2, 3):
        landed(zq.at[0, step(x, d)], p3.at[step(x, d)])
    for d in near_first:
        rcopy(zq.at[0, step(z, d)], zq.at[1 + c, z], sz.at[1, d], rz.at[1, z], to_z[d]).start()
    zq[1 + c, z] = zq[0, z]
    for d in (1, 2, 3):
        landed(za.at[c, step(z, d)], rz.at[0, step(z, d)])
    rcopy(za.at[c], za.at[c], sf.at[0], rf.at[0], sib).start()
    for d in (1, 2, 3):
        landed(zq.at[1 + c, step(z, d)], rz.at[1, step(z, d)])
    rcopy(zq.at[1 + c], zq.at[1 + c], sf.at[2], rf.at[2], sib).start()
    z_scatter_take(pbuf, pr)
    landed(za.at[1 - c], rf.at[0])
    landed(zd.at[1 - c], rf.at[1])
    landed(zq.at[2 - c], rf.at[2])
    landed(o_out.at[1 - c], rf.at[3])
    def sent(h, carry):
        landed(give.at[h], sg.at[h])
        for d in (1, 2, 3):
            landed(got_y.at[h, y], sy.at[h, d])
        return carry

    lax.fori_loop(0, HG, sent, 0)
    z_scatter_sent(part, ps, c, z)
    landed(hq, sc.at[0])
    landed(ob, sc.at[1])
    landed(vec, sv.at[0, 0])
    landed(o_out.at[0], sf.at[3])
    landed(za.at[0], sf.at[0])
    landed(zd.at[0], sf.at[1])
    landed(zq.at[1], sf.at[2])
    for d in (1, 2, 3):
        landed(rax.at[x], s1.at[0, d])
        landed(ray.at[y], s1.at[1, d])
        landed(fax.at[0], s2.at[0, d])
        landed(fd.at[0], s2.at[1, d])
        landed(fay.at[0], s2.at[2, d])
        landed(za.at[0, 0], s3.at[0, d])
        landed(fd.at[0], s3.at[1, d])
        landed(za.at[0, 0], sz.at[0, d])
        landed(zq.at[0, 0], sz.at[1, d])
        landed(rqx.at[0], q1.at[0, d])
        landed(rqy.at[0], q1.at[1, d])
        landed(fqx.at[0, 0], q2.at[0, d])
        landed(fqy.at[0, 0], q2.at[1, d])
        landed(zq.at[0, 0], q3.at[d])
        landed(ox.at[0], so.at[0, d])
        landed(ox.at[0], so.at[1, d])


def back(length, q, kv, wo, dmix, att, lse, ha, hd, tt, xg, wq, scale, inner, outer, vec):
    n = BLOCKS * ROWS
    V = pltpu.VMEM
    return remote_call(
        back_kernel,
        [
            ((4, ROWS, D), BF, "v"),
            ((3, 4, 80, D), BF, "v"),
            ((2, 4, 80, 640), BF, "v"),
            ((3, 4, 80, 512), BF, "v"),
            ((2, 80, 640), BF, "v"),
            ((8, D), F32, "v"),
        ],
        "svavvvvavaaavvvv",
        [
            V((HG, 2, 2, 2, 4, ROWS, 128), BF), V((HG, n, 128), F32), V((2, 2, ROWS, D), BF), V((2, 4, 4, 80, 512), BF),
            V((HG, BLOCKS, 2 * ROWS, 128), BF), V((HG, BLOCKS, 128), F32), V((BLOCKS, 128, ROWS), F32), V((8, TILE, 128), F32),
            V((n, GROUP), BF),
            V((HG, 2, 2, 4, ROWS, 128), BF), V((HG, 2, 2, 4, ROWS, 128), BF), V((HG, 2, 2, 4, ROWS, 128), BF),
            V((HG, 4, 2, 2, ROWS, 128), BF), V((HG, n, 128), F32), V((n, 1024), BF), V((8, HG * 128), F32),
            V((2, 2, ROWS, D), BF), V((2, 4, 4, 80, 512), BF), V((2, 4, 80, 640), BF),
            V((4, 80, CUT), BF), V((4, 80, D - CUT), BF), V((4, 4, 80, CUT), BF), V((4, 4, 80, D - CUT), BF),
            V((4, 80, CUT), BF), V((4, 80, D - CUT), BF), V((4, 80, 640), BF),
            V((4, 4, 80, 512), BF), V((4, 4, 80, 256), BF), V((4, 4, 80, 256), BF), V((5, 4, 80, 256), BF), V((5, 4, 80, 256), BF),
            V((4, 80, 640), BF), V((4, 80, 640), BF), V((4, 80, 640), BF), V((8, D), F32), V((10, 8, D), F32), V((8, 384), F32), V((7, 8, 384), F32),
            dma(6), dma(HG), dma(HG), dma(HG, 4), dma(HG, 4),
            dma(2, 4), dma(2, 4), dma(3, 4), dma(3, 4), dma(2, 4), dma(2, 4), dma(2, 4), dma(2, 4), dma(2), dma(2),
            dma(2, 4), dma(2, 4), dma(2, 4), dma(2, 4), dma(4), dma(4), dma(2, 4), dma(2, 4), dma(4, 4), dma(4, 4), dma(3, 4), dma(3, 4),
            dma(2, 2), dma(4), dma(4), dma(4),
        ],
        3,
        "back",
    )(length, q, kv, wo, dmix, att, lse, ha, hd, tt, xg, wq, scale, inner, outer, vec)


def finish_kernel(res, d_st, pbuf, za, zd, zq, out, vec, result, g_in, o_q, o_k, o_v, o_out, o_up, o_gate, o_down, o_vec):
    _, _, z, y = here()
    result[...] = res[...]
    g_in[...] = d_st[...] + total_of(pbuf)
    o_out[:, :640] = out[0].astype(F32)
    o_out[:, 640:] = out[1].astype(F32)
    for k in range(4):
        cols = slice(k * D, (k + 1) * D)
        o_up[:, cols] = za[0, k].astype(F32)
        o_gate[:, cols] = za[1, k].astype(F32)
        for h in range(2):
            o_down[k * 80 : (k + 1) * 80, h * 640 : (h + 1) * 640] = zd[h, k].astype(F32)
        a, b = zq[1, k].astype(F32), zq[2, k].astype(F32)
        at = k * GROUP
        pairs = [a[:, h * 128 : (h + 1) * 128] for h in range(4)] + [b[:, :128]]
        o_q[:, at : at + GROUP] = jnp.concatenate([v[:, :HDIM] for v in pairs], axis=1)
        o_k[:, at : at + GROUP] = jnp.concatenate([v[:, HDIM:] for v in pairs], axis=1)
        o_v[:, at : at + GROUP] = b[:, 128:448]
    v = vec[...]
    o_vec[0:2] = pltpu.roll(v, (16 - (z * 4 + y)) % 16 * 80, 1)[0:2]
    o_vec[2:4] = pltpu.roll(v, (4 - y) % 4 * 320, 1)[2:4]
    o_vec[4:] = pltpu.roll(v, (16 - y) % 16 * 80, 1)[4:]


def finish(res, d_st, pbuf, za, zd, zq, out, vec):
    return local_call(
        finish_kernel,
        [
            ((ROWS, D), BF),
            ((ROWS, D), F32),
            ((80, D), F32),
            ((80, D), F32),
            ((80, D), F32),
            ((80, D), F32),
            ((80, FF), F32),
            ((80, FF), F32),
            ((320, D), F32),
            ((8, D), F32),
        ],
        8,
        [],
        "finish",
    )(res, d_st, pbuf, za, zd, zq, out, vec)


def shards(
    states, w_query, w_key, w_value, w_out, w_up, w_gate, w_down,
    scale_qk, alpha_attn, alpha_mlp, scale_up, scale_gate, lengths, cotangent,
):
    x, c, z, y = here()
    st = states[0]

    def heads(w):
        return w.reshape(80, 4, HG, HDIM)

    q4, k4, v4 = heads(w_query), heads(w_key), heads(w_value)
    qk = jnp.stack([q4, k4], axis=3).reshape(80, 4, HG * 128)
    half1 = jnp.concatenate([qk[:, :, 512:], v4.reshape(80, 4, GROUP), jnp.zeros((80, 4, HDIM), BF)], axis=2)
    wq = jnp.stack([qk[:, :, :512], half1]).transpose(0, 2, 1, 3)
    vec = jnp.concatenate([scale_qk, alpha_attn, alpha_mlp, scale_up, scale_gate, jnp.zeros((16,), BF)])
    vec = jnp.broadcast_to(vec.astype(F32)[None], (8, 896))
    inner, outer = (jnp.asarray(t) for t in rope_tables())
    n = BLOCKS * ROWS
    part, att, lse, kv, q, turned, xg, wqkv, wo, scale, rate_a, rate_m, su, sg, uq, wd, gz = front(
        lengths, st, wq, vec, w_out, w_up, w_gate, w_down, inner, outer
    )
    result, d_st, dm, ha, hd, vec = middle(
        lengths, part, st, cotangent[0], rate_a, rate_m, su, sg, uq, wd.reshape(D, D), gz
    )
    pbuf, za, zd, zq, out, vec = back(
        lengths, q, kv, wo.reshape(GROUP, D), dm.reshape(n, D), att, lse, ha, hd, turned, xg, wqkv, scale, inner, outer, vec
    )
    result, g_in, o_q, o_k, o_v, o_out, o_up, o_gate, o_down, o_vec = finish(
        result, d_st, pbuf, za, zd, zq, out, vec
    )
    return (
        result[None],
        g_in[None],
        o_q,
        o_k,
        o_v,
        o_out,
        o_up,
        o_gate,
        o_down,
        o_vec[4, :80],
        o_vec[0, :80],
        o_vec[1, :80],
        o_vec[2, :320],
        o_vec[3, :320],
    )


def solution(mesh):
    row = P("grp", ("seq", "shard"), None)
    mat = P("shard", None)
    one = P("shard")
    return jax.shard_map(
        shards,
        mesh=mesh,
        in_specs=(row,) + (mat,) * 7 + (one,) * 5 + (P("grp"), row),
        out_specs=(row, row) + (mat,) * 7 + (one,) * 5,
        check_vma=False,
    )
```

time: 360 us -> 308 us (0.86)
  Pallas kernels: 346 us -> 297 us
    pallas_call x3 -> x1, Pallas kernels: 137 us -> 107 us  [back(): remote_call(back_kernel, [((4, ROWS, D), BF, 'v'), ((3, 4, 80, D), BF, 'v...]
    pallas_call x1, Pallas kernels: 92.2 us -> 82.3 us  [front(): remote_call(front_kernel, [((2, 2, ROWS, D), BF, 'v'), ((HG, n, HDIM), F3...]
    pallas_call x1, Pallas kernels: 110 us -> 101 us  [middle(): remote_call(mid_kernel, [((ROWS, D), BF, 'v'), ((ROWS, D), F32, 'v'), ((2...]
where the time goes in v4:
time: 308 us; the launch traced here: 307 us
  Pallas kernels  297 us (96%)
  local copies, waits for them, and re-layouts  7.46 us (2%)
    pallas_call x1, Pallas kernels, back(): remote_call(back_kernel, [((4, ROWS, D), BF, 'v'), ((3, 4, 80, D), BF, 'v...  107 us
    pallas_call x1, Pallas kernels, middle(): remote_call(mid_kernel, [((ROWS, D), BF, 'v'), ((ROWS, D), F32, 'v'), ((2...  101 us
    pallas_call x1, Pallas kernels, front(): remote_call(front_kernel, [((2, 2, ROWS, D), BF, 'v'), ((HG, n, HDIM), F3...  82.3 us
    pallas_call x1, Pallas kernels, finish(): local_call(finish_kernel, [((ROWS, D), BF), ((ROWS, D), F32), ((80, D), F...  6.67 us

profile of v4, /device:TPU:1, one launch (start us, length us, event | category | flops | bytes accessed | tf_op | source)
XLA Modules:
  0.0 307.2 jit_solution(4820680708155071558)
XLA Ops:
  1.3 1.2 reshape_reshape.3
  2.5 1.1 copy.34
  3.7 1.2 copy.33
  4.9 0.1 pad_maximum_fusion
  5.0 0.1 copy.35
  5.1 0.1 copy.40
  5.2 0.1 pad.4.clone
  5.3 0.1 maximum_bitcast_fusion.1
  5.4 0.0 copy-start
  5.4 0.0 copy-start.1
  5.4 0.0 copy-start.2
  5.4 0.0 copy-start.3
  5.4 0.0 copy-start.4
  5.5 0.2 copy.39
  5.7 0.9 maximum_bitcast_fusion.wq
  6.6 0.0 copy-done
  6.6 0.0 copy-done.1
  6.6 0.0 copy-done.2
  6.6 0.0 copy-done.3
  6.6 0.0 copy-done.4
  6.6 0.1 concatenate.14
  6.7 0.6 broadcast_in_dim.16.vec
  7.3 82.3 %front.1 = (bf16[2,2,128,1280]{3,2,1,0:T(8,128)(2,1)}, f32[5,512,64]{2,1,0:T(8,128)}, f32[5,4,128]{2,1,0:T(4,128)}, bf16[5,2,2,2,4,128,128]{6,5,4,3,2,1,0:T(8,12...) custom-call(s32[1]{0:T(128)S(6)} %copy.41.length, ...), custom_call_target="tpu_custom_call" | custom-call | tf_op jit(solution)/shard_map/front/pallas_call | solution.py:527
  89.6 101.1 %middle.1 = (bf16[128,1280]{1,0:T(8,128)(2,1)}, f32[128,1280]{1,0:T(8,128)}, bf16[2,2,128,1280]{3,2,1,0:T(8,128)(2,1)}, bf16[4,4,80,1280]{3,2,1,0:T(8,128)(2,1)}...) custom-call(s32[1]{0:T(128)S(6)} %copy.41.length, bf16[2,2,128,1280]{3,2,1,0:T(8,128)(2,1)} %get-tuple-element.53.part0, ...), custom_call_target="tpu_custom_call" | custom-call | tf_op jit(solution)/shard_map/middle/pallas_call | solution.py:876
  190.7 107.1 %back.1 = (bf16[4,128,1280]{2,1,0:T(8,128)(2,1)}, bf16[3,4,80,1280]{3,2,1,0:T(8,128)(2,1)}, bf16[2,4,80,640]{3,2,1,0:T(8,128)(2,1)}, bf16[3,4,80,512]{3,2,1,0:T(...) custom-call(s32[1]{0:T(128)S(6)} %copy.41.length, bf16[5,512,128]{2,1,0:T(8,128)(2,1)} %get-tuple-element.63.q, ...), custom_call_target="tpu_custom_call" | custom-call | tf_op jit(solution)/shard_map/back/pallas_call | solution.py:1281
  297.9 6.7 %finish.1 = (bf16[128,1280]{1,0:T(8,128)(2,1)}, f32[128,1280]{1,0:T(8,128)}, f32[80,1280]{1,0:T(8,128)}, f32[80,1280]{1,0:T(8,128)}, f32[80,1280]{1,0:T(8,128)},...) custom-call(bf16[128,1280]{1,0:T(8,128)(2,1)} %get-tuple-element.61., ...), custom_call_target="tpu_custom_call" | custom-call | tf_op jit(solution)/shard_map/finish/pallas_call | solution.py:1338
  304.5 1.3 slice_bitcast_fusion
  305.9 1.4 slice_reduce_fusion
  (5 shorter events, 0.1 us)
Async XLA Ops:
  5.4 1.2 copy-start
  5.4 1.2 copy-start.1
  5.4 1.2 copy-start.2
  5.4 1.2 copy-start.3
  5.4 1.2 copy-start.4

commit v5 on v4

--- a/solution.py
+++ b/solution.py
@@ -249,9 +249,9 @@
 
 
 def front_kernel(
-    length, st, wq, vec, w_out, w_up, w_gate, w_down, inner, outer,
+    length, st, w_query, w_key, w_value, v_qk, v_attn, v_mlp, v_up, v_gate, w_out, w_up, w_gate, w_down, inner, outer,
     part, att, lse, kv_o, q_o, t_o, xg_o, wqkv_o, wo_o, scale_o, rate_a, rate_m, su, sg, uq, wd, gz,
-    xg, wqkv, vecs, wo, y0, y1, kv, kvb, q, tt, low, acc, tot, uz,
+    xg, wqkv, vecs, wo, y0, y1, kv, kvb, q, tt, low, acc, tot, uz, wq, vec,
     xs, xr, w1s, w1r, w2s, w2r, w3s, w3r, vs, vr, os, orr, lo,
     f1s, f1r, f2s, f2r, f3s, f3r, f4s, f4r, fl, sy, ry, sf, rf, ss, rs, kl, ol,
 ):
@@ -263,12 +263,36 @@
     to_y = [None] + [dev(x, c, z, step(y, d)) for d in (1, 2, 3)]
     to_x = [None] + [dev(step(x, d), c, z, y) for d in (1, 2, 3)]
     near_first = (1, 3, 2)
+
+    def head(ref, k):
+        return ref[:, k * HDIM : (k + 1) * HDIM]
+
+    @pl.when(c == 0)
+    def _():
+        for zz in range(4):
+            for h in range(4):
+                k = zz * HG + h
+                wq[zz, :, h * 128 : (h + 1) * 128] = jnp.concatenate([head(w_query, k), head(w_key, k)], axis=1)
+
+    @pl.when(c == 1)
+    def _():
+        for zz in range(4):
+            k = zz * HG
+            wq[zz, :, 0:128] = jnp.concatenate([head(w_query, k + 4), head(w_key, k + 4)], axis=1)
+            for h in range(2):
+                wq[zz, :, 128 + h * 128 : 256 + h * 128] = w_value[:, (k + 2 * h) * HDIM : (k + 2 * h + 2) * HDIM]
+            last = head(w_value, k + 4)
+            wq[zz, :, 384:512] = jnp.concatenate([last, jnp.zeros_like(last)], axis=1)
+
+    vec[...] = jnp.zeros_like(vec)
+    for ref, at, n in ((v_qk, 0, 80), (v_attn, 80, 80), (v_mlp, 160, 80), (v_up, 240, 320), (v_gate, 560, 320)):
+        vec[:, at : at + n] = jnp.broadcast_to(ref[...].astype(F32), (8, n))
     greet(z_peers(x, c, z, y) + to_y[1:] + to_x[1:])
 
     for d in near_first:
-        rcopy(wq.at[c, step(z, d)], wqkv.at[c, z, y], w1s.at[d], w1r.at[z], to_z[d]).start()
+        rcopy(wq.at[step(z, d)], wqkv.at[c, z, y], w1s.at[d], w1r.at[z], to_z[d]).start()
         rcopy(vec, vecs.at[z, y], vs.at[0, d], vr.at[0, z], to_z[d]).start()
-    lcopy(wq.at[c, z], wqkv.at[c, z, y], lo.at[0]).start()
+    lcopy(wq.at[z], wqkv.at[c, z, y], lo.at[0]).start()
     lcopy(vec, vecs.at[z, y], lo.at[1]).start()
     for d in near_first:
         rcopy(w_out.at[:, half], wo.at[y, :, half], os.at[0, d], orr.at[0, y], to_y[d]).start()
@@ -366,8 +390,9 @@
             q[h, rows, :] = (jnp.where(lane < 64, both, 0.0).astype(BF).astype(F32) * 0.125).astype(BF)
             return carry
 
-        lax.fori_loop(0, BLOCKS, per_block, 0)
-        send(h)
+        lax.fori_loop(0, BLOCKS, per_block, 0, unroll=True)
+        if h < 2:
+            send(h)
     landed(wd.at[y, x, :, half], fl.at[2])
     for d in (1, 2, 3):
         landed(wd.at[step(y, d), x, :, half], f2r.at[1, step(y, d)])
@@ -430,11 +455,16 @@
         lcopy(uz, uq.at[y], fl.at[1]).start()
 
     near(0)
+    send(2)
 
     def per_head(i, carry):
         @pl.when(i + 1 < HG)
         def _():
             near(i + 1)
+
+        @pl.when(i + 3 < HG)
+        def _():
+            send(i + 3)
 
         @pl.when(i == HG)
         def _():
@@ -521,7 +551,7 @@
     landed(wo, ol.at[4])
 
 
-def front(length, st, wq, vec, w_out, w_up, w_gate, w_down, inner, outer):
+def front(length, st, w_query, w_key, w_value, vectors, w_out, w_up, w_gate, w_down, inner, outer):
     n = BLOCKS * ROWS
     V = pltpu.VMEM
     return remote_call(
@@ -545,19 +575,20 @@
             ((4, 4, 80, D), BF, "a"),
             ((4, 80, 640), BF, "a"),
         ],
-        "saavaaaavv",
+        "savvvvvvvvaaaavv",
         [
             V((2, 2, ROWS, D), BF), V((2, 4, 4, 80, 512), BF), V((4, 4, 8, 896), F32), V((4, 80, D), BF),
             V((2, 256, 512), F32), V((2, 256, 512), F32),
             V((HG, 2, 2, ROWS, 128), BF), V((HG, 2, 2, 2, 4, ROWS, 128), BF), V((HG, n, 128), BF), V((HG, n, 128), F32),
             V((n, GROUP), BF), V((BLOCKS, 128, ROWS), F32), V((BLOCKS, 8, ROWS), F32), V((80, 640), BF),
+            V((4, 80, 512), BF), V((8, 896), F32),
             dma(4), dma(2, 2), dma(4), dma(4), dma(4), dma(4), dma(5), dma(5), dma(2, 4), dma(2, 4), dma(2, 4), dma(2, 4), dma(3),
             dma(2, 4), dma(5), dma(2, 4), dma(2, 4), dma(4), dma(4), dma(4), dma(4), dma(3),
             dma(HG, 2), dma(HG, 2), dma(HG, 2), dma(HG, 2), dma(HG, 5), dma(HG, 5), dma(HG), dma(5),
         ],
         0,
         "front",
-    )(length, st, wq, vec, w_out, w_up, w_gate, w_down, inner, outer)
+    )(length, st, w_query, w_key, w_value, *vectors, w_out, w_up, w_gate, w_down, inner, outer)
 
 
 def inv_rms(v):
@@ -949,11 +980,13 @@
             qdo[h, j, :ROWS] = q[h, rows, :]
             qdo[h, j, ROWS:] = wide[rows]
             delta[h, j : j + 1, :] = jnp.sum(prod[rows].T, axis=0, keepdims=True)
-    for k in range(2):
-        g = tn(low[...], dmix[:, k * 640 : (k + 1) * 640])
-        go[k] = g.astype(BF).reshape(4, 80, 640)
-    rcopy(go.at[1 - c], ob, sc.at[1], rc.at[1], sib).start()
     rcopy(vec, vb.at[0], sv.at[0, 0], rv.at[0, 0], sib).start()
+
+    def small_start():
+        for k in range(2):
+            g = tn(low[...], dmix[:, k * 640 : (k + 1) * 640])
+            go[k] = g.astype(BF).reshape(4, 80, 640)
+        rcopy(go.at[1 - c], ob, sc.at[1], rc.at[1], sib).start()
 
     def small_cores():
         landed(ob, rc.at[1])
@@ -1043,7 +1076,7 @@
     def per_head(h, carry):
         acc[...] = jnp.zeros_like(acc)
         dqt[...] = jnp.zeros_like(dqt)
-        for k, f in ((1, small_cores), (2, small_y), (2, down_x), (3, small_x), (4, small_z), (4, down_done)):
+        for k, f in ((1, small_start), (2, small_cores), (3, small_y), (2, down_x), (4, small_x), (4, down_done)):
             pl.when(h == k)(f)
 
         def body(g, carry):
@@ -1051,7 +1084,7 @@
             def _():
                 settle(h - 1)
 
-            pl.when(jnp.logical_and(g == 2, h == HG - 1))(up_first)
+            pl.when(jnp.logical_and(g == 0, h == HG - 1))(up_first)
             key = lax.broadcasted_iota(jnp.int32, (TILE, ROWS), 0)
             its = [item(g * STEP + u) for u in range(STEP)]
             ks = [key_tile(kv, h, t) for _, t, _ in its]
@@ -1076,7 +1109,7 @@
             mine[h, zi, k] = acc[k * 4 + owner_z(c, zi)].astype(BF).reshape(4, ROWS, 128)
             return carry
 
-        lax.fori_loop(0, 4, store, 0)
+        lax.fori_loop(0, 4, store, 0, unroll=True)
         rcopy(give.at[h], got.at[h], sg.at[h], rg.at[h], sib).start()
         for j in range(BLOCKS):
             dq[h, j * ROWS : (j + 1) * ROWS, :] = dqt[j].T * 0.125
@@ -1084,6 +1117,17 @@
 
     lax.fori_loop(0, HG, per_head, 0)
     settle(HG - 1)
+    for d in (1, 2, 3):
+        landed(fax.at[step(y, d)], r2.at[0, step(y, d)])
+        landed(fay.at[step(x, d)], r2.at[2, step(x, d)])
+    v, w = oax[y].astype(F32), oay[x].astype(F32)
+    for d in (1, 2, 3):
+        v = v + fax[step(y, d)].astype(F32)
+        w = w + fay[step(x, d)].astype(F32)
+    za[2, x, :, 0:CUT] = v.astype(BF)
+    za[2, x, :, CUT:D] = w.astype(BF)
+    for d in near_first:
+        rcopy(za.at[2, x], za.at[2, x], s3.at[0, d], r3.at[0, x], to_x[d]).start()
     ws[...] = jnp.zeros_like(ws)
     landed(tt, lo.at[3])
     landed(xg, lo.at[4])
@@ -1119,33 +1163,11 @@
             dd[rows, pair] = jnp.where(lane < 64, before, jnp.where(odd, grads, 0.0)).astype(BF)
             return carry
 
-        lax.fori_loop(0, BLOCKS, per_block, 0)
+        lax.fori_loop(0, BLOCKS, per_block, 0, unroll=True)
         return carry
 
-    lax.fori_loop(0, HG - 1, through, 0)
-    for d in (1, 2, 3):
-        landed(fax.at[step(y, d)], r2.at[0, step(y, d)])
-        landed(fay.at[step(x, d)], r2.at[2, step(x, d)])
-    v, w = oax[y].astype(F32), oay[x].astype(F32)
-    for d in (1, 2, 3):
-        v = v + fax[step(y, d)].astype(F32)
-        w = w + fay[step(x, d)].astype(F32)
-    za[2, x, :, 0:CUT] = v.astype(BF)
-    za[2, x, :, CUT:D] = w.astype(BF)
-    for d in near_first:
-        rcopy(za.at[2, x], za.at[2, x], s3.at[0, d], r3.at[0, x], to_x[d]).start()
-    through(HG - 1, 0)
-
-    def weights(i, carry):
-        h = jnp.where(i == 0, 1 - c, c)
-        cols = pl.ds(pl.multiple_of(h * 512, 128), 512)
-        gq[h] = tn(xg[...].reshape(512, D), dd[:, cols]).astype(BF).reshape(4, 4, 80, 512)
-
-        @pl.when(i == 0)
-        def _():
-            rcopy(gq.at[1 - c], hq, sc.at[0], rc.at[0], sib).start()
-
-        return carry
+    lax.fori_loop(0, HG, through, 0)
+    small_z()
 
     def inputs(p, carry):
         rows = pl.ds(pl.multiple_of(p * 256, 256), 256)
@@ -1154,6 +1176,26 @@
         z_scatter_pair(part, pbuf, ps, pr, p, x, c, z, y)
         return carry
 
+    def along_z():
+        for d in (1, 2, 3):
+            landed(za.at[2, step(x, d)], r3.at[0, step(x, d)])
+        for d in near_first:
+            rcopy(za.at[2, step(z, d)], za.at[c, z], sz.at[0, d], rz.at[0, z], to_z[d]).start()
+        za[c, z] = za[2, z]
+
+    def weights(i, carry):
+        h = jnp.where(i == 0, 1 - c, c)
+        cols = pl.ds(pl.multiple_of(h * 512, 128), 512)
+        gq[h] = tn(xg[...].reshape(512, D), dd[:, cols]).astype(BF).reshape(4, 4, 80, 512)
+
+        @pl.when(i == 0)
+        def _():
+            rcopy(gq.at[1 - c], hq, sc.at[0], rc.at[0], sib).start()
+            along_z()
+            lax.fori_loop(0, 2, inputs, 0)
+
+        return carry
+
     lax.fori_loop(0, 2, weights, 0)
     for h in range(HG):
         v = jnp.sum(sums[:, h * 128 : (h + 1) * 128], axis=0, keepdims=True)
@@ -1178,12 +1220,6 @@
     ws[...] = ws[...] + wb[0]
     for d in near_first:
         rcopy(ws, wb.at[d], sw.at[1, d], rw.at[1, d], to_y[d]).start()
-    for d in (1, 2, 3):
-        landed(za.at[2, step(x, d)], r3.at[0, step(x, d)])
-    for d in near_first:
-        rcopy(za.at[2, step(z, d)], za.at[c, z], sz.at[0, d], rz.at[0, z], to_z[d]).start()
-    za[c, z] = za[2, z]
-    lax.fori_loop(0, 2, inputs, 0)
     for d in (1, 2, 3):
         landed(rqx.at[step(x, d)], p1.at[0, step(x, d)])
         landed(rqy.at[step(y, d)], p1.at[1, step(y, d)])
@@ -1310,48 +1346,80 @@
     )(length, q, kv, wo, dmix, att, lse, ha, hd, tt, xg, wq, scale, inner, outer, vec)
 
 
-def finish_kernel(res, d_st, pbuf, za, zd, zq, out, vec, result, g_in, o_q, o_k, o_v, o_out, o_up, o_gate, o_down, o_vec):
+def finish_kernel(
+    res, d_st, pbuf, za, zd, zq, out, vec,
+    result, g_in, o_q, o_k, o_v, o_out, o_up, o_gate, o_down, v_qk, v_attn, v_mlp, v_up, v_gate,
+):
     _, _, z, y = here()
+    step_no = pl.program_id(0)
     result[...] = res[...]
     g_in[...] = d_st[...] + total_of(pbuf)
-    o_out[:, :640] = out[0].astype(F32)
-    o_out[:, 640:] = out[1].astype(F32)
+    o_up[...] = za[0, 0].astype(F32)
+    o_gate[...] = za[1, 0].astype(F32)
+    for h in range(2):
+        o_down[:, h * 640 : (h + 1) * 640] = zd[h, 0].astype(F32)
+    a, b = zq[1, 0].astype(F32), zq[2, 0].astype(F32)
+    pairs = [a[:, h * 128 : (h + 1) * 128] for h in range(4)] + [b[:, :128]]
     for k in range(4):
-        cols = slice(k * D, (k + 1) * D)
-        o_up[:, cols] = za[0, k].astype(F32)
-        o_gate[:, cols] = za[1, k].astype(F32)
-        for h in range(2):
-            o_down[k * 80 : (k + 1) * 80, h * 640 : (h + 1) * 640] = zd[h, k].astype(F32)
-        a, b = zq[1, k].astype(F32), zq[2, k].astype(F32)
-        at = k * GROUP
-        pairs = [a[:, h * 128 : (h + 1) * 128] for h in range(4)] + [b[:, :128]]
-        o_q[:, at : at + GROUP] = jnp.concatenate([v[:, :HDIM] for v in pairs], axis=1)
-        o_k[:, at : at + GROUP] = jnp.concatenate([v[:, HDIM:] for v in pairs], axis=1)
-        o_v[:, at : at + GROUP] = b[:, 128:448]
-    v = vec[...]
-    o_vec[0:2] = pltpu.roll(v, (16 - (z * 4 + y)) % 16 * 80, 1)[0:2]
-    o_vec[2:4] = pltpu.roll(v, (4 - y) % 4 * 320, 1)[2:4]
-    o_vec[4:] = pltpu.roll(v, (16 - y) % 16 * 80, 1)[4:]
+
+        @pl.when(step_no == k)
+        def _(at=k * GROUP):
+            o_q[:, at : at + GROUP] = jnp.concatenate([v[:, :HDIM] for v in pairs], axis=1)
+            o_k[:, at : at + GROUP] = jnp.concatenate([v[:, HDIM:] for v in pairs], axis=1)
+            o_v[:, at : at + GROUP] = b[:, 128:448]
+
+    @pl.when(step_no == 0)
+    def _():
+        o_out[:, :640] = out[0].astype(F32)
+        o_out[:, 640:] = out[1].astype(F32)
+        v = vec[...]
+        by_shard = pltpu.roll(v, (16 - (z * 4 + y)) % 16 * 80, 1)
+        by_y = pltpu.roll(v, (4 - y) % 4 * 320, 1)
+        v_attn[...] = by_shard[0:1, :80]
+        v_mlp[...] = by_shard[1:2, :80]
+        v_up[...] = by_y[2:3, :320]
+        v_gate[...] = by_y[3:4, :320]
+        v_qk[...] = pltpu.roll(v, (16 - y) % 16 * 80, 1)[4:5, :80]
 
 
 def finish(res, d_st, pbuf, za, zd, zq, out, vec):
-    return local_call(
+    def whole(*shape):
+        return pl.BlockSpec(shape, lambda k: (0,) * len(shape))
+
+    rows = ROWS // 4
+    outs = [
+        ((ROWS, D), BF, pl.BlockSpec((rows, D), lambda k: (k, 0))),
+        ((ROWS, D), F32, pl.BlockSpec((rows, D), lambda k: (k, 0))),
+        ((80, D), F32, whole(80, D)),
+        ((80, D), F32, whole(80, D)),
+        ((80, D), F32, whole(80, D)),
+        ((80, D), F32, whole(80, D)),
+        ((80, FF), F32, pl.BlockSpec((80, D), lambda k: (0, k))),
+        ((80, FF), F32, pl.BlockSpec((80, D), lambda k: (0, k))),
+        ((320, D), F32, pl.BlockSpec((80, D), lambda k: (k, 0))),
+        ((1, 80), F32, whole(1, 80)),
+        ((1, 80), F32, whole(1, 80)),
+        ((1, 80), F32, whole(1, 80)),
+        ((1, 320), F32, whole(1, 320)),
+        ((1, 320), F32, whole(1, 320)),
+    ]
+    return pl.pallas_call(
         finish_kernel,
-        [
-            ((ROWS, D), BF),
-            ((ROWS, D), F32),
-            ((80, D), F32),
-            ((80, D), F32),
-            ((80, D), F32),
-            ((80, D), F32),
-            ((80, FF), F32),
-            ((80, FF), F32),
-            ((320, D), F32),
-            ((8, D), F32),
+        grid=(4,),
+        out_shape=[jax.ShapeDtypeStruct(s, d) for s, d, _ in outs],
+        in_specs=[
+            pl.BlockSpec((rows, D), lambda k: (k, 0)),
+            pl.BlockSpec((rows, D), lambda k: (k, 0)),
+            pl.BlockSpec((4, rows, D), lambda k: (0, k, 0)),
+            pl.BlockSpec((2, 1, 80, D), lambda k: (0, k, 0, 0)),
+            pl.BlockSpec((2, 1, 80, 640), lambda k: (0, k, 0, 0)),
+            pl.BlockSpec((3, 1, 80, 512), lambda k: (0, k, 0, 0)),
+            whole(2, 80, 640),
+            whole(8, D),
         ],
-        8,
-        [],
-        "finish",
+        out_specs=[spec for _, _, spec in outs],
+        compiler_params=pltpu.CompilerParams(vmem_limit_bytes=VMEM_LIMIT),
+        name="finish",
     )(res, d_st, pbuf, za, zd, zq, out, vec)
 
 
@@ -1362,19 +1430,11 @@
     x, c, z, y = here()
     st = states[0]
 
-    def heads(w):
-        return w.reshape(80, 4, HG, HDIM)
-
-    q4, k4, v4 = heads(w_query), heads(w_key), heads(w_value)
-    qk = jnp.stack([q4, k4], axis=3).reshape(80, 4, HG * 128)
-    half1 = jnp.concatenate([qk[:, :, 512:], v4.reshape(80, 4, GROUP), jnp.zeros((80, 4, HDIM), BF)], axis=2)
-    wq = jnp.stack([qk[:, :, :512], half1]).transpose(0, 2, 1, 3)
-    vec = jnp.concatenate([scale_qk, alpha_attn, alpha_mlp, scale_up, scale_gate, jnp.zeros((16,), BF)])
-    vec = jnp.broadcast_to(vec.astype(F32)[None], (8, 896))
+    vectors = [v.reshape(1, -1) for v in (scale_qk, alpha_attn, alpha_mlp, scale_up, scale_gate)]
     inner, outer = (jnp.asarray(t) for t in rope_tables())
     n = BLOCKS * ROWS
     part, att, lse, kv, q, turned, xg, wqkv, wo, scale, rate_a, rate_m, su, sg, uq, wd, gz = front(
-        lengths, st, wq, vec, w_out, w_up, w_gate, w_down, inner, outer
+        lengths, st, w_query, w_key, w_value, vectors, w_out, w_up, w_gate, w_down, inner, outer
     )
     result, d_st, dm, ha, hd, vec = middle(
         lengths, part, st, cotangent[0], rate_a, rate_m, su, sg, uq, wd.reshape(D, D), gz
@@ -1382,25 +1442,8 @@
     pbuf, za, zd, zq, out, vec = back(
         lengths, q, kv, wo.reshape(GROUP, D), dm.reshape(n, D), att, lse, ha, hd, turned, xg, wqkv, scale, inner, outer, vec
     )
-    result, g_in, o_q, o_k, o_v, o_out, o_up, o_gate, o_down, o_vec = finish(
-        result, d_st, pbuf, za, zd, zq, out, vec
-    )
-    return (
-        result[None],
-        g_in[None],
-        o_q,
-        o_k,
-        o_v,
-        o_out,
-        o_up,
-        o_gate,
-        o_down,
-        o_vec[4, :80],
-        o_vec[0, :80],
-        o_vec[1, :80],
-        o_vec[2, :320],
-        o_vec[3, :320],
-    )
+    outs = finish(result, d_st, pbuf, za, zd, zq, out, vec)
+    return (outs[0][None], outs[1][None], *outs[2:9], *(v.reshape(-1) for v in outs[9:]))
 
 
 def solution(mesh):

time: 308 us -> 291 us (0.945)
  Pallas kernels: 297 us -> 285 us
  local copies, waits for them, and re-layouts: 7.46 us -> 2.49 us
    pallas_call x1, Pallas kernels: 107 us -> 99.9 us  [back(): remote_call(back_kernel, [((4, ROWS, D), BF, 'v'), ((3, 4, 80, D), BF, 'v...]
    pallas_call x1, Pallas kernels: 82.3 us -> 76.6 us  [front(): remote_call(front_kernel, [((2, 2, ROWS, D), BF, 'v'), ((HG, n, HDIM), F3...]
where the time goes in v5:
time: 291 us
  Pallas kernels  285 us (98%)
    pallas_call x1, Pallas kernels, middle(): remote_call(mid_kernel, [((ROWS, D), BF, 'v'), ((ROWS, D), F32, 'v'), ((2...  101 us
    pallas_call x1, Pallas kernels, back(): remote_call(back_kernel, [((4, ROWS, D), BF, 'v'), ((3, 4, 80, D), BF, 'v...  99.9 us
    pallas_call x1, Pallas kernels, front(): remote_call(front_kernel, [((2, 2, ROWS, D), BF, 'v'), ((HG, n, HDIM), F3...  76.6 us
    pallas_call x1, Pallas kernels, finish(): pl.pallas_call(finish_kernel, grid=(4,), out_shape=[jax.ShapeDtypeStruct(...  6.79 us

profile of v5, /device:TPU:1, one launch (start us, length us, event | category | flops | bytes accessed | tf_op | source)
XLA Modules:
  0.0 291.0 jit_solution(15596013580152998208)
XLA Ops:
  1.3 1.2 reshape.70.v_up
  2.5 1.2 reshape.71.v_gate
  3.8 76.6 %front.1 = (bf16[2,2,128,1280]{3,2,1,0:T(8,128)(2,1)}, f32[5,512,64]{2,1,0:T(8,128)}, f32[5,4,128]{2,1,0:T(4,128)}, bf16[5,2,2,2,4,128,128]{6,5,4,3,2,1,0:T(8,12...) custom-call(s32[1]{0:T(128)S(6)} %copy.31.length, ...), custom_call_target="tpu_custom_call" | custom-call | tf_op jit(solution)/shard_map/front/pallas_call | solution.py:557
  80.4 101.3 %middle.1 = (bf16[128,1280]{1,0:T(8,128)(2,1)}, f32[128,1280]{1,0:T(8,128)}, bf16[2,2,128,1280]{3,2,1,0:T(8,128)(2,1)}, bf16[4,4,80,1280]{3,2,1,0:T(8,128)(2,1)}...) custom-call(s32[1]{0:T(128)S(6)} %copy.31.length, bf16[2,2,128,1280]{3,2,1,0:T(8,128)(2,1)} %get-tuple-element.57.part0, ...), custom_call_target="tpu_custom_call" | custom-call | tf_op jit(solution)/shard_map/middle/pallas_call | solution.py:907
  181.7 99.9 %back.1 = (bf16[4,128,1280]{2,1,0:T(8,128)(2,1)}, bf16[3,4,80,1280]{3,2,1,0:T(8,128)(2,1)}, bf16[2,4,80,640]{3,2,1,0:T(8,128)(2,1)}, bf16[3,4,80,512]{3,2,1,0:T(...) custom-call(s32[1]{0:T(128)S(6)} %copy.31.length, bf16[5,512,128]{2,1,0:T(8,128)(2,1)} %get-tuple-element.67.q, ...), custom_call_target="tpu_custom_call" | custom-call | tf_op jit(solution)/shard_map/back/pallas_call | solution.py:1317
  281.7 6.8 %finish.1 = (bf16[128,1280]{1,0:T(8,128)(2,1)}, f32[128,1280]{1,0:T(8,128)}, f32[80,1280]{1,0:T(8,128)}, f32[80,1280]{1,0:T(8,128)}, f32[80,1280]{1,0:T(8,128)},...) custom-call(bf16[128,1280]{1,0:T(8,128)(2,1)} %get-tuple-element.65., ...), custom_call_target="tpu_custom_call" | custom-call | tf_op jit(solution)/shard_map/finish/pallas_call | solution.py:1406
  288.4 1.3 reduce
  289.7 1.3 reduce.1

commit v6 on v5

--- a/solution.py
+++ b/solution.py
@@ -286,7 +286,7 @@
 
     vec[...] = jnp.zeros_like(vec)
     for ref, at, n in ((v_qk, 0, 80), (v_attn, 80, 80), (v_mlp, 160, 80), (v_up, 240, 320), (v_gate, 560, 320)):
-        vec[:, at : at + n] = jnp.broadcast_to(ref[...].astype(F32), (8, n))
+        vec[:, at : at + n] = jnp.broadcast_to(ref[...].astype(F32).reshape(1, n), (8, n))
     greet(z_peers(x, c, z, y) + to_y[1:] + to_x[1:])
 
     for d in near_first:
@@ -935,9 +935,9 @@
 
 
 def back_kernel(
-    length, q, kv_in, wo, dmix, att, lse, ha, hd, tt_in, xg_in, wq_in, scale, inner, outer, vec,
+    length, q_in, kv_in, wo_in, dmix_in, att_in, lse, ha, hd, tt_in, xg_in, wq_in, scale, inner, outer, vec,
     pbuf, za, zd, zq, o_out, o_vec,
-    kv, tt, xg, wq,
+    q, wo, dmix, att, kv, tt, xg, wq,
     qdo, delta, dqt, acc, low, give, mine, got, got_y, dq, dd, sums, part, gq, go,
     oax, oay, rax, ray, fax, fay, fd, hq, rqx, rqy, fqx, fqy, ob, ox, o2, vs, vb, ws, wb,
     lo, sg, rg, sy, ry, s1, r1, s2, r2, s3, r3, sz, rz, sc, rc, q1, p1, q2, p2, q3, p3, so, ro, sv, rv, sw, rw, ps, pr, sf, rf,
@@ -948,6 +948,8 @@
     to_x = [None] + [dev(step(x, d), c, z, y) for d in (1, 2, 3)]
     to_z = [None] + [dev(x, c, step(z, d), y) for d in (1, 2, 3)]
     near_first = (1, 3, 2)
+    for i, (a, b) in enumerate(((dmix_in, dmix), (wo_in, wo), (att_in, att), (q_in, q))):
+        lcopy(a, b, lo.at[6 + i]).start()
     lcopy(kv_in, kv, lo.at[0]).start()
     lcopy(ha.at[x, :, :, 0:CUT], oax, lo.at[1]).start()
     lcopy(ha.at[:, y, :, CUT:D], oay, lo.at[2]).start()
@@ -956,8 +958,6 @@
     lcopy(wq_in, wq, lo.at[5]).start()
     greet(z_peers(x, c, z, y) + to_y[1:] + to_x[1:])
     for d in near_first:
-        rcopy(hd.at[step(x, d)], fd.at[x], s2.at[1, d], r2.at[1, x], to_x[d]).start()
-    for d in near_first:
         rcopy(ha.at[step(x, d), :, :, 0:CUT], rax.at[x], s1.at[0, d], r1.at[0, x], to_x[d]).start()
         rcopy(ha.at[:, step(y, d), :, CUT:D], ray.at[y], s1.at[1, d], r1.at[1, y], to_y[d]).start()
 
@@ -969,6 +969,8 @@
         for d in near_first:
             rcopy(mine.at[h, :, :, step(y, d)], got_y.at[h, y], sy.at[h, d], ry.at[h, y], to_y[d]).start()
 
+    for i, b in enumerate((dmix, wo, att, q)):
+        landed(b, lo.at[6 + i])
     d_att = nt(dmix[...], wo[...]).astype(BF)
     for h in range(HG):
         low[:, h * HDIM : (h + 1) * HDIM] = att[h].astype(BF)
@@ -1069,6 +1071,8 @@
         for d in near_first:
             rcopy(oax.at[step(y, d)], fax.at[y], s2.at[0, d], r2.at[0, y], to_y[d]).start()
             rcopy(oay.at[step(x, d)], fay.at[x], s2.at[2, d], r2.at[2, x], to_x[d]).start()
+        for d in near_first:
+            rcopy(hd.at[step(x, d)], fd.at[x], s2.at[1, d], r2.at[1, x], to_x[d]).start()
 
     landed(kv, lo.at[0])
     item = work_items(c, y, length[0])
@@ -1076,7 +1080,7 @@
     def per_head(h, carry):
         acc[...] = jnp.zeros_like(acc)
         dqt[...] = jnp.zeros_like(dqt)
-        for k, f in ((1, small_start), (2, small_cores), (3, small_y), (2, down_x), (4, small_x), (4, down_done)):
+        for k, f in ((1, small_start), (3, small_cores)):
             pl.when(h == k)(f)
 
         def body(g, carry):
@@ -1085,6 +1089,7 @@
                 settle(h - 1)
 
             pl.when(jnp.logical_and(g == 0, h == HG - 1))(up_first)
+            pl.when(jnp.logical_and(g == 1, h == HG - 1))(small_y)
             key = lax.broadcasted_iota(jnp.int32, (TILE, ROWS), 0)
             its = [item(g * STEP + u) for u in range(STEP)]
             ks = [key_tile(kv, h, t) for _, t, _ in its]
@@ -1166,8 +1171,10 @@
         lax.fori_loop(0, BLOCKS, per_block, 0, unroll=True)
         return carry
 
-    lax.fori_loop(0, HG, through, 0)
-    small_z()
+    lax.fori_loop(0, 2, through, 0)
+    down_x()
+    small_x()
+    lax.fori_loop(2, HG, through, 0)
 
     def inputs(p, carry):
         rows = pl.ds(pl.multiple_of(p * 256, 256), 256)
@@ -1202,6 +1209,7 @@
         ws[:, h * HDIM : (h + 1) * HDIM] = jnp.broadcast_to(v[:, :HDIM] + v[:, HDIM:], (8, HDIM))
     rcopy(ws, wb.at[0], sw.at[0, 0], rw.at[0, 0], sib).start()
 
+    small_z()
     landed(hq, rc.at[0])
 
     def add_q(k, carry):
@@ -1255,6 +1263,7 @@
     zq[0, x] = jnp.concatenate([a, b], axis=1).astype(BF)
     for d in near_first:
         rcopy(zq.at[0, x], zq.at[0, x], q3.at[d], p3.at[x], to_x[d]).start()
+    down_done()
     tot = ws[...]
     for d in (1, 2, 3):
         landed(wb.at[3 + d], rw.at[2, d])
@@ -1324,8 +1333,9 @@
             ((2, 80, 640), BF, "v"),
             ((8, D), F32, "v"),
         ],
-        "svavvvvavaaavvvv",
+        "saaaaavavaaavvvv",
         [
+            V((HG, n, 128), BF), V((GROUP, D), BF), V((n, D), BF), V((HG, n, HDIM), F32),
             V((HG, 2, 2, 2, 4, ROWS, 128), BF), V((HG, n, 128), F32), V((2, 2, ROWS, D), BF), V((2, 4, 4, 80, 512), BF),
             V((HG, BLOCKS, 2 * ROWS, 128), BF), V((HG, BLOCKS, 128), F32), V((BLOCKS, 128, ROWS), F32), V((8, TILE, 128), F32),
             V((n, GROUP), BF),
@@ -1336,7 +1346,7 @@
             V((4, 80, CUT), BF), V((4, 80, D - CUT), BF), V((4, 80, 640), BF),
             V((4, 4, 80, 512), BF), V((4, 4, 80, 256), BF), V((4, 4, 80, 256), BF), V((5, 4, 80, 256), BF), V((5, 4, 80, 256), BF),
             V((4, 80, 640), BF), V((4, 80, 640), BF), V((4, 80, 640), BF), V((8, D), F32), V((10, 8, D), F32), V((8, 384), F32), V((7, 8, 384), F32),
-            dma(6), dma(HG), dma(HG), dma(HG, 4), dma(HG, 4),
+            dma(10), dma(HG), dma(HG), dma(HG, 4), dma(HG, 4),
             dma(2, 4), dma(2, 4), dma(3, 4), dma(3, 4), dma(2, 4), dma(2, 4), dma(2, 4), dma(2, 4), dma(2), dma(2),
             dma(2, 4), dma(2, 4), dma(2, 4), dma(2, 4), dma(4), dma(4), dma(2, 4), dma(2, 4), dma(4, 4), dma(4, 4), dma(3, 4), dma(3, 4),
             dma(2, 2), dma(4), dma(4), dma(4),
@@ -1375,11 +1385,11 @@
         v = vec[...]
         by_shard = pltpu.roll(v, (16 - (z * 4 + y)) % 16 * 80, 1)
         by_y = pltpu.roll(v, (4 - y) % 4 * 320, 1)
-        v_attn[...] = by_shard[0:1, :80]
-        v_mlp[...] = by_shard[1:2, :80]
-        v_up[...] = by_y[2:3, :320]
-        v_gate[...] = by_y[3:4, :320]
-        v_qk[...] = pltpu.roll(v, (16 - y) % 16 * 80, 1)[4:5, :80]
+        v_attn[...] = by_shard[0:1, :80].reshape(80)
+        v_mlp[...] = by_shard[1:2, :80].reshape(80)
+        v_up[...] = by_y[2:3, :320].reshape(320)
+        v_gate[...] = by_y[3:4, :320].reshape(320)
+        v_qk[...] = pltpu.roll(v, (16 - y) % 16 * 80, 1)[4:5, :80].reshape(80)
 
 
 def finish(res, d_st, pbuf, za, zd, zq, out, vec):
@@ -1397,11 +1407,11 @@
         ((80, FF), F32, pl.BlockSpec((80, D), lambda k: (0, k))),
         ((80, FF), F32, pl.BlockSpec((80, D), lambda k: (0, k))),
         ((320, D), F32, pl.BlockSpec((80, D), lambda k: (k, 0))),
-        ((1, 80), F32, whole(1, 80)),
-        ((1, 80), F32, whole(1, 80)),
-        ((1, 80), F32, whole(1, 80)),
-        ((1, 320), F32, whole(1, 320)),
-        ((1, 320), F32, whole(1, 320)),
+        ((80,), F32, whole(80)),
+        ((80,), F32, whole(80)),
+        ((80,), F32, whole(80)),
+        ((320,), F32, whole(320)),
+        ((320,), F32, whole(320)),
     ]
     return pl.pallas_call(
         finish_kernel,
@@ -1430,7 +1440,7 @@
     x, c, z, y = here()
     st = states[0]
 
-    vectors = [v.reshape(1, -1) for v in (scale_qk, alpha_attn, alpha_mlp, scale_up, scale_gate)]
+    vectors = (scale_qk, alpha_attn, alpha_mlp, scale_up, scale_gate)
     inner, outer = (jnp.asarray(t) for t in rope_tables())
     n = BLOCKS * ROWS
     part, att, lse, kv, q, turned, xg, wqkv, wo, scale, rate_a, rate_m, su, sg, uq, wd, gz = front(
@@ -1443,7 +1453,7 @@
         lengths, q, kv, wo.reshape(GROUP, D), dm.reshape(n, D), att, lse, ha, hd, turned, xg, wqkv, scale, inner, outer, vec
     )
     outs = finish(result, d_st, pbuf, za, zd, zq, out, vec)
-    return (outs[0][None], outs[1][None], *outs[2:9], *(v.reshape(-1) for v in outs[9:]))
+    return (outs[0][None], outs[1][None], *outs[2:])
 
 
 def solution(mesh):

time: 291 us -> 284 us (0.976)
  no operation moved by 1% of the time
where the time goes in v6:
time: 284 us
  Pallas kernels  283 us (100%)
    pallas_call x1, Pallas kernels, middle(): remote_call(mid_kernel, [((ROWS, D), BF, 'v'), ((ROWS, D), F32, 'v'), ((2...  101 us
    pallas_call x1, Pallas kernels, back(): remote_call(back_kernel, [((4, ROWS, D), BF, 'v'), ((3, 4, 80, D), BF, 'v...  98 us
    pallas_call x1, Pallas kernels, front(): remote_call(front_kernel, [((2, 2, ROWS, D), BF, 'v'), ((HG, n, HDIM), F3...  76.7 us
    pallas_call x1, Pallas kernels, finish(): pl.pallas_call(finish_kernel, grid=(4,), out_shape=[jax.ShapeDtypeStruct(...  6.79 us

profile of v6, /device:TPU:1, one launch (start us, length us, event | category | flops | bytes accessed | tf_op | source)
XLA Modules:
  0.0 284.2 jit_solution(8276768809491736856)
XLA Ops:
  1.3 76.7 %front.1 = (bf16[2,2,128,1280]{3,2,1,0:T(8,128)(2,1)}, f32[5,512,64]{2,1,0:T(8,128)}, f32[5,4,128]{2,1,0:T(4,128)}, bf16[5,2,2,2,4,128,128]{6,5,4,3,2,1,0:T(8,12...) custom-call(s32[1]{0:T(128)S(6)} %copy.31.length, ...), custom_call_target="tpu_custom_call" | custom-call | tf_op jit(solution)/shard_map/front/pallas_call | solution.py:557
  78.0 101.3 %middle.1 = (bf16[128,1280]{1,0:T(8,128)(2,1)}, f32[128,1280]{1,0:T(8,128)}, bf16[2,2,128,1280]{3,2,1,0:T(8,128)(2,1)}, bf16[4,4,80,1280]{3,2,1,0:T(8,128)(2,1)}...) custom-call(s32[1]{0:T(128)S(6)} %copy.31.length, bf16[2,2,128,1280]{3,2,1,0:T(8,128)(2,1)} %get-tuple-element.57.part0, ...), custom_call_target="tpu_custom_call" | custom-call | tf_op jit(solution)/shard_map/middle/pallas_call | solution.py:907
  179.3 98.0 %back.1 = (bf16[4,128,1280]{2,1,0:T(8,128)(2,1)}, bf16[3,4,80,1280]{3,2,1,0:T(8,128)(2,1)}, bf16[2,4,80,640]{3,2,1,0:T(8,128)(2,1)}, bf16[3,4,80,512]{3,2,1,0:T(...) custom-call(s32[1]{0:T(128)S(6)} %copy.31.length, bf16[5,512,128]{2,1,0:T(8,128)(2,1)} %get-tuple-element.67.q_in, ...), custom_call_target="tpu_custom_call" | custom-call | tf_op jit(solution)/shard_map/back/pallas_call | solution.py:1326
  277.2 6.8 %finish.1 = (bf16[128,1280]{1,0:T(8,128)(2,1)}, f32[128,1280]{1,0:T(8,128)}, f32[80,1280]{1,0:T(8,128)}, f32[80,1280]{1,0:T(8,128)}, f32[80,1280]{1,0:T(8,128)},...) custom-call(bf16[128,1280]{1,0:T(8,128)(2,1)} %get-tuple-element.65., ...), custom_call_target="tpu_custom_call" | custom-call | tf_op jit(solution)/shard_map/finish/pallas_call | solution.py:1416

commit v7 on v6

--- a/solution.py
+++ b/solution.py
@@ -623,8 +623,8 @@
 
 def mid_kernel(
     length, part0, st, cot, rate_a, rate_m, su, sg, uq, wd_in, gz,
-    result, d_st, dm, ha, hd, vec,
-    buf, low, xg, dd, wu, wg, wd, up, gate, hid, dug, part, xt, ht, mixed, first, dfirst, ga, gd, ra, rd, rdy,
+    result, d_st, dm, ha_out, hd, vec,
+    ha, buf, low, xg, dd, wu, wg, wd, up, gate, hid, dug, part, xt, ht, mixed, first, dfirst, ga, gd, ra, rd, rdy,
     ps, pr, gs, gr, s2, r2, s3, r3, sx, rx, sy, ry, lo,
 ):
     x, c, z, y = here()
@@ -874,6 +874,7 @@
         return carry
 
     lax.fori_loop(0, 16, add_a, 0)
+    lcopy(ha, ha_out, lo.at[3]).start()
     for d in (1, 2, 3):
         landed(rdy.at[step(y, d)], ry.at[step(y, d)])
 
@@ -898,6 +899,7 @@
             landed(gz, s2.at[i, d])
     landed(ra, sx.at[0])
     landed(rd, sx.at[1])
+    landed(ha, lo.at[3])
     for d in (1, 2, 3):
         landed(rdy.at[y], sy.at[d])
 
@@ -910,12 +912,13 @@
             ((ROWS, D), BF, "v"),
             ((ROWS, D), F32, "v"),
             ((2, 2, ROWS, D), BF, "a"),
-            ((4, 4, 80, D), BF, "v"),
+            ((4, 4, 80, D), BF, "a"),
             ((4, 80, 640), BF, "v"),
             ((8, D), F32, "v"),
         ],
         "savvvvvvaaa",
         [
+            V((4, 4, 80, D), BF),
             V((3, 4, ROWS, D), BF), V((3, ROWS, D), BF), V((2, 2, ROWS, D), BF), V((2, 2, ROWS, D), BF),
             V((4, 4, 80, D), BF), V((4, 4, 80, D), BF), V((D, D), BF),
             V((2, 256, D), F32), V((2, 256, D), F32), V((2, 256, D), BF), V((2, 2, 256, D), BF),
@@ -924,14 +927,14 @@
             V((2, 4, 4, 80, D), BF), V((2, 4, 4, 80, 640), BF), V((4, 4, 80, D), BF), V((4, 4, 80, 640), BF),
             V((4, 4, 80, 640), BF),
             dma(3, 2, 2, 2), dma(3, 2, 4), dma(3, 2, 4), dma(3, 2, 2, 2),
-            dma(2, 4), dma(2, 4), dma(2, 4), dma(2, 4), dma(2), dma(2), dma(4), dma(4), dma(3),
+            dma(2, 4), dma(2, 4), dma(2, 4), dma(2, 4), dma(2), dma(2), dma(4), dma(4), dma(4),
         ],
         2,
         "middle",
     )(length, part0, st, cot, rate_a, rate_m, su, sg, uq, wd, gz)
 
 
-CUT = 768
+CUT = 896
 
 
 def back_kernel(

time: 284 us -> 281 us (0.989)
  Pallas kernels: 283 us -> 279 us
where the time goes in v7:
time: 281 us
  Pallas kernels  279 us (99%)
    pallas_call x1, Pallas kernels, middle(): remote_call(mid_kernel, [((ROWS, D), BF, 'v'), ((ROWS, D), F32, 'v'), ((2...  100 us
    pallas_call x1, Pallas kernels, back(): remote_call(back_kernel, [((4, ROWS, D), BF, 'v'), ((3, 4, 80, D), BF, 'v...  95.3 us
    pallas_call x1, Pallas kernels, front(): remote_call(front_kernel, [((2, 2, ROWS, D), BF, 'v'), ((HG, n, HDIM), F3...  76.7 us
    pallas_call x1, Pallas kernels, finish(): pl.pallas_call(finish_kernel, grid=(4,), out_shape=[jax.ShapeDtypeStruct(...  6.79 us

profile of v7, /device:TPU:1, one launch (start us, length us, event | category | flops | bytes accessed | tf_op | source)
XLA Modules:
  0.0 280.6 jit_solution(9311267242252284571)
XLA Ops:
  1.3 76.7 %front.1 = (bf16[2,2,128,1280]{3,2,1,0:T(8,128)(2,1)}, f32[5,512,64]{2,1,0:T(8,128)}, f32[5,4,128]{2,1,0:T(4,128)}, bf16[5,2,2,2,4,128,128]{6,5,4,3,2,1,0:T(8,12...) custom-call(s32[1]{0:T(128)S(6)} %copy.31.length, ...), custom_call_target="tpu_custom_call" | custom-call | tf_op jit(solution)/shard_map/front/pallas_call | solution.py:557
  78.0 100.3 %middle.1 = (bf16[128,1280]{1,0:T(8,128)(2,1)}, f32[128,1280]{1,0:T(8,128)}, bf16[2,2,128,1280]{3,2,1,0:T(8,128)(2,1)}, bf16[4,4,80,1280]{3,2,1,0:T(8,128)(2,1)}...) custom-call(s32[1]{0:T(128)S(6)} %copy.31.length, bf16[2,2,128,1280]{3,2,1,0:T(8,128)(2,1)} %get-tuple-element.57.part0, ...), custom_call_target="tpu_custom_call" | custom-call | tf_op jit(solution)/shard_map/middle/pallas_call | solution.py:909
  178.3 95.3 %back.1 = (bf16[4,128,1280]{2,1,0:T(8,128)(2,1)}, bf16[3,4,80,1280]{3,2,1,0:T(8,128)(2,1)}, bf16[2,4,80,640]{3,2,1,0:T(8,128)(2,1)}, bf16[3,4,80,512]{3,2,1,0:T(...) custom-call(s32[1]{0:T(128)S(6)} %copy.31.length, bf16[5,512,128]{2,1,0:T(8,128)(2,1)} %get-tuple-element.67.q_in, ...), custom_call_target="tpu_custom_call" | custom-call | tf_op jit(solution)/shard_map/back/pallas_call | solution.py:1329
  273.6 6.8 %finish.1 = (bf16[128,1280]{1,0:T(8,128)(2,1)}, f32[128,1280]{1,0:T(8,128)}, f32[80,1280]{1,0:T(8,128)}, f32[80,1280]{1,0:T(8,128)}, f32[80,1280]{1,0:T(8,128)},...) custom-call(bf16[128,1280]{1,0:T(8,128)(2,1)} %get-tuple-element.65., ...), custom_call_target="tpu_custom_call" | custom-call | tf_op jit(solution)/shard_map/finish/pallas_call | solution.py:1419
